TPU v7x, 32 devices: a whole 2x2x4 slice. The times are simulated.
32 devices in a mesh: fsdp: 8 (over z, x), ctx: 2 (over y), tp: 2 (over core).
Axes of the slice: x: 2, y: 2, z: 4, core: 2. Of those that a mesh axis runs over, the one named last changes fastest.
Arguments:
- prompt: bfloat16 [8, 1024, 768], P('fsdp', 'ctx'), may hold values from -6 to 6
- continuations: bfloat16 [8, 2, 256, 768], P('fsdp', 'ctx'), may hold values from -6 to 6
- prev_logits: bfloat16 [8, 2, 12, 256, 1280], P('fsdp', 'ctx', 'tp'), may hold values from -6 to 6
- cont_len: int32 [8, 2], P('fsdp', 'ctx'), may hold values from 1 to 256, 384 in all within a row
- query_weight: bfloat16 [768, 768], P('fsdp', 'tp'), may hold values from -0.21875 to 0.21875
- query_bias: bfloat16 [12, 64], P('tp', 'fsdp'), may hold values from -3 to 3
- key_weight: bfloat16 [768, 768], P('fsdp', 'tp'), may hold values from -0.21875 to 0.21875
- value_weight: bfloat16 [768, 768], P('fsdp', 'tp'), may hold values from -0.21875 to 0.21875
- value_bias: bfloat16 [12, 64], P('tp', 'fsdp'), may hold values from -3 to 3
- output_weight: bfloat16 [768, 768], P('tp', 'fsdp'), may hold values from -3.5 to 3.5
- output_bias: bfloat16 [768], P('fsdp'), may hold values from -3 to 3
- first_gain: bfloat16 [768], P('fsdp'), may hold values from 0.5 to 1.5
- first_shift: bfloat16 [768], P('fsdp'), may hold values from -3 to 3
- up_weight: bfloat16 [768, 3072], P('fsdp', 'tp'), may hold values from -0.21875 to 0.21875
- up_bias: bfloat16 [24, 128], P('tp', 'fsdp'), may hold values from -3 to 3
- down_weight: bfloat16 [3072, 768], P('tp', 'fsdp'), may hold values from -0.109375 to 0.109375
- down_bias: bfloat16 [768], P('fsdp'), may hold values from -3 to 3
- second_gain: bfloat16 [768], P('fsdp'), may hold values from 0.5 to 1.5
- second_shift: bfloat16 [768], P('fsdp'), may hold values from -3 to 3
- cot_prompt: bfloat16 [8, 1024, 768], P('fsdp', 'ctx'), may hold values from -6 to 6
- cot_conts: bfloat16 [8, 2, 256, 768], P('fsdp', 'ctx'), may hold values from -6 to 6
- cot_logits: bfloat16 [8, 2, 12, 256, 1280], P('fsdp', 'ctx', 'tp'), may hold values from -0.29882812 to 0.29882812
Outputs:
- prompt_out: bfloat16 [8, 1024, 768], P('fsdp', 'ctx')
- conts_out: bfloat16 [8, 2, 256, 768], P('fsdp', 'ctx')
- new_logits: bfloat16 [8, 2, 12, 256, 1280], P('fsdp', 'ctx', 'tp')
- grad_prompt: float32 [8, 1024, 768], P('fsdp', 'ctx')
- grad_conts: float32 [8, 2, 256, 768], P('fsdp', 'ctx')
- grad_prev: bfloat16 [8, 2, 12, 256, 1280], P('fsdp', 'ctx', 'tp')
- query_weight_grad: float32 [768, 768], P('fsdp', 'tp')
- query_bias_grad: float32 [12, 64], P('tp', 'fsdp')
- key_weight_grad: float32 [768, 768], P('fsdp', 'tp')
- value_weight_grad: float32 [768, 768], P('fsdp', 'tp')
- value_bias_grad: float32 [12, 64], P('tp', 'fsdp')
- output_weight_grad: float32 [768, 768], P('tp', 'fsdp')
- output_bias_grad: float32 [768], P('fsdp')
- first_gain_grad: float32 [768], P('fsdp')
- first_shift_grad: float32 [768], P('fsdp')
- up_weight_grad: float32 [768, 3072], P('fsdp', 'tp')
- up_bias_grad: float32 [24, 128], P('tp', 'fsdp')
- down_weight_grad: float32 [3072, 768], P('tp', 'fsdp')
- down_bias_grad: float32 [768], P('fsdp')
- second_gain_grad: float32 [768], P('fsdp')
- second_shift_grad: float32 [768], P('fsdp')
Inputs may be any that keep to these rules, and one draw needn't show every extreme that they name: `cont_len`: A group's lengths sum to 384.
All inputs are finite; a program needn't handle non-finite values.
Results may differ from a plain program's by a relative error of at most 0.02.
Values may be sent and summed in bfloat16 or wider, within the bound.
No kernel may reach another device: no remote copies, remote signals or barrier semaphores. Data moves between devices by JAX's collectives and lax.ppermute only.
A program may use at most 192 MiB of HBM per device.

v0:
```python
import math

import jax
import jax.numpy as jnp
from jax import lax
from jax.sharding import PartitionSpec as P

epsilon = 1e-06


def product(left_mat, right_mat):
    return jnp.dot(left_mat, right_mat, preferred_element_type=jnp.float32)


def contract_rows(left_mat, right_mat):
    return lax.dot_general(
        left_mat, right_mat, (((0,), (0,)), ((), ())), preferred_element_type=jnp.float32
    )


def contract_cols(left_mat, right_mat):
    return lax.dot_general(
        left_mat, right_mat, (((1,), (1,)), ((), ())), preferred_element_type=jnp.float32
    )


def split_heads(matrix, head_count):
    return matrix.reshape(matrix.shape[0], head_count, -1)


def soft_rows(scores):
    row_peak = jnp.max(scores, axis=-1, keepdims=True)
    logsum = row_peak + jnp.log(jnp.sum(jnp.exp(scores - row_peak), axis=-1, keepdims=True))
    return (jnp.exp(scores - logsum), logsum)


def norm_forward(hidden_in, gain_full, shift_full):
    centre = jnp.mean(hidden_in, axis=-1, keepdims=True)
    shifted = hidden_in - centre
    spread = jnp.mean(shifted * shifted, axis=-1, keepdims=True)
    inverse = lax.rsqrt(spread + epsilon)
    normed = shifted * inverse
    return (normed * gain_full + shift_full, normed, inverse)


def norm_backward(upstream, normed, inverse, gain_full):
    scaled = upstream * gain_full
    mean_one = jnp.mean(scaled, axis=-1, keepdims=True)
    mean_two = jnp.mean(scaled * normed, axis=-1, keepdims=True)
    grad_in = inverse * (scaled - mean_one - normed * mean_two)
    return (grad_in, jnp.sum(upstream * normed, axis=0), jnp.sum(upstream, axis=0))


def per_device(
    prompt,
    continuations,
    prev_logits,
    cont_len,
    query_weight,
    query_bias,
    key_weight,
    value_weight,
    value_bias,
    output_weight,
    output_bias,
    first_gain,
    first_shift,
    up_weight,
    up_bias,
    down_weight,
    down_bias,
    second_gain,
    second_shift,
    cot_prompt,
    cot_conts,
    cot_logits,
):
    (
        query_mat,
        query_add,
        key_mat,
        value_mat,
        value_add,
        output_mat,
        output_add,
        gain_one,
        shift_one,
        up_mat,
        up_add,
        down_mat,
        down_add,
        gain_two,
        shift_two,
    ) = (
        lax.all_gather(query_weight, "fsdp", axis=0, tiled=True),
        lax.all_gather(query_bias, "fsdp", axis=1, tiled=True),
        lax.all_gather(key_weight, "fsdp", axis=0, tiled=True),
        lax.all_gather(value_weight, "fsdp", axis=0, tiled=True),
        lax.all_gather(value_bias, "fsdp", axis=1, tiled=True),
        lax.all_gather(output_weight, "fsdp", axis=1, tiled=True),
        lax.all_gather(output_bias, "fsdp", axis=0, tiled=True),
        lax.all_gather(first_gain, "fsdp", axis=0, tiled=True),
        lax.all_gather(first_shift, "fsdp", axis=0, tiled=True),
        lax.all_gather(up_weight, "fsdp", axis=0, tiled=True),
        lax.all_gather(up_bias, "fsdp", axis=1, tiled=True),
        lax.all_gather(down_weight, "fsdp", axis=1, tiled=True),
        lax.all_gather(down_bias, "fsdp", axis=0, tiled=True),
        lax.all_gather(second_gain, "fsdp", axis=0, tiled=True),
        lax.all_gather(second_shift, "fsdp", axis=0, tiled=True),
    )
    gain_one = gain_one.astype(jnp.float32)
    gain_two = gain_two.astype(jnp.float32)
    prompt_len = prompt.shape[1]
    cont_size = continuations.shape[2]
    head_count = query_add.shape[0]
    scale = 1.0 / math.sqrt(query_add.shape[1])
    inputs = jnp.concatenate([prompt[0], continuations[0, 0]], 0)
    query_rows = (product(inputs, query_mat) + query_add.reshape(-1).astype(jnp.float32)).astype(
        jnp.bfloat16
    )
    key_rows = product(inputs, key_mat).astype(jnp.bfloat16)
    value_rows = (product(inputs, value_mat) + value_add.reshape(-1).astype(jnp.float32)).astype(
        jnp.bfloat16
    )
    all_keys, all_values = (
        lax.all_gather(key_rows[:prompt_len], "ctx", axis=0, tiled=True),
        lax.all_gather(value_rows[:prompt_len], "ctx", axis=0, tiled=True),
    )
    full_len = all_keys.shape[0]
    query_prompt = split_heads(query_rows[:prompt_len], head_count)
    query_cont = split_heads(query_rows[prompt_len:], head_count)
    key_prompt = split_heads(all_keys, head_count)
    value_prompt = split_heads(all_values, head_count)
    key_cont = split_heads(jnp.concatenate([all_keys, key_rows[prompt_len:]], 0), head_count)
    value_cont = split_heads(jnp.concatenate([all_values, value_rows[prompt_len:]], 0), head_count)
    column = lax.broadcasted_iota(jnp.int32, (1, 1, full_len + cont_size), 2)
    live_cols = (column < full_len) | (column - full_len < cont_len[0, 0])

    def prompt_scores():
        return (
            jnp.einsum("qhd,khd->hqk", query_prompt, key_prompt, preferred_element_type=jnp.float32)
            * scale
        )

    def cont_scores():
        return (
            prev_logits[0, 0].astype(jnp.float32)
            + jnp.einsum("qhd,khd->hqk", query_cont, key_cont, preferred_element_type=jnp.float32)
            * scale
        )

    raw_scores = cont_scores()
    new_logits = raw_scores.astype(jnp.bfloat16)[None, None]
    probs_prompt, logsum_prompt = soft_rows(prompt_scores())
    probs_cont, logsum_cont = soft_rows(jnp.where(live_cols, raw_scores, -1e30))
    out_prompt = jnp.einsum(
        "hqk,khd->qhd",
        probs_prompt.astype(jnp.bfloat16),
        value_prompt,
        preferred_element_type=jnp.float32,
    )
    out_cont = jnp.einsum(
        "hqk,khd->qhd",
        probs_cont.astype(jnp.bfloat16),
        value_cont,
        preferred_element_type=jnp.float32,
    )
    attended = jnp.concatenate(
        [out_prompt.reshape(prompt_len, -1), out_cont.reshape(cont_size, -1)], 0
    ).astype(jnp.bfloat16)
    branch = lax.psum(product(attended, output_mat).astype(jnp.bfloat16), "tp").astype(
        jnp.float32
    ) + output_add.astype(jnp.float32)
    first_out, first_norm, first_inv = norm_forward(
        inputs.astype(jnp.float32) + branch, gain_one, shift_one.astype(jnp.float32)
    )
    first_low = first_out.astype(jnp.bfloat16)
    inner_act = product(first_low, up_mat) + up_add.reshape(-1).astype(jnp.float32)
    activated = jax.nn.gelu(inner_act, approximate=False).astype(jnp.bfloat16)
    second = lax.psum(product(activated, down_mat).astype(jnp.bfloat16), "tp").astype(
        jnp.float32
    ) + down_add.astype(jnp.float32)
    result, second_norm, second_inv = norm_forward(
        first_out + second, gain_two, shift_two.astype(jnp.float32)
    )
    result_low = result.astype(jnp.bfloat16)
    query_held, key_held, value_held, output_held, up_held, down_held, result_held = (
        lax.optimization_barrier(
            (
                query_weight,
                key_weight,
                value_weight,
                output_weight,
                up_weight,
                down_weight,
                result_low,
            )
        )
    )
    query_mat, key_mat, value_mat, output_mat, up_mat, down_mat = (
        lax.all_gather(query_held, "fsdp", axis=0, tiled=True),
        lax.all_gather(key_held, "fsdp", axis=0, tiled=True),
        lax.all_gather(value_held, "fsdp", axis=0, tiled=True),
        lax.all_gather(output_held, "fsdp", axis=1, tiled=True),
        lax.all_gather(up_held, "fsdp", axis=0, tiled=True),
        lax.all_gather(down_held, "fsdp", axis=1, tiled=True),
    )
    upstream = jnp.concatenate([cot_prompt[0], cot_conts[0, 0]], 0).astype(jnp.float32)
    grad_second, gain_two_grad, shift_two_grad = norm_backward(
        upstream, second_norm, second_inv, gain_two
    )
    down_low = grad_second.astype(jnp.bfloat16)
    down_add_grad = jnp.sum(down_low.astype(jnp.float32), axis=0)
    down_mat_grad = contract_rows(activated, down_low)
    act_grad = contract_cols(down_low, down_mat)
    gelu_value, gelu_pull = jax.vjp(
        lambda pre_act: jax.nn.gelu(pre_act, approximate=False), inner_act
    )
    inner_low = gelu_pull(act_grad)[0].astype(jnp.bfloat16)
    up_mat_grad = contract_rows(first_low, inner_low)
    up_add_grad = jnp.sum(inner_low.astype(jnp.float32), axis=0).reshape(up_add.shape)
    first_grad = grad_second + lax.psum(
        contract_cols(inner_low, up_mat).astype(jnp.bfloat16), "tp"
    ).astype(jnp.float32)
    grad_first, gain_one_grad, shift_one_grad = norm_backward(
        first_grad, first_norm, first_inv, gain_one
    )
    branch_low = grad_first.astype(jnp.bfloat16)
    output_add_grad = jnp.sum(branch_low.astype(jnp.float32), axis=0)
    output_mat_grad = contract_rows(attended, branch_low)
    attended_grad = contract_cols(branch_low, output_mat).astype(jnp.bfloat16)
    dout_prompt = split_heads(attended_grad[:prompt_len], head_count)
    dout_cont = split_heads(attended_grad[prompt_len:], head_count)
    probs_p = jnp.exp(prompt_scores() - logsum_prompt)
    dprob_p = jnp.einsum(
        "qhd,khd->hqk", dout_prompt, value_prompt, preferred_element_type=jnp.float32
    )
    dscore_p = (probs_p * (dprob_p - jnp.sum(dprob_p * probs_p, axis=-1, keepdims=True))).astype(
        jnp.bfloat16
    )
    grad_query_prompt = (
        jnp.einsum("hqk,khd->qhd", dscore_p, key_prompt, preferred_element_type=jnp.float32) * scale
    )
    grad_key_prompt = (
        jnp.einsum("hqk,qhd->khd", dscore_p, query_prompt, preferred_element_type=jnp.float32)
        * scale
    )
    grad_value_prompt = jnp.einsum(
        "hqk,qhd->khd",
        probs_p.astype(jnp.bfloat16),
        dout_prompt,
        preferred_element_type=jnp.float32,
    )
    probs_c = jnp.exp(jnp.where(live_cols, cont_scores(), -1e30) - logsum_cont)
    dprob_c = jnp.einsum("qhd,khd->hqk", dout_cont, value_cont, preferred_element_type=jnp.float32)
    dscore_c = (
        probs_c * (dprob_c - jnp.sum(dprob_c * probs_c, axis=-1, keepdims=True))
        + cot_logits[0, 0].astype(jnp.float32)
    ).astype(jnp.bfloat16)
    grad_prev = dscore_c[None, None]
    grad_query_cont = (
        jnp.einsum("hqk,khd->qhd", dscore_c, key_cont, preferred_element_type=jnp.float32) * scale
    )
    grad_key_cont = (
        jnp.einsum("hqk,qhd->khd", dscore_c, query_cont, preferred_element_type=jnp.float32) * scale
    )
    grad_value_cont = jnp.einsum(
        "hqk,qhd->khd", probs_c.astype(jnp.bfloat16), dout_cont, preferred_element_type=jnp.float32
    )
    key_part = (grad_key_prompt + grad_key_cont[:full_len]).reshape(full_len, -1)
    value_part = (grad_value_prompt + grad_value_cont[:full_len]).reshape(full_len, -1)
    key_mine, value_mine = (
        lax.psum_scatter(
            key_part.astype(jnp.bfloat16), "ctx", scatter_dimension=0, tiled=True
        ).astype(jnp.float32),
        lax.psum_scatter(
            value_part.astype(jnp.bfloat16), "ctx", scatter_dimension=0, tiled=True
        ).astype(jnp.float32),
    )
    query_low = jnp.concatenate(
        [grad_query_prompt.reshape(prompt_len, -1), grad_query_cont.reshape(cont_size, -1)], 0
    ).astype(jnp.bfloat16)
    key_low = jnp.concatenate(
        [key_mine, grad_key_cont[full_len:].reshape(cont_size, -1)], 0
    ).astype(jnp.bfloat16)
    value_low = jnp.concatenate(
        [value_mine, grad_value_cont[full_len:].reshape(cont_size, -1)], 0
    ).astype(jnp.bfloat16)
    query_mat_grad = contract_rows(inputs, query_low)
    query_add_grad = jnp.sum(query_low.astype(jnp.float32), axis=0).reshape(query_add.shape)
    key_mat_grad = contract_rows(inputs, key_low)
    value_mat_grad = contract_rows(inputs, value_low)
    value_add_grad = jnp.sum(value_low.astype(jnp.float32), axis=0).reshape(value_add.shape)
    input_grad = grad_first + lax.psum(
        (
            contract_cols(query_low, query_mat)
            + contract_cols(key_low, key_mat)
            + contract_cols(value_low, value_mat)
        ).astype(jnp.bfloat16),
        "tp",
    ).astype(jnp.float32)
    shards = (
        lax.psum_scatter(
            query_mat_grad.astype(jnp.bfloat16), "fsdp", scatter_dimension=0, tiled=True
        ).astype(jnp.float32),
        lax.psum_scatter(
            query_add_grad.astype(jnp.bfloat16), "fsdp", scatter_dimension=1, tiled=True
        ).astype(jnp.float32),
        lax.psum_scatter(
            key_mat_grad.astype(jnp.bfloat16), "fsdp", scatter_dimension=0, tiled=True
        ).astype(jnp.float32),
        lax.psum_scatter(
            value_mat_grad.astype(jnp.bfloat16), "fsdp", scatter_dimension=0, tiled=True
        ).astype(jnp.float32),
        lax.psum_scatter(
            value_add_grad.astype(jnp.bfloat16), "fsdp", scatter_dimension=1, tiled=True
        ).astype(jnp.float32),
        lax.psum_scatter(
            output_mat_grad.astype(jnp.bfloat16), "fsdp", scatter_dimension=1, tiled=True
        ).astype(jnp.float32),
        lax.psum_scatter(
            output_add_grad.astype(jnp.bfloat16), "fsdp", scatter_dimension=0, tiled=True
        ).astype(jnp.float32),
        lax.psum_scatter(
            gain_one_grad.astype(jnp.bfloat16), "fsdp", scatter_dimension=0, tiled=True
        ).astype(jnp.float32),
        lax.psum_scatter(
            shift_one_grad.astype(jnp.bfloat16), "fsdp", scatter_dimension=0, tiled=True
        ).astype(jnp.float32),
        lax.psum_scatter(
            up_mat_grad.astype(jnp.bfloat16), "fsdp", scatter_dimension=0, tiled=True
        ).astype(jnp.float32),
        lax.psum_scatter(
            up_add_grad.astype(jnp.bfloat16), "fsdp", scatter_dimension=1, tiled=True
        ).astype(jnp.float32),
        lax.psum_scatter(
            down_mat_grad.astype(jnp.bfloat16), "fsdp", scatter_dimension=1, tiled=True
        ).astype(jnp.float32),
        lax.psum_scatter(
            down_add_grad.astype(jnp.bfloat16), "fsdp", scatter_dimension=0, tiled=True
        ).astype(jnp.float32),
        lax.psum_scatter(
            gain_two_grad.astype(jnp.bfloat16), "fsdp", scatter_dimension=0, tiled=True
        ).astype(jnp.float32),
        lax.psum_scatter(
            shift_two_grad.astype(jnp.bfloat16), "fsdp", scatter_dimension=0, tiled=True
        ).astype(jnp.float32),
    )
    summed = (
        lax.psum(shards[0].astype(jnp.bfloat16), "ctx").astype(jnp.float32),
        lax.psum(shards[1].astype(jnp.bfloat16), "ctx").astype(jnp.float32),
        lax.psum(shards[2].astype(jnp.bfloat16), "ctx").astype(jnp.float32),
        lax.psum(shards[3].astype(jnp.bfloat16), "ctx").astype(jnp.float32),
        lax.psum(shards[4].astype(jnp.bfloat16), "ctx").astype(jnp.float32),
        lax.psum(shards[5].astype(jnp.bfloat16), "ctx").astype(jnp.float32),
        lax.psum(shards[6].astype(jnp.bfloat16), "ctx").astype(jnp.float32),
        lax.psum(shards[7].astype(jnp.bfloat16), "ctx").astype(jnp.float32),
        lax.psum(shards[8].astype(jnp.bfloat16), "ctx").astype(jnp.float32),
        lax.psum(shards[9].astype(jnp.bfloat16), "ctx").astype(jnp.float32),
        lax.psum(shards[10].astype(jnp.bfloat16), "ctx").astype(jnp.float32),
        lax.psum(shards[11].astype(jnp.bfloat16), "ctx").astype(jnp.float32),
        lax.psum(shards[12].astype(jnp.bfloat16), "ctx").astype(jnp.float32),
        lax.psum(shards[13].astype(jnp.bfloat16), "ctx").astype(jnp.float32),
        lax.psum(shards[14].astype(jnp.bfloat16), "ctx").astype(jnp.float32),
    )
    return (
        result_low[:prompt_len][None],
        result_low[prompt_len:][None, None],
        new_logits,
        input_grad[:prompt_len][None],
        input_grad[prompt_len:][None, None],
        grad_prev,
        summed[0],
        summed[1],
        summed[2],
        summed[3],
        summed[4],
        summed[5],
        summed[6],
        summed[7],
        summed[8],
        summed[9],
        summed[10],
        summed[11],
        summed[12],
        summed[13],
        summed[14],
    )


def solution(mesh):
    return jax.shard_map(
        per_device,
        mesh=mesh,
        in_specs=(
            P("fsdp", "ctx", None),
            P("fsdp", "ctx", None, None),
            P("fsdp", "ctx", "tp", None, None),
            P("fsdp", "ctx"),
            P("fsdp", "tp"),
            P("tp", "fsdp"),
            P("fsdp", "tp"),
            P("fsdp", "tp"),
            P("tp", "fsdp"),
            P("tp", "fsdp"),
            P("fsdp"),
            P("fsdp"),
            P("fsdp"),
            P("fsdp", "tp"),
            P("tp", "fsdp"),
            P("tp", "fsdp"),
            P("fsdp"),
            P("fsdp"),
            P("fsdp"),
            P("fsdp", "ctx", None),
            P("fsdp", "ctx", None, None),
            P("fsdp", "ctx", "tp", None, None),
        ),
        out_specs=(
            P("fsdp", "ctx", None),
            P("fsdp", "ctx", None, None),
            P("fsdp", "ctx", "tp", None, None),
            P("fsdp", "ctx", None),
            P("fsdp", "ctx", None, None),
            P("fsdp", "ctx", "tp", None, None),
            P("fsdp", "tp"),
            P("tp", "fsdp"),
            P("fsdp", "tp"),
            P("fsdp", "tp"),
            P("tp", "fsdp"),
            P("tp", "fsdp"),
            P("fsdp"),
            P("fsdp"),
            P("fsdp"),
            P("fsdp", "tp"),
            P("tp", "fsdp"),
            P("tp", "fsdp"),
            P("fsdp"),
            P("fsdp"),
            P("fsdp"),
        ),
        check_vma=False,
    )
```

profile of v0, /device:TPU:8, one launch (start us, length us, event | category | flops | bytes accessed | tf_op | source)
XLA Modules:
  0.0 1139.2 jit_solution(9417707215432942518)
XLA Ops:
  8.1 29.1 %all_gather.74 = bf16[768,384]{1,0:T(8,128)(2,1)S(1)} all-gather(bf16[96,384]{1,0:T(8,128)(2,1)} %param.28), channel_id=1, replica_groups=mesh['fsdp'=8,'ctx'=2,'tp'=2] {'fsdp'}, dimensions={0}, use_global_device_ids=true | all-gather | bytes 663552 | tf_op jit(solution)/shard_map/all_gather | solution.py:97
  39.4 31.4 %all_gather.69 = bf16[768,384]{1,0:T(8,128)(2,1)S(1)} all-gather(bf16[96,384]{1,0:T(8,128)(2,1)S(1)} %copy-done.45), channel_id=1, replica_groups=mesh['fsdp'=8,'ctx'=2,'tp'=2] {'fsdp'}, dimensions={0}, use_global_device_ids=true | all-gather | bytes 663552 | tf_op jit(solution)/shard_map/all_gather | solution.py:98
  70.9 27.8 %all_gather.70 = bf16[6,64]{0,1:T(8,128)(2,1)S(1)} all-gather(bf16[6,8]{0,1:T(8,128)(2,1)S(1)} %copy.72), channel_id=1, replica_groups=mesh['fsdp'=8,'ctx'=2,'tp'=2] {'fsdp'}, dimensions={1}, use_global_device_ids=true | all-gather | bytes 864 | tf_op jit(solution)/shard_map/all_gather | solution.py:99
  101.2 29.6 %all_gather.72 = bf16[768,384]{1,0:T(8,128)(2,1)S(1)} all-gather(bf16[96,384]{1,0:T(8,128)(2,1)S(1)} %copy-done.43), channel_id=1, replica_groups=mesh['fsdp'=8,'ctx'=2,'tp'=2] {'fsdp'}, dimensions={0}, use_global_device_ids=true | all-gather | bytes 663552 | tf_op jit(solution)/shard_map/all_gather | solution.py:95
  130.9 27.6 %all_gather.73 = bf16[6,64]{0,1:T(8,128)(2,1)S(1)} all-gather(bf16[6,8]{0,1:T(8,128)(2,1)S(1)} %copy.75), channel_id=1, replica_groups=mesh['fsdp'=8,'ctx'=2,'tp'=2] {'fsdp'}, dimensions={1}, use_global_device_ids=true | all-gather | bytes 864 | tf_op jit(solution)/shard_map/all_gather | solution.py:96
  160.2 8.4 all_gather.75
  172.3 3.9 select_reduce_fusion
  176.3 3.8 convert_bitcast_fusion
  181.2 8.4 all_gather.71
  200.0 30.0 %all_gather.76 = bf16[384,768]{0,1:T(8,128)(2,1)S(1)} all-gather(bf16[384,96]{0,1:T(8,128)(2,1)S(1)} %copy-done.41), channel_id=1, replica_groups=mesh['fsdp'=8,'ctx'=2,'tp'=2] {'fsdp'}, dimensions={1}, use_global_device_ids=true | all-gather | bytes 663552 | tf_op jit(solution)/shard_map/all_gather | solution.py:100
  230.0 4.8 convolution_convert_fusion.12
  244.1 35.2 %all-reduce.15 = (bf16[768]{0:T(1024)(128)(2,1)S(1)}, bf16[768]{0:T(1024)(128)(2,1)S(1)}, bf16[768]{0:T(1024)(128)(2,1)S(1)}, bf16[768]{0:T(1024)(128)(2,1)S(1)}...) all-reduce(bf16[768]{0:T(1024)(128)(2,1)S(1)} %dynamic-update-slice, ...), channel_id=1, replica_groups=mesh['fsdp'=8,'ctx'=2,'tp'=2] {'fsdp'}, use_global_device_ids=true, to_apply=%add.2 | all-reduce | flops 4608 | bytes 18432
  279.4 31.1 %all_gather.81 = bf16[12,128]{0,1:T(8,128)(2,1)S(1)} all-gather(bf16[12,16]{0,1:T(8,128)(2,1)S(1)} %copy.80), channel_id=1, replica_groups=mesh['fsdp'=8,'ctx'=2,'tp'=2] {'fsdp'}, dimensions={1}, use_global_device_ids=true | all-gather | bytes 3456 | tf_op jit(solution)/shard_map/all_gather | solution.py:105
  313.2 16.1 %multiply_convert_fusion.1 = (bf16[768,1536]{1,0:T(8,128)(2,1)}, f32[768,1536]{1,0:T(8,128)}, f32[768,1536]{1,0:T(8,128)}) fusion(f32[1536]{0:T(1024)S(1)} %bitcast_convert_fusion, bf16[768,1536]{1,0:T(8,128)(2,1)} %all-gather.5.cloned.1.call-done, f32[768]{0:T(1024)S(1)} %convert_element_type.294, f32[768]{0:T(1024)S(1)} %convert_element_type.293, ...), kind=kOutput, calls=%fused_computation.19 | convolution fusion | flops 1896873984 | bytes 16536576 | tf_op jit(solution)/shard_map/dot_general | solution.py:12
  329.3 18.9 %all-gather.7.cloned.1.call-done = bf16[1536,768]{0,1:T(8,128)(2,1)} async-done(((bf16[1536,96]{0,1:T(8,128)(2,1)}), bf16[1536,768]{0,1:T(8,128)(2,1)}) %all-gather.7.cloned.1.call-update) | async-done | bytes 2359312 | tf_op jit(solution)/shard_map/all_gather | solution.py:106
  348.2 5.4 convolution_convert_fusion.4
  355.9 16.4 %all-reduce.26.cloned.1.call-done = bf16[768,768]{1,0:T(8,128)(2,1)} async-done(((bf16[768,768]{1,0:T(8,128)(2,1)}), bf16[768,768]{1,0:T(8,128)(2,1)}) %all-reduce.26.cloned.1.call-update) | async-done | bytes 1179664 | tf_op jit(solution)/shard_map/psum | solution.py:180
  376.3 3.1 fusion.23
  380.9 4.0 convert_reduce_fusion.1
  384.9 47.2 %all-gather.9.cloned.1.call-done = bf16[1536,768]{0,1:T(8,128)(2,1)} async-done(((bf16[1536,96]{0,1:T(8,128)(2,1)}), bf16[1536,768]{0,1:T(8,128)(2,1)}) %all-gather.9.cloned.1.call-update) | async-done | bytes 2359312 | tf_op jit(solution)/shard_map/all_gather | solution.py:206
  432.1 10.4 fusion.70
  442.5 42.0 %all-gather.11.cloned.1.call-done = bf16[768,1536]{1,0:T(8,128)(2,1)} async-done(((bf16[96,1536]{1,0:T(8,128)(2,1)}), bf16[768,1536]{1,0:T(8,128)(2,1)}) %all-gather.11.cloned.1.call-update) | async-done | bytes 2359312 | tf_op jit(solution)/shard_map/all_gather | solution.py:205
  484.6 5.6 convolution_convert_fusion.3
  490.2 31.1 %all_gather.88 = bf16[384,768]{0,1:T(8,128)(2,1)} all-gather(bf16[384,96]{0,1:T(8,128)(2,1)} %param.31), channel_id=1, replica_groups=mesh['fsdp'=8,'ctx'=2,'tp'=2] {'fsdp'}, dimensions={1}, use_global_device_ids=true | all-gather | bytes 663552 | tf_op jit(solution)/shard_map/all_gather | solution.py:204
  521.5 4.0 multiply_reduce_fusion.3
  528.7 4.9 convolution_bitcast_fusion
  533.7 7.0 multiply_reduce_fusion
  540.7 3.5 fusion.26
  544.3 13.4 %fusion.2 = bf16[6,256,1280]{2,1,0:T(8,128)(2,1)} fusion(f32[6,256,1280]{2,1,0:T(8,128)} %copy-done.1, bf16[1,1,6,256,1280]{4,3,2,1,0:T(8,128)(2,1)} %param.43, f32[6,256]{1,0:T(8,128)} %log_add_fusion.1, pred[1280]{0:T(1024)(128)(4,1)} %copy-done.65, bf16[256,6,64]{0,2,1:T(8,128)(2,1)} %bitcast.167, bf16[1280,6,64]{0,2,1:T(8,128)(2,1)} %bitcast.158), kind=kOutput, calls=%fused_computation.8 | convolution fusion | flops 522980096 | bytes 16915712 | tf_op jit(solution)/shard_map/sub | solution.py:257
  557.7 3.1 fusion.16
  560.8 10.2 multiply_convert_fusion
  575.1 5.9 convolution_convert_fusion
  584.0 4.4 bitcast_reduce_fusion.1
  588.5 5.6 bitcast_reduce_fusion
  603.7 3.1 convolution_convert_fusion.7
  606.9 5.9 convolution_convert_fusion.1
  613.6 31.7 %all_gather.90 = bf16[768,384]{1,0:T(8,128)(2,1)S(1)} all-gather(bf16[96,384]{1,0:T(8,128)(2,1)S(1)} %copy-done.42), channel_id=1, replica_groups=mesh['fsdp'=8,'ctx'=2,'tp'=2] {'fsdp'}, dimensions={0}, use_global_device_ids=true | all-gather | bytes 663552 | tf_op jit(solution)/shard_map/all_gather | solution.py:202
  645.3 32.7 %all_gather.89 = bf16[768,384]{1,0:T(8,128)(2,1)S(1)} all-gather(bf16[96,384]{1,0:T(8,128)(2,1)S(1)} %copy-done.44), channel_id=1, replica_groups=mesh['fsdp'=8,'ctx'=2,'tp'=2] {'fsdp'}, dimensions={0}, use_global_device_ids=true | all-gather | bytes 663552 | tf_op jit(solution)/shard_map/all_gather | solution.py:201
  678.0 32.5 %all_gather.91 = bf16[768,384]{1,0:T(8,128)(2,1)S(1)} all-gather(bf16[96,384]{1,0:T(8,128)(2,1)S(1)} %copy-done.46), channel_id=1, replica_groups=mesh['fsdp'=8,'ctx'=2,'tp'=2] {'fsdp'}, dimensions={0}, use_global_device_ids=true | all-gather | bytes 663552 | tf_op jit(solution)/shard_map/all_gather | solution.py:203
  722.4 34.5 %all-reduce.14 = (bf16[6,64]{1,0:T(8,128)(2,1)S(1)}, bf16[6,64]{1,0:T(8,128)(2,1)S(1)}, bf16[768]{0:T(1024)(128)(2,1)S(1)}, bf16[768]{0:T(1024)(128)(2,1)S(1)}, ...) all-reduce(bf16[6,64]{1,0:T(8,128)(2,1)S(1)} %reduce_sum.258, ...), channel_id=5, replica_groups=mesh['fsdp'=8,'ctx'=2,'tp'=2] {'fsdp'}, use_global_device_ids=true, to_apply=%region_24.25.clone | all-reduce | flops 5376 | bytes 21504
  757.5 8.3 all-reduce.16
  770.7 21.3 %reduce-scatter.24.cloned.1.call-done = bf16[384,96]{0,1:T(8,128)(2,1)} async-done(((bf16[384,768]{0,1:T(8,128)(2,1)}), bf16[384,96]{0,1:T(8,128)(2,1)}) %reduce-scatter.24.cloned.1.call-update) | async-done | bytes 73744 | tf_op jit(solution)/shard_map/reduce_scatter | solution.py:318
  791.9 65.6 %reduce-scatter.18.cloned.1.call-done = bf16[96,384]{1,0:T(8,128)(2,1)} async-done(((bf16[768,384]{1,0:T(8,128)(2,1)}), bf16[96,384]{1,0:T(8,128)(2,1)}) %reduce-scatter.18.cloned.1.call-update) | async-done | bytes 73744 | tf_op jit(solution)/shard_map/reduce_scatter | solution.py:303
  857.5 65.4 %reduce-scatter.22.cloned.1.call-done = bf16[96,384]{1,0:T(8,128)(2,1)} async-done(((bf16[768,384]{1,0:T(8,128)(2,1)}), bf16[96,384]{1,0:T(8,128)(2,1)}) %reduce-scatter.22.cloned.1.call-update) | async-done | bytes 73744 | tf_op jit(solution)/shard_map/reduce_scatter | solution.py:312
  923.0 65.6 %reduce-scatter.20.cloned.1.call-done = bf16[96,384]{1,0:T(8,128)(2,1)} async-done(((bf16[768,384]{1,0:T(8,128)(2,1)}), bf16[96,384]{1,0:T(8,128)(2,1)}) %reduce-scatter.20.cloned.1.call-update) | async-done | bytes 73744 | tf_op jit(solution)/shard_map/reduce_scatter | solution.py:309
  988.6 71.5 %reduce-scatter.26.cloned.1.call-done = bf16[96,1536]{1,0:T(8,128)(2,1)} async-done(((bf16[768,1536]{1,0:T(8,128)(2,1)}), bf16[96,1536]{1,0:T(8,128)(2,1)}) %reduce-scatter.26.cloned.1.call-update) | async-done | bytes 294928 | tf_op jit(solution)/shard_map/reduce_scatter | solution.py:330
  1060.1 22.2 %all-reduce.30.cloned.1.call-done = bf16[768,768]{1,0:T(8,128)(2,1)} async-done(((bf16[768,768]{1,0:T(8,128)(2,1)}), bf16[768,768]{1,0:T(8,128)(2,1)}) %all-reduce.30.cloned.1.call-update) | async-done | bytes 1179664 | tf_op jit(solution)/shard_map/psum | solution.py:294
  1086.0 36.4 %all-reduce.32.cloned.1.call-done = (bf16[96,384]{1,0:T(8,128)(2,1)}, bf16[96,384]{1,0:T(8,128)(2,1)}, bf16[96,384]{1,0:T(8,128)(2,1)}, bf16[384,96]{0,1:T(8,128...) async-done(((bf16[96,384]{1,0:T(8,128)(2,1)}, bf16[96,384]{1,0:T(8,128)(2,1)}, bf16[96,384]{1,0:T(8,128)(2,1)}, bf16[384,96]{0,1:T(8,128)(2,1)}, ...) | async-done | bytes 884752 | tf_op jit(solution)/shard_map/psum | solution.py:350
  (339 shorter events, 89.0 us)
Async XLA Ops:
  8.0 302.6 %all-reduce.24.cloned.1.call-start = ((), (), s32[]{:S(2)}) async-start(), calls=%async_computation.9 | async-start | bytes 2359296 | tf_op jit(solution)/shard_map/psum | solution.py:171
  37.2 33.6 %copy-start.79 = (bf16[6,8]{1,0:T(8,128)(2,1)S(1)}, bf16[6,8]{1,0:T(8,128)(2,1)}, u32[]{:S(2)}) copy-start(bf16[6,8]{1,0:T(8,128)(2,1)} %param.30) | copy-start | bytes 292
  37.2 61.7 %copy-start.6 = (bf16[1,512,768]{2,1,0:T(8,128)(2,1)S(1)}, bf16[1,512,768]{2,1,0:T(8,128)(2,1)}, u32[]{:S(2)}) copy-start(bf16[1,512,768]{2,1,0:T(8,128)(2,1)} %param.22) | copy-start | bytes 2359300
  37.2 61.7 %copy-start.9 = (bf16[1,1,256,768]{3,2,1,0:T(8,128)(2,1)S(1)}, bf16[1,1,256,768]{3,2,1,0:T(8,128)(2,1)}, u32[]{:S(2)}) copy-start(bf16[1,1,256,768]{3,2,1,0:T(8,128)(2,1)} %param.23) | copy-start | bytes 1179652
  39.4 60.3 %copy-start.32 = (bf16[768,384]{1,0:T(8,128)(2,1)}, bf16[768,384]{1,0:T(8,128)(2,1)S(1)}, u32[]{:S(2)}) copy-start(bf16[768,384]{1,0:T(8,128)(2,1)S(1)} %convolution_convert_fusion.10) | copy-start | bytes 1769476
  98.9 31.9 %copy-start.80 = (bf16[6,8]{1,0:T(8,128)(2,1)S(1)}, bf16[6,8]{1,0:T(8,128)(2,1)}, u32[]{:S(2)}) copy-start(bf16[6,8]{1,0:T(8,128)(2,1)} %param.27) | copy-start | bytes 292
  159.4 9.6 slice-start.5
  159.4 12.9 %copy-start.26 = (bf16[256,384]{0,1:T(8,128)(2,1)}, bf16[256,384]{0,1:T(8,128)(2,1)S(1)}, u32[]{:S(2)}) copy-start(bf16[256,384]{0,1:T(8,128)(2,1)S(1)} %slice.70) | copy-start | bytes 589828
  168.9 25.4 %copy-start.19 = (bf16[1024,384]{0,1:T(8,128)(2,1)}, bf16[1024,384]{0,1:T(8,128)(2,1)S(1)}, u32[]{:S(2)}) copy-start(bf16[1024,384]{0,1:T(8,128)(2,1)S(1)} %copy.77) | copy-start | bytes 2359300
  189.9 44.9 %copy-start.15 = (bf16[1024,384]{0,1:T(8,128)(2,1)}, bf16[1024,384]{0,1:T(8,128)(2,1)S(1)}, u32[]{:S(2)}) copy-start(bf16[1024,384]{0,1:T(8,128)(2,1)S(1)} %copy.74) | copy-start | bytes 2359300
  197.3 37.5 %copy-start = (f32[6,512,1024]{2,1,0:T(8,128)}, f32[6,512,1024]{2,1,0:T(8,128)S(1)}, u32[]{:S(2)}) copy-start(f32[6,512,1024]{2,1,0:T(8,128)S(1)} %get-tuple-element.87) | copy-start | bytes 37748740
  197.3 32.7 %copy-start.34 = (bf16[1280,384]{0,1:T(8,128)(2,1)S(1)}, bf16[1280,384]{0,1:T(8,128)(2,1)}, u32[]{:S(2)}) copy-start(bf16[1280,384]{0,1:T(8,128)(2,1)} %copy.78) | copy-start | bytes 2949124
  197.3 32.7 %copy-start.66 = (pred[1280]{0:T(1024)(128)(4,1)S(1)}, pred[1280]{0:T(1024)(128)(4,1)}, u32[]{:S(2)}) copy-start(pred[1280]{0:T(1024)(128)(4,1)} %copy-done.65) | copy-start | bytes 3844
  197.3 32.7 %copy-start.68 = (f32[6,256]{1,0:T(8,128)S(1)}, f32[6,256]{1,0:T(8,128)}, u32[]{:S(2)}) copy-start(f32[6,256]{1,0:T(8,128)} %log_add_fusion.1) | copy-start | bytes 18436
  237.7 41.6 %copy-start.77 = (bf16[12,16]{1,0:T(8,128)(2,1)S(1)}, bf16[12,16]{1,0:T(8,128)(2,1)}, u32[]{:S(2)}) copy-start(bf16[12,16]{1,0:T(8,128)(2,1)} %param.36) | copy-start | bytes 1156
  240.2 73.0 %all-gather.5.cloned.1.call-start = ((), (), s32[]{:S(2)}) async-start(), calls=%async_computation.10 | async-start | bytes 2654208 | tf_op jit(solution)/shard_map/all_gather | solution.py:104
  240.8 107.4 %all-gather.7.cloned.1.call-start = ((), (), s32[]{:S(2)}) async-start(), calls=%async_computation.11 | async-start | bytes 2654208 | tf_op jit(solution)/shard_map/all_gather | solution.py:106
  241.4 130.9 %all-reduce.26.cloned.1.call-start = ((), (), s32[]{:S(2)}) async-start(), calls=%async_computation.12 | async-start | bytes 2359296 | tf_op jit(solution)/shard_map/psum | solution.py:180
  279.3 33.9 %copy-start.48 = (f32[768]{0:T(1024)}, f32[768]{0:T(1024)S(1)}, u32[]{:S(2)}) copy-start(f32[768]{0:T(1024)S(1)} %convert_element_type.292) | copy-start | bytes 9220
  279.3 33.9 %copy-start.56 = (f32[768]{0:T(1024)}, f32[768]{0:T(1024)S(1)}, u32[]{:S(2)}) copy-start(f32[768]{0:T(1024)S(1)} %convert_element_type.293) | copy-start | bytes 9220
  279.3 33.9 %copy-start.70 = (f32[768]{0:T(1024)}, f32[768]{0:T(1024)S(1)}, u32[]{:S(2)}) copy-start(f32[768]{0:T(1024)S(1)} %convert_element_type.294) | copy-start | bytes 9220
  312.5 16.8 %copy-start.51 = (f32[768]{0:T(1024)}, f32[768]{0:T(1024)S(1)}, u32[]{:S(2)}) copy-start(f32[768]{0:T(1024)S(1)} %broadcast_multiply_fusion.5) | copy-start | bytes 9220
  313.1 16.1 %copy-start.59 = (f32[768]{0:T(1024)}, f32[768]{0:T(1024)S(1)}, u32[]{:S(2)}) copy-start(f32[768]{0:T(1024)S(1)} %add_rsqrt_fusion.1) | copy-start | bytes 9220
  353.6 78.5 %all-gather.9.cloned.1.call-start = ((), (), s32[]{:S(2)}) async-start(), calls=%async_computation.13 | async-start | bytes 2654208 | tf_op jit(solution)/shard_map/all_gather | solution.py:206
  379.4 105.2 %all-gather.11.cloned.1.call-start = ((), (), s32[]{:S(2)}) async-start(), calls=%async_computation.14 | async-start | bytes 2654208 | tf_op jit(solution)/shard_map/all_gather | solution.py:205
  380.2 141.2 %all-reduce.28.cloned.1.call-start = ((), (), s32[]{:S(2)}) async-start(), calls=%async_computation.15 | async-start | bytes 2359296 | tf_op jit(solution)/shard_map/psum | solution.py:222
  484.6 36.8 %copy-start.4 = (f32[768,768]{1,0:T(8,128)S(1)}, f32[768,768]{1,0:T(8,128)}, u32[]{:S(2)}) copy-start(f32[768,768]{1,0:T(8,128)} %get-tuple-element.70) | copy-start | bytes 7077892
  490.2 108.7 %reduce-scatter.16.cloned.1.call-start = ((), (), s32[]{:S(2)}) async-start(), calls=%async_computation.17 | async-start | bytes 1179648 | tf_op jit(solution)/shard_map/reduce_scatter | solution.py:276
  525.6 8.1 slice-start
  544.2 59.4 %reduce-scatter.14.cloned.1.call-start = ((), (), s32[]{:S(2)}) async-start(), calls=%async_computation.16 | async-start | bytes 1179648 | tf_op jit(solution)/shard_map/reduce_scatter | solution.py:273
  560.8 10.3 copy-start.12
  560.8 10.3 copy-start.22
  574.0 145.9 %reduce-scatter.30.cloned.1.call-start = ((), (), s32[]{:S(2)}) async-start(), calls=%async_computation.25 | async-start | bytes 36864
  574.9 195.8 %reduce-scatter.28.cloned.1.call-start = ((), (), s32[]{:S(2)}) async-start(), calls=%async_computation.24 | async-start | bytes 2654208 | tf_op jit(solution)/shard_map/reduce_scatter | solution.py:336
  581.0 210.9 %reduce-scatter.24.cloned.1.call-start = ((), (), s32[]{:S(2)}) async-start(), calls=%async_computation.22 | async-start | bytes 663552 | tf_op jit(solution)/shard_map/reduce_scatter | solution.py:318
  584.0 273.6 %reduce-scatter.18.cloned.1.call-start = ((), (), s32[]{:S(2)}) async-start(), calls=%async_computation.19 | async-start | bytes 663552 | tf_op jit(solution)/shard_map/reduce_scatter | solution.py:303
  596.5 326.5 %reduce-scatter.22.cloned.1.call-start = ((), (), s32[]{:S(2)}) async-start(), calls=%async_computation.21 | async-start | bytes 663552 | tf_op jit(solution)/shard_map/reduce_scatter | solution.py:312
  601.9 386.7 %reduce-scatter.20.cloned.1.call-start = ((), (), s32[]{:S(2)}) async-start(), calls=%async_computation.20 | async-start | bytes 663552 | tf_op jit(solution)/shard_map/reduce_scatter | solution.py:309
  606.8 453.4 %reduce-scatter.26.cloned.1.call-start = ((), (), s32[]{:S(2)}) async-start(), calls=%async_computation.23 | async-start | bytes 2654208 | tf_op jit(solution)/shard_map/reduce_scatter | solution.py:330
  612.7 32.6 %copy-start.44 = (bf16[96,384]{1,0:T(8,128)(2,1)S(1)}, bf16[96,384]{1,0:T(8,128)(2,1)}, u32[]{:S(2)}) copy-start(bf16[96,384]{1,0:T(8,128)(2,1)} %param.26) | copy-start | bytes 221188
  612.7 65.3 %copy-start.46 = (bf16[96,384]{1,0:T(8,128)(2,1)S(1)}, bf16[96,384]{1,0:T(8,128)(2,1)}, u32[]{:S(2)}) copy-start(bf16[96,384]{1,0:T(8,128)(2,1)} %param.29) | copy-start | bytes 221188
  612.7 97.9 %copy-start.28 = (bf16[6,64,512]{2,1,0:T(8,128)(2,1)S(1)}, bf16[6,64,512]{2,1,0:T(8,128)(2,1)}, u32[]{:S(2)}) copy-start(bf16[6,64,512]{2,1,0:T(8,128)(2,1)} %copy-done.27) | copy-start | bytes 1179652
  612.7 97.8 %copy-start.37 = (bf16[6,64,256]{2,1,0:T(8,128)(2,1)S(1)}, bf16[6,64,256]{2,1,0:T(8,128)(2,1)}, u32[]{:S(2)}) copy-start(bf16[6,64,256]{2,1,0:T(8,128)(2,1)} %copy-done.36) | copy-start | bytes 589828
  612.8 469.6 %all-reduce.30.cloned.1.call-start = ((), (), s32[]{:S(2)}) async-start(), calls=%async_computation.18 | async-start | bytes 2359296 | tf_op jit(solution)/shard_map/psum | solution.py:294
  645.3 66.1 %copy-start.38 = (bf16[256,6,64]{0,2,1:T(8,128)(2,1)S(1)}, bf16[256,6,64]{0,2,1:T(8,128)(2,1)}, u32[]{:S(2)}) copy-start(bf16[256,6,64]{0,2,1:T(8,128)(2,1)} %slice.95) | copy-start | bytes 589828
  645.3 66.1 %copy-start.40 = (bf16[512,384]{0,1:T(8,128)(2,1)S(1)}, bf16[512,384]{0,1:T(8,128)(2,1)}, u32[]{:S(2)}) copy-start(bf16[512,384]{0,1:T(8,128)(2,1)} %reduce-scatter.14.cloned.1.call-done) | copy-start | bytes 1179652
  714.5 407.9 %all-reduce.32.cloned.1.call-start = ((), (), s32[]{:S(2)}) async-start(), calls=%async_computation.26 | async-start | bytes 1769472 | tf_op jit(solution)/shard_map/psum | solution.py:350
  1122.4 8.4 copy-start.54
  (63 other events, 240.2 us)
Sparse Core Ops, SparseCore 0:
  240.3 20.9 all-reduce.23
  353.7 18.4 all-reduce.25
  490.3 18.4 all-reduce.27
  544.4 18.8 reduce-scatter.15
  574.2 18.7 reduce-scatter.13
  596.6 54.8 reduce-scatter.29
  654.9 71.4 reduce-scatter.27
  729.7 62.1 reduce-scatter.23
  795.8 61.6 reduce-scatter.17
  861.2 61.6 reduce-scatter.21
  926.9 61.6 reduce-scatter.19
  991.9 68.1 reduce-scatter.25
  1062.5 19.8 all-reduce.29
  1084.8 37.5 all-reduce.31
Sparse Core Ops, SparseCore 1:
  242.9 52.8 all-gather.4
  297.8 50.3 all-gather.6
  379.5 52.6 all-gather.8
  434.3 50.2 all-gather.10
where the time goes:
time: 1150 us; the launch traced here: 1140 us
  waiting for transfers between devices  475 us (41%)
  blocking collectives  430 us (37%)
  matrix products  128 us (11%)
  other arithmetic  60.9 us (5%)
  local copies, waits for them, and re-layouts  24.5 us (2%)
  between operations  19.9 us (2%)
    reduce_scatter x1, waiting for transfers between devices, per_device(): lax.psum_scatter(up_mat_grad.astype(jnp.bfloat16), 'fsdp', scatter_dimens...  71.5 us
    unnamed x2, blocking collectives  69.6 us
    reduce_scatter x1, waiting for transfers between devices, per_device(): lax.psum_scatter(key_mat_grad.astype(jnp.bfloat16), 'fsdp', scatter_dimen...  65.6 us
    reduce_scatter x1, waiting for transfers between devices, per_device(): lax.psum_scatter(query_mat_grad.astype(jnp.bfloat16), 'fsdp', scatter_dim...  65.6 us
    reduce_scatter x1, waiting for transfers between devices, per_device(): lax.psum_scatter(value_mat_grad.astype(jnp.bfloat16), 'fsdp', scatter_dim...  65.4 us
    all_gather x1, waiting for transfers between devices, per_device(): lax.all_gather(down_held, 'fsdp', axis=1, tiled=True)  47.2 us
    all_gather x1, waiting for transfers between devices, per_device(): lax.all_gather(up_held, 'fsdp', axis=0, tiled=True)  42 us
    psum x1, waiting for transfers between devices, per_device(): lax.psum(shards[0].astype(jnp.bfloat16), 'ctx').astype(jnp.float32)  36.4 us
  transfers between devices with their start and end apart: 18, of which 11 were waited for; matrix products, arithmetic and copies ran while one was open for 11% of the time, Pallas kernels for 0%

commit v1 on v0

v1 whole, which is shorter than its diff:
```python
import math

import jax
import jax.numpy as jnp
from jax import lax
from jax.experimental import pallas as pl
from jax.experimental.pallas import tpu as pltpu
from jax.sharding import PartitionSpec as P

epsilon = 1e-06
f32 = jnp.float32
bf16 = jnp.bfloat16
LANES = 128


def product(left_mat, right_mat):
    return jnp.dot(left_mat, right_mat, preferred_element_type=f32)


def contract_rows(left_mat, right_mat):
    return lax.dot_general(
        left_mat, right_mat, (((0,), (0,)), ((), ())), preferred_element_type=f32
    )


def contract_cols(left_mat, right_mat):
    return lax.dot_general(
        left_mat, right_mat, (((1,), (1,)), ((), ())), preferred_element_type=f32
    )


class Grid:
    def __init__(self, sizes):
        self.fsdp, self.ctx, self.tp = sizes
        self.staged = sizes == (8, 2, 2)
        place = lax.axis_index("fsdp")
        self.outer, self.inner = place // 2, place % 2
        self.row = lax.axis_index("ctx")
        self.core = lax.axis_index("tp")
        self.place = jnp.stack([self.outer, self.inner, self.row]).astype(jnp.int32)

    def over_inner(self, array):
        return lax.ppermute(array, "fsdp", [(i, i ^ 1) for i in range(8)])

    def over_outer(self, array, step):
        return lax.ppermute(array, "fsdp", [(i, i ^ (2 * step)) for i in range(8)])

    def over_ctx(self, array):
        return lax.ppermute(array, "ctx", [(0, 1), (1, 0)])

    def over_tp(self, array):
        return lax.ppermute(array, "tp", [(0, 1), (1, 0)])

    def tp_sum(self, partial):
        low = partial.astype(bf16)
        return low.astype(f32) + self.over_tp(low).astype(f32)


def assemble(place, cuts, own, across, along, far_one, far_two):
    half = own.shape[1]
    edges = [sum(cuts[:i]) for i in range(len(cuts) + 1)]

    def body(place_ref, own_ref, across_ref, along_ref, one_ref, two_ref, *outs):
        outer, inner, row = place_ref[0], place_ref[1], place_ref[2]

        def put(piece, at_piece, step, swap_inner, swap_row):
            at = ((outer ^ step) * 2 + (inner ^ swap_inner)) * 2 + (row ^ swap_row)
            here = pl.ds(pl.multiple_of(at * half, 16), half)
            for out, low, high in zip(outs, edges, edges[1:]):
                out[here, :] = piece[at_piece, :, low:high]

        for step in range(4):
            put(own_ref, step, step, 0, 0)
            put(across_ref, step, step, 1, 0)
            put(along_ref, step, step, 0, 1)
            put(one_ref if step < 2 else two_ref, step % 2, step, 1, 1)

    vmem = pl.BlockSpec(memory_space=pltpu.VMEM)
    outs = [like((16 * half, cols), own.dtype) for cols in cuts]
    return pl.pallas_call(
        body,
        out_shape=outs,
        in_specs=[pl.BlockSpec(memory_space=pltpu.SMEM)] + [vmem] * 5,
        out_specs=[vmem] * len(outs),
        compiler_params=pltpu.CompilerParams(vmem_limit_bytes=VMEM_LIMIT),
        cost_estimate=cost(0, *outs, *outs),
        name="assemble",
    )(place, own, across, along, far_one, far_two)


def gather_rows(grid, early, late):
    cuts = [[a.shape[1] for a in arrays] for arrays in (early, late)]
    if not grid.staged:
        return [[lax.all_gather(a, "fsdp", axis=0, tiled=True) for a in arrays] for arrays in (early, late)]
    early, late = [jnp.concatenate(arrays, 1) for arrays in (early, late)]
    half = early.shape[0] // 2

    def lines(mine):
        return [grid.over_outer(mine, step) for step in (1, 2, 3)]

    def pairs(own):
        return grid.over_inner(own), grid.over_ctx(own)

    def corners(across, along):
        return grid.over_ctx(across[:2]), grid.over_inner(along[2:])

    mine, late_mine = [
        lax.dynamic_slice_in_dim(a, grid.row * half, half, 0) for a in (early, late)
    ]
    came = lines(mine)
    came, late_mine = lax.optimization_barrier((came, late_mine))
    own = jnp.stack([mine] + came)
    across, along = pairs(own)
    far = corners(across, along)
    late_came = lines(late_mine)
    far, late_came = lax.optimization_barrier((far, late_came))
    late_own = jnp.stack([late_mine] + late_came)
    late_pairs = pairs(late_own)
    late_far = corners(*late_pairs)
    return (
        assemble(grid.place, cuts[0], own, across, along, *far),
        assemble(grid.place, cuts[1], late_own, *late_pairs, *late_far),
    )


def pick(array, at, axis):
    return lax.dynamic_index_in_dim(array, at, axis, keepdims=False)


def add_low(left, right):
    return (left.astype(f32) + right.astype(f32)).astype(bf16)


VMEM_LIMIT = 60 * 1024 * 1024


def whole_block(array):
    rank = array.ndim
    return pl.BlockSpec(array.shape, lambda *_: (0,) * rank)


def cost(flops, *arrays, transcendentals=0):
    moved = sum(math.prod(a.shape) * jnp.dtype(a.dtype).itemsize for a in arrays)
    return pl.CostEstimate(
        flops=int(flops), transcendentals=int(transcendentals), bytes_accessed=int(moved)
    )


def like(shape, dtype):
    return jax.ShapeDtypeStruct(shape, dtype)


def norm_rows(hidden_in):
    centre = jnp.mean(hidden_in, axis=-1, keepdims=True)
    shifted = hidden_in - centre
    spread = jnp.mean(shifted * shifted, axis=-1, keepdims=True)
    inverse = lax.rsqrt(spread + epsilon)
    return shifted * inverse, inverse


def norm_pull(upstream, normed, inverse, gain):
    scaled = upstream * gain
    mean_one = jnp.mean(scaled, axis=-1, keepdims=True)
    mean_two = jnp.mean(scaled * normed, axis=-1, keepdims=True)
    return inverse * (scaled - mean_one - normed * mean_two)


def column_sums(values):
    return jnp.sum(values, axis=0, keepdims=True)


def row_tile(rows):
    return 256 if rows % 256 == 0 else rows


def ffn_forward(inputs, part, other, output_add, gain, shift, up_mat, up_add, down_turned):
    rows, width = inputs.shape
    hidden = up_mat.shape[1]
    tile = row_tile(rows)

    def body(x, p, o, b, g, s, up, ub, dn, norm_out, inv_out, act_out, slope_out, part_out):
        hidden_in = x[...].astype(f32) + (p[...].astype(f32) + o[...].astype(f32)) + b[...]
        normed, inverse = norm_rows(hidden_in)
        norm_out[...] = normed
        inv_out[...] = jnp.broadcast_to(inverse, inv_out.shape)
        low = (normed * g[...] + s[...]).astype(bf16)
        inner = product(low, up[...]) + ub[...]
        normal_cdf = 0.5 * (1.0 + lax.erf(inner * math.sqrt(0.5)))
        act = (inner * normal_cdf).astype(bf16)
        act_out[...] = act
        density = jnp.exp(-0.5 * inner * inner) * (1.0 / math.sqrt(2.0 * math.pi))
        slope_out[...] = (normal_cdf + inner * density).astype(bf16)
        part_out[...] = contract_cols(act, dn[...]).astype(bf16)

    outs = [
        like((rows, width), f32),
        like((rows, LANES), f32),
        like((rows, hidden), bf16),
        like((rows, hidden), bf16),
        like((rows, width), bf16),
    ]

    def tiled(array):
        return pl.BlockSpec((tile, array.shape[1]), lambda i: (i, 0))

    args = [inputs, part, other, output_add, gain, shift, up_mat, up_add, down_turned]
    return pl.pallas_call(
        body,
        grid=(rows // tile,),
        out_shape=outs,
        in_specs=[tiled(a) for a in args[:3]] + [whole_block(a) for a in args[3:]],
        out_specs=[tiled(a) for a in outs],
        compiler_params=pltpu.CompilerParams(vmem_limit_bytes=VMEM_LIMIT),
        cost_estimate=cost(4 * rows * width * hidden, *args, *outs, transcendentals=2 * rows * hidden),
        name="ffn_forward",
    )(*args)


def split_out(grid, length, cols):
    if grid.staged:
        return [like((length // 2, cols), bf16), like((length // 2, cols), bf16)]
    return [like((length, cols), bf16)]


def store_split(grid, place, full_ref, outs, over_inner):
    if not grid.staged:
        outs[0][...] = full_ref[...]
        return
    half = full_ref.shape[0] // 16
    for out, flip in zip(outs, (0, 1)):
        if over_inner:
            for outer in range(4):
                at = pl.multiple_of((2 * outer + (place[1] ^ flip)) * (2 * half), 32)
                out[2 * half * outer : 2 * half * (outer + 1), :] = full_ref[pl.ds(at, 2 * half), :]
        else:
            for block in range(8):
                at = pl.multiple_of((2 * block + (place[2] ^ flip)) * half, 16)
                out[half * block : half * (block + 1), :] = full_ref[pl.ds(at, half), :]


def ffn_backward(grid, norm1, gain1, shift1, part, other, down_add, gain2, shift2, cots, act, slope, up_mat, down_turned):
    rows, width = norm1.shape
    hidden = up_mat.shape[1]
    tile = 256
    chunk = row_tile(rows)
    prompt_len = cots[0].shape[0]
    count = 2 if grid.staged else 1

    def body(place, n1, g1, s1, p, o, db, g2, s2, cp, cc, u, sl, up, dn, *rest):
        outs, scratch = rest[:-6], rest[-6:]
        y_p, y_c, dh2, dx1, sums, up_sum = outs[:6]
        up_outs, down_outs = outs[6 : 6 + count], outs[6 + count :]
        df, x1_t, df_t, acc, full_up, full_down = scratch
        step = pl.program_id(0)

        @pl.when(step == 0)
        def _():
            total = [jnp.zeros((1, width), f32) for _ in range(3)]
            for at in range(0, rows, chunk):
                here = slice(at, at + chunk)
                first = n1[here, :] * g1[...] + s1[...]
                second = first + (p[here, :].astype(f32) + o[here, :].astype(f32)) + db[...]
                normed, inverse = norm_rows(second)
                result = (normed * g2[...] + s2[...]).astype(bf16)
                if at < prompt_len:
                    y_p[here, :] = result
                    cot = cp[here, :].astype(f32)
                else:
                    there = slice(at - prompt_len, at - prompt_len + chunk)
                    y_c[there, :] = result
                    cot = cc[there, :].astype(f32)
                grad = norm_pull(cot, normed, inverse, g2[...])
                dh2[here, :] = grad
                low = grad.astype(bf16)
                df[here, :] = low
                wide = low.astype(f32)
                df_t[:, here] = wide.T.astype(bf16)
                x1_t[:, here] = first.T.astype(bf16)
                total[0] += column_sums(cot * normed)
                total[1] += column_sums(cot)
                total[2] += column_sums(wide)
            sums[...] = jnp.zeros(sums.shape, f32)
            for i in range(3):
                sums[i : i + 1, :] = total[i]
            acc[...] = jnp.zeros_like(acc)

        inner = (product(df[...], dn[...]) * sl[...].astype(f32)).astype(bf16)
        up_sum[...] = jnp.broadcast_to(column_sums(inner.astype(f32)), up_sum.shape)
        full_up[...] = product(x1_t[...], inner).astype(bf16)
        full_down[...] = product(df_t[...], u[...]).astype(bf16)
        acc[...] += contract_cols(inner, up[...])
        store_split(grid, place, full_up, up_outs, True)
        store_split(grid, place, full_down, down_outs, False)

        @pl.when(step == hidden // tile - 1)
        def _():
            dx1[...] = acc[...].astype(bf16)

    def tiled(array):
        return pl.BlockSpec((array.shape[0], tile), lambda j: (0, j))

    fixed = [norm1, gain1, shift1, part, other, down_add, gain2, shift2, *cots]
    moving = [act, slope, up_mat, down_turned]
    outs = [
        like((prompt_len, width), bf16),
        like((rows - prompt_len, width), bf16),
        like((rows, width), f32),
        like((rows, width), bf16),
        like((8, width), f32),
        like((8, hidden), f32),
    ]
    grads = split_out(grid, width, hidden) * 2
    return pl.pallas_call(
        body,
        grid=(hidden // tile,),
        out_shape=outs + grads,
        in_specs=[pl.BlockSpec(memory_space=pltpu.SMEM)]
        + [whole_block(a) for a in fixed]
        + [tiled(a) for a in moving],
        out_specs=[whole_block(a) for a in outs[:5]] + [tiled(a) for a in outs[5:] + grads],
        scratch_shapes=[
            pltpu.VMEM((rows, width), bf16),
            pltpu.VMEM((width, rows), bf16),
            pltpu.VMEM((width, rows), bf16),
            pltpu.VMEM((rows, width), f32),
            pltpu.VMEM((width, tile), bf16),
            pltpu.VMEM((width, tile), bf16),
        ],
        compiler_params=pltpu.CompilerParams(vmem_limit_bytes=VMEM_LIMIT),
        cost_estimate=cost(8 * rows * width * hidden, *fixed, *moving, *outs, *grads),
        name="ffn_backward",
    )(grid.place, *fixed, *moving)


def fold_pair(grid, first, second):
    half = first[0].shape[0] // 8
    outs = []
    for kept, _ in (first, second):
        outs += [like((4 * half, kept.shape[1]), bf16)] * 2

    def body(place, fk, fa, sk, sa, f_keep, f_send, s_keep, s_send):
        for kept, came, keep, send, mine in (
            (fk, fa, f_keep, f_send, place[2]),
            (sk, sa, s_keep, s_send, place[1]),
        ):
            for out, flip in ((send, 1), (keep, 0)):
                at = pl.multiple_of((mine ^ flip) * half, 16)
                here = pl.ds(at, half)
                out[...] = (kept[here, :].astype(f32) + came[here, :].astype(f32)).astype(bf16)

    args = [*first, *second]
    return pl.pallas_call(
        body,
        grid=(4,),
        out_shape=outs,
        in_specs=[pl.BlockSpec(memory_space=pltpu.SMEM)]
        + [pl.BlockSpec((2 * half, a.shape[1]), lambda i: (i, 0)) for a in args],
        out_specs=[pl.BlockSpec((half, a.shape[1]), lambda i: (i, 0)) for a in outs],
        cost_estimate=cost(0, *args, *outs),
        name="fold_pair",
    )(grid.place, *args)


def fold_line(grid, first, second):
    half = first[0].shape[0] // 4
    left, right = first[0].shape[1], second[0].shape[1]
    outs = [like((half, left + right), f32)] + [like((half, left + right), bf16)] * 3

    def body(place, fk, fa, sk, sa, *out_refs):
        for step, out in enumerate(out_refs):
            here = pl.ds(pl.multiple_of((place[0] ^ step) * half, 16), half)
            out[:, :left] = (fk[here, :].astype(f32) + fa[here, :].astype(f32)).astype(out.dtype)
            out[:, left:] = (sk[here, :].astype(f32) + sa[here, :].astype(f32)).astype(out.dtype)

    vmem = pl.BlockSpec(memory_space=pltpu.VMEM)
    args = [*first, *second]
    return pl.pallas_call(
        body,
        out_shape=outs,
        in_specs=[pl.BlockSpec(memory_space=pltpu.SMEM)] + [vmem] * 4,
        out_specs=[vmem] * 4,
        cost_estimate=cost(0, *args, *outs),
        name="fold_line",
    )(grid.place, *args)


def scatter_split(grid, first, second):
    if not grid.staged:
        both = jnp.concatenate([first[0], second[0]], 1)
        both = lax.psum_scatter(both, "fsdp", scatter_dimension=0, tiled=True)
        return lax.psum(both, "ctx")
    came_first = grid.over_inner(first[1])
    came_second = grid.over_ctx(second[1])
    f_keep, f_send, s_keep, s_send = fold_pair(grid, (first[0], came_first), (second[0], came_second))
    came_first = grid.over_ctx(f_send)
    came_second = grid.over_inner(s_send)
    total, *sent = fold_line(grid, (f_keep, came_first), (s_keep, came_second))
    for step in (1, 2, 3):
        total = total + grid.over_outer(sent[step - 1], step).astype(f32)
    total = total.astype(bf16)
    other = grid.over_ctx(total)
    low = jnp.where(grid.row == 0, total, other)
    high = jnp.where(grid.row == 0, other, total)
    return jnp.concatenate([low, high], 0)


def head_lanes(shape, index):
    lane = lax.broadcasted_iota(jnp.int32, shape, 1)
    return (lane < LANES // 2) if index == 0 else (lane >= LANES // 2)


def attention_forward(queries, keys, values, prev_logits, cont_len, prompt_len):
    rows, width = queries.shape
    total = keys.shape[0]
    cont_size = rows - prompt_len
    full_len = total - cont_size
    heads = prev_logits.shape[0]
    chunk = row_tile(prompt_len)

    def body(length, q, k, v, prev, logits, probs_p, probs_c, out):
        def soft(scores):
            weights = jnp.exp(scores - jnp.max(scores, axis=-1, keepdims=True))
            return (weights * (1.0 / jnp.sum(weights, axis=-1, keepdims=True))).astype(bf16)

        column = lax.broadcasted_iota(jnp.int32, (1, total), 1)
        live = column < full_len + length[0, 0]
        for at in range(0, rows, chunk):
            here = slice(at, at + chunk)
            halves = []
            for head in range(2):
                one = jnp.where(head_lanes((chunk, LANES), head), q[here, :], 0)
                if at < prompt_len:
                    probs = soft(contract_cols(one, k[:full_len, :]))
                    probs_p[head, here, :] = probs
                    halves.append(product(probs, v[:full_len, :]))
                else:
                    there = slice(at - prompt_len, at - prompt_len + chunk)
                    raw = prev[head, there, :].astype(f32) + contract_cols(one, k[...])
                    logits[head, there, :] = raw.astype(bf16)
                    probs = soft(jnp.where(live, raw, -1e30))
                    probs_c[head, there, :] = probs
                    halves.append(product(probs, v[...]))
            first = head_lanes((chunk, LANES), 0)
            out[here, :] = jnp.where(first, halves[0], halves[1]).astype(bf16)

    outs = [
        like((heads, cont_size, total), bf16),
        like((heads, prompt_len, full_len), bf16),
        like((heads, cont_size, total), bf16),
        like((rows, width), bf16),
    ]

    def columns(array):
        return pl.BlockSpec((array.shape[0], LANES), lambda i: (0, i))

    def pairs(array):
        return pl.BlockSpec((2,) + array.shape[1:], lambda i: (i, 0, 0))

    args = [queries, keys, values, prev_logits]
    scores = heads * (prompt_len * full_len + cont_size * total)
    return pl.pallas_call(
        body,
        grid=(heads // 2,),
        out_shape=outs,
        in_specs=[pl.BlockSpec(memory_space=pltpu.SMEM)]
        + [columns(a) for a in args[:3]]
        + [pairs(prev_logits)],
        out_specs=[pairs(a) for a in outs[:3]] + [columns(outs[3])],
        compiler_params=pltpu.CompilerParams(vmem_limit_bytes=VMEM_LIMIT),
        cost_estimate=cost(512 * scores, *args, *outs, transcendentals=scores),
        name="attention_forward",
    )(cont_len, *args)


def attention_backward(queries, keys, values, dout, attended, probs_p, probs_c, cots, scale):
    rows, width = queries.shape
    total = keys.shape[0]
    heads, prompt_len, full_len = probs_p.shape
    cont_size = rows - prompt_len
    chunk = row_tile(prompt_len)

    def body(q, k, v, do, o, pp, pc, cot, prev_out, dq, dk, dv, acc_k, acc_v):
        acc_k[...] = jnp.zeros_like(acc_k)
        acc_v[...] = jnp.zeros_like(acc_v)
        for at in range(0, rows, chunk):
            here = slice(at, at + chunk)
            grads = []
            for head in range(2):
                mine = head_lanes((chunk, LANES), head)
                one_q = jnp.where(mine, q[here, :], 0)
                one_do = jnp.where(mine, do[here, :], 0)
                delta = jnp.sum(
                    one_do.astype(f32) * o[here, :].astype(f32), axis=-1, keepdims=True
                )
                if at < prompt_len:
                    span = full_len
                    probs = pp[head, here, :]
                    dprob = contract_cols(one_do, v[:span, :])
                    dscore = (probs.astype(f32) * (dprob - delta)).astype(bf16)
                else:
                    span = total
                    there = slice(at - prompt_len, at - prompt_len + chunk)
                    probs = pc[head, there, :]
                    dprob = contract_cols(one_do, v[...])
                    dscore = (
                        probs.astype(f32) * (dprob - delta) + cot[head, there, :].astype(f32)
                    ).astype(bf16)
                    prev_out[head, there, :] = dscore
                grads.append(product(dscore, k[:span, :]))
                acc_k[:span, :] += contract_rows(dscore, one_q)
                acc_v[:span, :] += contract_rows(probs, one_do)
            first = head_lanes((chunk, LANES), 0)
            dq[here, :] = (jnp.where(first, grads[0], grads[1]) * scale).astype(bf16)
        dk[...] = acc_k[...].astype(bf16)
        dv[...] = acc_v[...].astype(bf16)

    outs = [
        like((heads, cont_size, total), bf16),
        like((rows, width), bf16),
        like((total, width), bf16),
        like((total, width), bf16),
    ]

    def columns(array):
        return pl.BlockSpec((array.shape[0], LANES), lambda i: (0, i))

    def pairs(array):
        return pl.BlockSpec((2,) + array.shape[1:], lambda i: (i, 0, 0))

    args = [queries, keys, values, dout, attended, probs_p, probs_c, cots]
    scores = heads * (prompt_len * full_len + cont_size * total)
    return pl.pallas_call(
        body,
        grid=(heads // 2,),
        out_shape=outs,
        in_specs=[columns(a) for a in args[:5]] + [pairs(a) for a in args[5:]],
        out_specs=[pairs(outs[0])] + [columns(a) for a in outs[1:]],
        scratch_shapes=[pltpu.VMEM((total, LANES), f32), pltpu.VMEM((total, LANES), f32)],
        compiler_params=pltpu.CompilerParams(vmem_limit_bytes=VMEM_LIMIT),
        cost_estimate=cost(1024 * scores, *args, *outs),
        name="attention_backward",
    )(*args)


def first_norm_backward(grad_second, part, other, norm1, inv1, gain1, output_turned):
    rows, width = grad_second.shape
    tile = row_tile(rows)

    def body(d2, p, o, n1, r1, g1, ot, dh1, dout, sums):
        @pl.when(pl.program_id(0) == 0)
        def _():
            sums[...] = jnp.zeros_like(sums)

        upstream = d2[...] + (p[...].astype(f32) + o[...].astype(f32))
        normed = n1[...]
        grad = norm_pull(upstream, normed, r1[:, :1], g1[...])
        dh1[...] = grad
        low = grad.astype(bf16)
        dout[...] = product(low, ot[...]).astype(bf16)
        sums[0:1, :] += column_sums(upstream * normed)
        sums[1:2, :] += column_sums(upstream)
        sums[2:3, :] += column_sums(low.astype(f32))

    def tiled(array):
        return pl.BlockSpec((tile, array.shape[1]), lambda i: (i, 0))

    args = [grad_second, part, other, norm1, inv1, gain1, output_turned]
    outs = [
        like((rows, width), f32),
        like((rows, output_turned.shape[1]), bf16),
        like((8, width), f32),
    ]
    return pl.pallas_call(
        body,
        grid=(rows // tile,),
        out_shape=outs,
        in_specs=[tiled(a) for a in args[:5]] + [whole_block(a) for a in args[5:]],
        out_specs=[tiled(a) for a in outs[:2]] + [whole_block(outs[2])],
        compiler_params=pltpu.CompilerParams(vmem_limit_bytes=VMEM_LIMIT),
        cost_estimate=cost(2 * rows * width * output_turned.shape[1], *args, *outs),
        name="first_norm_backward",
    )(*args)


def weight_grads(grid, shards, grad_first, attended, inputs_t, whole_t, dq, dk, dv, sums1, sums2, up_sum):
    rows, width = grad_first.shape
    part = dq.shape[1]
    hidden = up_sum.shape[1]
    count = 2 if grid.staged else 1
    block = width // shards
    sides = pl.cdiv((6 * width + 2 * part + hidden) // LANES, block)
    extra = sides * LANES

    def body(place, d1, o, xt, wt, q, k, v, s1, s2, us, *rest):
        firsts, seconds = rest[:count], rest[count : 2 * count]
        full_a, full_b = rest[2 * count :]
        turned = d1[...].T.astype(bf16)
        full_a[:, :part] = product(turned, o[...]).astype(bf16)
        full_a[:, part:] = product(xt[...], q[...]).astype(bf16)
        full_b[:, :part] = product(wt[...], k[...]).astype(bf16)
        full_b[:, part : 2 * part] = product(wt[...], v[...]).astype(bf16)
        wide = 2 * part
        lines = [(s1, i) for i in range(3)] + [(s2, i) for i in range(3)]
        pieces = []
        for ref, i in lines:
            pieces += [ref[i : i + 1, at : at + LANES] for at in range(0, width, LANES)]
        for sums in (column_sums(q[...].astype(f32)), column_sums(v[...].astype(f32))):
            pieces += [sums[:, at : at + LANES] for at in range(0, part, LANES)]
        pieces += [us[0:1, at : at + LANES] for at in range(0, hidden, LANES)]
        pieces.append(jnp.zeros((sides * block - len(pieces), LANES), f32))
        table = jnp.concatenate(pieces, 0).astype(bf16)
        for shard in range(shards):
            for side in range(sides):
                low = wide + side * LANES
                full_b[shard * block : (shard + 1) * block, low : low + LANES] = table[
                    side * block : (side + 1) * block
                ]
        store_split(grid, place, full_a, firsts, True)
        store_split(grid, place, full_b, seconds, False)

    args = [grad_first, attended, inputs_t, whole_t, dq, dk, dv, sums1, sums2, up_sum]
    outs = split_out(grid, width, 2 * part) + split_out(grid, width, 2 * part + extra)
    vmem = pl.BlockSpec(memory_space=pltpu.VMEM)
    return pl.pallas_call(
        body,
        out_shape=outs,
        in_specs=[pl.BlockSpec(memory_space=pltpu.SMEM)] + [vmem] * len(args),
        out_specs=[vmem] * len(outs),
        scratch_shapes=[
            pltpu.VMEM((width, 2 * part), bf16),
            pltpu.VMEM((width, 2 * part + extra), bf16),
        ],
        compiler_params=pltpu.CompilerParams(vmem_limit_bytes=VMEM_LIMIT),
        cost_estimate=cost(4 * width * part * (rows + whole_t.shape[1]), *args, *outs),
        name="weight_grads",
    )(grid.place, *args)


def unpack_small(grid, packed, heads, head_size, up_rows):
    width = packed.shape[0]
    shards = grid.fsdp
    block, per_head, per_up = width // shards, head_size // shards, LANES // shards

    def body(packed_ref, lines, query_out, value_out, up_out):
        source = lax.broadcasted_iota(jnp.int32, (LANES, width), 0)
        target = lax.broadcasted_iota(jnp.int32, (LANES, width), 1)
        whole = jnp.zeros((32, width), f32)
        by_head = jnp.zeros((32, LANES), f32)
        by_up = jnp.zeros((32, LANES), f32)
        near, far = source[:, :LANES], target[:, :LANES]
        for shard in range(shards):
            piece = packed_ref[shard * block : shard * block + 32, :]
            put = (target - source == shard * block) & (source < block)
            whole += product(piece, put.astype(bf16))
            place = shard * per_head
            shift = far - near
            put = ((shift == place) | (shift == place + head_size)) & (near < per_head)
            by_head += product(piece, put.astype(bf16))
            put = (shift == shard * per_up) & (near < per_up)
            by_up += product(piece, put.astype(bf16))
        lines[...] = whole[:8, :]
        low = lax.broadcasted_iota(jnp.int32, (1, LANES), 1) < head_size
        for pair in range(heads // 2):
            at = slice(pair * LANES, (pair + 1) * LANES)
            for out, base in ((query_out, 6), (value_out, 6 + heads)):
                row = base + 2 * pair
                out[:, at] = jnp.where(low, by_head[row : row + 1, :], by_head[row + 1 : row + 2, :])
        for i in range(up_rows):
            row = 6 + 2 * heads + i
            up_out[:, i * LANES : (i + 1) * LANES] = by_up[row : row + 1, :]

    outs = [
        like((8, width), f32),
        like((1, heads * head_size), f32),
        like((1, heads * head_size), f32),
        like((1, up_rows * LANES), f32),
    ]
    vmem = pl.BlockSpec(memory_space=pltpu.VMEM)
    return pl.pallas_call(
        body,
        out_shape=outs,
        in_specs=[vmem],
        out_specs=[vmem] * 4,
        cost_estimate=cost(0, packed, *outs),
        name="unpack_small",
    )(packed)


def per_device(
    sizes,
    prompt,
    continuations,
    prev_logits,
    cont_len,
    query_weight,
    query_bias,
    key_weight,
    value_weight,
    value_bias,
    output_weight,
    output_bias,
    first_gain,
    first_shift,
    up_weight,
    up_bias,
    down_weight,
    down_bias,
    second_gain,
    second_shift,
    cot_prompt,
    cot_conts,
    cot_logits,
):
    grid = Grid(sizes)
    rows = query_weight.shape[0]
    width = query_weight.shape[1]
    hidden = up_weight.shape[1]
    prompt_len = prompt.shape[1]
    cont_size = continuations.shape[2]
    head_count = query_bias.shape[0]
    head_size = width // head_count
    scale = 1.0 / math.sqrt(head_size)

    lines = [v[None] for v in (output_bias, first_gain, first_shift, down_bias, second_gain, second_shift)]
    lines += [query_bias, value_bias, up_bias]
    small = jnp.concatenate([jnp.pad(v, ((0, 0), (0, LANES - v.shape[1]))) for v in lines], 0)
    small = jnp.pad(small, ((0, rows - small.shape[0]), (0, 0)))
    early, late = gather_rows(
        grid,
        [query_weight, key_weight, value_weight, small],
        [output_weight.T, up_weight, down_weight.T],
    )
    query_mat, key_mat, value_mat, small = early
    output_turned, up_mat, down_turned = late
    vectors, query_add, value_add, up_line = unpack_small(
        grid, small, head_count, head_size, up_bias.shape[0]
    )
    output_line, gain1, shift1, down_line, gain2, shift2 = [vectors[i : i + 1] for i in range(6)]

    mine = prompt[0]
    inputs = jnp.concatenate([mine, continuations[0, 0]], 0)
    if sizes[1] == 2:
        theirs = grid.over_ctx(mine)
        whole = jnp.concatenate(
            [
                jnp.where(grid.row == 0, mine, theirs),
                jnp.where(grid.row == 0, theirs, mine),
                continuations[0, 0],
            ],
            0,
        )
    else:
        whole = jnp.concatenate(
            [lax.all_gather(mine, "ctx", axis=0, tiled=True), continuations[0, 0]], 0
        )
    full_len = whole.shape[0] - cont_size
    whole_t, inputs_t = whole.T, inputs.T

    queries = ((product(inputs, query_mat) + query_add) * scale).astype(bf16)
    keys = product(whole, key_mat).astype(bf16)
    values = (product(whole, value_mat) + value_add).astype(bf16)
    new_logits, probs_p, probs_c, attended = attention_forward(
        queries, keys, values, prev_logits[0, 0], cont_len, prompt_len
    )
    part = contract_cols(attended, output_turned).astype(bf16)
    first_norm, first_inv, activated, slope, part2 = ffn_forward(
        inputs, part, grid.over_tp(part), output_line, gain1, shift1, up_mat, up_line, down_turned
    )
    results = ffn_backward(
        grid,
        first_norm,
        gain1,
        shift1,
        part2,
        grid.over_tp(part2),
        down_line,
        gain2,
        shift2,
        (cot_prompt[0], cot_conts[0, 0]),
        activated,
        slope,
        up_mat,
        down_turned,
    )
    result_prompt, result_cont, grad_second, part3, sums2, up_sum = results[:6]
    splits = results[6:]
    half = len(splits) // 2
    ffn_shard = scatter_split(grid, splits[:half], splits[half:]).astype(f32)
    grad_first, dout, sums1 = first_norm_backward(
        grad_second, part3, grid.over_tp(part3), first_norm, first_inv, gain1, output_turned
    )
    grad_prev, dq, dk, dv = attention_backward(
        queries, keys, values, dout, attended, probs_p, probs_c, cot_logits[0, 0], scale
    )
    splits = weight_grads(
        grid, sizes[0], grad_first, attended, inputs_t, whole_t, dq, dk, dv, sums1, sums2, up_sum
    )
    half = len(splits) // 2
    late_shard = scatter_split(grid, splits[:half], splits[half:]).astype(f32)

    from_query = contract_cols(dq, query_mat)
    from_keyvalue = contract_cols(dk, key_mat) + contract_cols(dv, value_mat)
    shared, own_cont = from_keyvalue[:full_len], from_keyvalue[full_len:]
    if sizes[1] == 2 and sizes[2] == 2:
        shared = shared.reshape(2, prompt_len, -1)
        abroad = pick(shared, 1 - grid.row, 0).astype(bf16).reshape(2, prompt_len // 2, -1)
        abroad_sum = add_low(
            pick(abroad, grid.core, 0), grid.over_tp(pick(abroad, 1 - grid.core, 0))
        )
        arrived = grid.over_ctx(abroad_sum).astype(f32)
        own = (pick(shared, grid.row, 0) + from_query[:prompt_len]).reshape(2, prompt_len // 2, -1)
        at = lax.broadcasted_iota(jnp.int32, (2, 1, 1), 0)
        own = own + jnp.where(at == grid.core, arrived[None], 0.0)
        own = own.reshape(prompt_len, -1)
    else:
        own = lax.psum_scatter(
            shared.astype(bf16), "ctx", scatter_dimension=0, tiled=True
        ).astype(f32)
        own = own + from_query[:prompt_len]
    partial = jnp.concatenate([own, own_cont + from_query[prompt_len:]], 0)
    input_grad = grad_first + grid.tp_sum(partial)

    table = late_shard[:, 4 * width :]
    table = jnp.concatenate([table[:, at : at + LANES] for at in range(0, table.shape[1], LANES)], 0)
    model = whole.shape[1]
    place = lax.axis_index("fsdp")
    at = 6 * (model // LANES)
    long_lines = table[:at].reshape(6, model)
    long_lines = lax.dynamic_slice_in_dim(long_lines, place * rows, rows, 1)
    shorts = []
    for bias in (query_bias, value_bias, up_bias):
        height, cols = bias.shape
        span = height * cols * sizes[0] // LANES
        block = table[at : at + span].reshape(height, -1)
        shorts.append(lax.dynamic_slice_in_dim(block, place * cols, cols, 1))
        at += span
    gain_one_grad, shift_one_grad, output_add_grad = long_lines[0], long_lines[1], long_lines[2]
    gain_two_grad, shift_two_grad, down_add_grad = long_lines[3], long_lines[4], long_lines[5]
    return (
        result_prompt[None],
        result_cont[None, None],
        new_logits[None, None],
        input_grad[:prompt_len][None],
        input_grad[prompt_len:][None, None],
        grad_prev[None, None],
        late_shard[:, width : 2 * width],
        shorts[0],
        late_shard[:, 2 * width : 3 * width],
        late_shard[:, 3 * width : 4 * width],
        shorts[1],
        late_shard[:, :width].T,
        output_add_grad,
        gain_one_grad,
        shift_one_grad,
        ffn_shard[:, :hidden],
        shorts[2],
        ffn_shard[:, hidden:].T,
        down_add_grad,
        gain_two_grad,
        shift_two_grad,
    )


def solution(mesh):
    sizes = tuple(mesh.shape[name] for name in ("fsdp", "ctx", "tp"))

    def step(*arrays):
        return per_device(sizes, *arrays)

    return jax.shard_map(
        step,
        mesh=mesh,
        in_specs=(
            P("fsdp", "ctx", None),
            P("fsdp", "ctx", None, None),
            P("fsdp", "ctx", "tp", None, None),
            P("fsdp", "ctx"),
            P("fsdp", "tp"),
            P("tp", "fsdp"),
            P("fsdp", "tp"),
            P("fsdp", "tp"),
            P("tp", "fsdp"),
            P("tp", "fsdp"),
            P("fsdp"),
            P("fsdp"),
            P("fsdp"),
            P("fsdp", "tp"),
            P("tp", "fsdp"),
            P("tp", "fsdp"),
            P("fsdp"),
            P("fsdp"),
            P("fsdp"),
            P("fsdp", "ctx", None),
            P("fsdp", "ctx", None, None),
            P("fsdp", "ctx", "tp", None, None),
        ),
        out_specs=(
            P("fsdp", "ctx", None),
            P("fsdp", "ctx", None, None),
            P("fsdp", "ctx", "tp", None, None),
            P("fsdp", "ctx", None),
            P("fsdp", "ctx", None, None),
            P("fsdp", "ctx", "tp", None, None),
            P("fsdp", "tp"),
            P("tp", "fsdp"),
            P("fsdp", "tp"),
            P("fsdp", "tp"),
            P("tp", "fsdp"),
            P("tp", "fsdp"),
            P("fsdp"),
            P("fsdp"),
            P("fsdp"),
            P("fsdp", "tp"),
            P("tp", "fsdp"),
            P("tp", "fsdp"),
            P("fsdp"),
            P("fsdp"),
            P("fsdp"),
        ),
        check_vma=False,
    )
```

time: 1150 us -> 311 us (0.27)
  blocking collectives: 430 us -> 0 us
  waiting for transfers between devices: 475 us -> 105 us
  matrix products: 128 us -> 17.5 us
  Pallas kernels: 0 us -> 102 us
  other arithmetic: 60.9 us -> 19.8 us
  starting transfers between devices: 1.37 us -> 36.6 us
  between operations: 19.9 us -> 1.71 us
    all_gather x13 -> x0, blocking collectives: 352 us -> none  [the longest x1 32.7 us: per_device(): lax.all_gather(query_held, 'fsdp', axis=0, tiled=True)]
    reduce_scatter x8 -> x0, waiting for transfers between devices: 289 us -> none  [the longest x1 71.5 us: per_device(): lax.psum_scatter(up_mat_grad.astype(jnp.bfloat16), 'fsdp', scatter_dimens...]
    all_gather x4 -> x0, waiting for transfers between devices: 108 us -> none  [the longest x1 47.2 us: per_device(): lax.all_gather(down_held, 'fsdp', axis=1, tiled=True)]
    ppermute x0 -> x37, waiting for transfers between devices: none -> 105 us  [the longest x12 49.5 us: over_outer(): return lax.ppermute(array, 'fsdp', [(i, i ^ 2 * step) for i in range(8)])]
    pallas_call x0 -> x13, Pallas kernels: none -> 102 us  [the longest x1 21.5 us: ffn_backward(): pl.pallas_call(body, grid=(hidden // tile,), out_shape=outs + grads, in_s...]
    dot_general x23 -> x3, matrix products: 94.8 us -> 8.39 us  [product(): return jnp.dot(left_mat, right_mat, preferred_element_type=f32)]
    psum x5 -> x0, waiting for transfers between devices: 75 us -> none  [the longest x1 36.4 us: per_device(): lax.psum(shards[0].astype(jnp.bfloat16), 'ctx').astype(jnp.float32)]
    unnamed x2 -> x0, blocking collectives: 69.6 us -> none
  transfers between devices with their start and end apart: 18 -> 37, of which waited for: 11 -> 18; matrix products, arithmetic and copies ran while one was open for 11% -> 15% of each run, Pallas kernels for 0% -> 21%
where the time goes in v1:
time: 311 us; the launch traced here: 309 us
  waiting for transfers between devices  105 us (34%)
  Pallas kernels  102 us (33%)
  starting transfers between devices  36.6 us (12%)
  local copies, waits for them, and re-layouts  26.8 us (9%)
  other arithmetic  19.8 us (6%)
  matrix products  17.5 us (6%)
    ppermute x12, waiting for transfers between devices, over_outer(): return lax.ppermute(array, 'fsdp', [(i, i ^ 2 * step) for i in range(8)])  49.5 us
    ppermute x8, waiting for transfers between devices, over_inner(): return lax.ppermute(array, 'fsdp', [(i, i ^ 1) for i in range(8)])  47.4 us
    pallas_call x1, Pallas kernels, ffn_backward(): pl.pallas_call(body, grid=(hidden // tile,), out_shape=outs + grads, in_s...  21.5 us
    pallas_call x1, Pallas kernels, attention_backward(): pl.pallas_call(body, grid=(heads // 2,), out_shape=outs, in_specs=[column...  16.1 us
    pallas_call x1, Pallas kernels, attention_forward(): pl.pallas_call(body, grid=(heads // 2,), out_shape=outs, in_specs=[pl.Blo...  15.5 us
    ppermute x12, starting transfers between devices, over_outer(): return lax.ppermute(array, 'fsdp', [(i, i ^ 2 * step) for i in range(8)])  14.9 us
    ppermute x12, starting transfers between devices, over_ctx(): return lax.ppermute(array, 'ctx', [(0, 1), (1, 0)])  12.6 us
    pallas_call x1, Pallas kernels, ffn_forward(): pl.pallas_call(body, grid=(rows // tile,), out_shape=outs, in_specs=[tile...  9.75 us
  transfers between devices with their start and end apart: 37, of which 18 were waited for; matrix products, arithmetic and copies ran while one was open for 15% of the time, Pallas kernels for 21%

profile of v1, /device:TPU:8, one launch (start us, length us, event | category | flops | bytes accessed | tf_op | source)
XLA Modules:
  0.0 308.9 jit_solution(5430846283026698704)
XLA Ops:
  8.0 3.0 collective-permute-start.1
  13.4 6.4 %collective-permute-done.1 = bf16[48,1280]{1,0:T(8,128)(2,1)S(1)} collective-permute-done((bf16[48,1280]{1,0:T(8,128)(2,1)S(1)}, bf16[48,1280]{1,0:T(8,128)(2,1)S(1)}, u32[]{:S(2)}, u32[]{:S(2)}) %collective-permute-start.1) | collective-permute-done | bytes 122912 | tf_op jit(solution)/shard_map/ppermute | solution.py:46
  19.8 2.4 collective-permute-done.2
  22.3 1.6 collective-permute-start.3
  25.5 2.9 collective-permute-start.8
  28.9 5.1 %collective-permute-done.3.across_ref = bf16[4,48,1280]{2,1,0:T(8,128)(2,1)S(1)} collective-permute-done((bf16[4,48,1280]{2,1,0:T(8,128)(2,1)S(1)}, bf16[4,48,1280]{2,1,0:T(8,128)(2,1)S(1)}, u32[]{:S(2)}, u32[]{:S(2)}) %collective-permute-start.3) | collective-permute-done | bytes 491552 | tf_op jit(solution)/shard_map/ppermute | solution.py:43
  39.5 11.1 %collective-permute-done.8 = bf16[48,3456]{1,0:T(8,128)(2,1)S(1)} collective-permute-done((bf16[48,3456]{1,0:T(8,128)(2,1)S(1)}, bf16[48,3456]{1,0:T(8,128)(2,1)S(1)}, u32[]{:S(2)}, u32[]{:S(2)}) %collective-permute-start.8) | collective-permute-done | bytes 331808 | tf_op jit(solution)/shard_map/ppermute | solution.py:46
  50.6 5.1 %collective-permute-done.9 = bf16[48,3456]{1,0:T(8,128)(2,1)} collective-permute-done((bf16[48,3456]{1,0:T(8,128)(2,1)S(1)}, bf16[48,3456]{1,0:T(8,128)(2,1)}, u32[]{:S(2)}, u32[]{:S(2)}) %collective-permute-start.9) | collective-permute-done | bytes 331808 | tf_op jit(solution)/shard_map/ppermute | solution.py:46
  59.6 2.1 broadcast_select_fusion.1
  61.8 3.3 %assemble.2 = (bf16[768,384]{1,0:T(8,128)(2,1)}, bf16[768,384]{1,0:T(8,128)(2,1)}, bf16[768,384]{1,0:T(8,128)(2,1)}, bf16[768,128]{1,0:T(8,128)(2,1)}) custom-call(s32[3]{0:T(128)} %pad_add_fusion.place_ref.place, bf16[4,48,1280]{2,1,0:T(8,128)(2,1)} %copy-done.12, bf16[4,48,1280]{2,1,0:T(8,128)(2,1)} %copy-done.16, bf16[4,48,1280]{2,1,0:T(8,128)(2,1)} %copy-done.17, ...), custom_call_target="tpu_custom_call" | custom-call | bytes 3932160 | tf_op jit(solution)/shard_map/assemble/pallas_call | solution.py:80
  65.0 1.8 unpack_small.1
  67.5 3.5 %convolution_convert_fusion.k = bf16[1280,384]{1,0:T(8,128)(2,1)} fusion(bf16[768,384]{1,0:T(8,128)(2,1)} %get-tuple-element.96, bf16[256,768]{0,1:T(8,128)(2,1)S(1)} %bitcast.84, bf16[512,768]{0,1:T(8,128)(2,1)} %get-tuple-element.154, bf16[512,768]{0,1:T(8,128)(2,1)S(1)} %get-tuple-element.153), kind=kOutput, calls=%fused_computation.3 | convolution fusion | flops 761364480 | bytes 3538944 | tf_op jit(solution)/shard_map/dot_general | solution.py:17
  71.0 14.3 %collective-permute-done.11.across_ref = bf16[4,48,3456]{2,1,0:T(8,128)(2,1)} collective-permute-done((bf16[4,48,3456]{2,1,0:T(8,128)(2,1)S(1)}, bf16[4,48,3456]{2,1,0:T(8,128)(2,1)}, u32[]{:S(2)}, u32[]{:S(2)}) %collective-permute-start.11) | collective-permute-done | bytes 1327136 | tf_op jit(solution)/shard_map/ppermute | solution.py:43
  85.3 2.0 slice.135
  87.8 2.0 slice.136
  90.3 1.7 fusion.4.q
  92.0 3.3 %fusion.v = bf16[1280,384]{1,0:T(8,128)(2,1)} fusion(bf16[768,384]{1,0:T(8,128)(2,1)} %get-tuple-element.97, f32[384]{0:T(512)S(1)} %reduce.1, bf16[256,768]{0,1:T(8,128)(2,1)S(1)} %bitcast.86, bf16[512,768]{0,1:T(8,128)(2,1)S(1)} %copy-done.9, bf16[512,768]{0,1:T(8,128)(2,1)S(1)} %get-tuple-element.153), kind=kOutput, calls=%fused_computation.2 | convolution fusion | flops 761856000 | bytes 3540480 | tf_op jit(solution)/shard_map/dot_general | solution.py:17
  95.2 15.5 %attention_forward.1 = (bf16[6,256,1280]{2,1,0:T(8,128)(2,1)}, bf16[6,512,1024]{2,1,0:T(8,128)(2,1)}, bf16[6,256,1280]{2,1,0:T(8,128)(2,1)}, bf16[768,384]{1,0:T(8,128)(2,1)}) custom-call(s32[1,1]{1,0:T(1,128)S(6)} %copy.46.length, bf16[768,384]{1,0:T(8,128)(2,1)} %fusion.4.q, bf16[1280,384]{1,0:T(8,128)(2,1)} %convolution_convert_fusion.k, ...), custom_call_target="tpu_custom_call" | custom-call | flops 2617245696 | bytes 21233664 | tf_op jit(solution)/shard_map/attention_forward/pallas_call | solution.py:461
  110.8 5.4 %assemble.3 = (bf16[768,384]{1,0:T(8,128)(2,1)}, bf16[768,1536]{1,0:T(8,128)(2,1)}, bf16[768,1536]{1,0:T(8,128)(2,1)}) custom-call(s32[3]{0:T(128)} %pad_add_fusion.place_ref.place, bf16[4,48,3456]{2,1,0:T(8,128)(2,1)} %copy-done.4, bf16[4,48,3456]{2,1,0:T(8,128)(2,1)} %collective-permute-done.11.across_ref, ...), custom_call_target="tpu_custom_call" | custom-call | bytes 10616832 | tf_op jit(solution)/shard_map/assemble/pallas_call | solution.py:80
  116.2 1.9 convolution_convert_fusion.1.p
  121.5 9.7 %ffn_forward.1 = (f32[768,768]{1,0:T(8,128)}, f32[768,128]{1,0:T(8,128)}, bf16[768,1536]{1,0:T(8,128)(2,1)}, bf16[768,1536]{1,0:T(8,128)(2,1)}, bf16[768,768]{1,0:T(8,128)(2,1)}) custom-call(bf16[768,768]{1,0:T(8,128)(2,1)} %copy.45.x, bf16[768,768]{1,0:T(8,128)(2,1)} %copy-done.15, bf16[768,768]{1,0:T(8,128)(2,1)} %collective-permute-done.15.o, ...), custom_call_target="tpu_custom_call" | custom-call | flops 3623878656 | bytes 16923648 | tf_op jit(solution)/shard_map/ffn_forward/pallas_call | solution.py:207
  131.7 2.7 collective-permute-done.16.o
  135.4 21.5 %ffn_backward.1 = (bf16[512,768]{1,0:T(8,128)(2,1)}, bf16[256,768]{1,0:T(8,128)(2,1)}, f32[768,768]{1,0:T(8,128)}, bf16[768,768]{1,0:T(8,128)(2,1)}, f32[8,768]{...) custom-call(s32[3]{0:T(128)} %pad_add_fusion.place_ref.place, ...), custom_call_target="tpu_custom_call" | custom-call | flops 7247757312 | bytes 24861696 | tf_op jit(solution)/shard_map/ffn_backward/pallas_call | solution.py:313
  156.9 1.6 collective-permute-start.29
  160.0 25.4 %collective-permute-done.29.fa = bf16[384,1536]{1,0:T(8,128)(2,1)S(1)} collective-permute-done((bf16[384,1536]{1,0:T(8,128)(2,1)}, bf16[384,1536]{1,0:T(8,128)(2,1)S(1)}, u32[]{:S(2)}, u32[]{:S(2)}) %collective-permute-start.29) | collective-permute-done | bytes 1179680 | tf_op jit(solution)/shard_map/ppermute | solution.py:43
  186.7 4.3 %fold_pair.3 = (bf16[192,1536]{1,0:T(8,128)(2,1)}, bf16[192,1536]{1,0:T(8,128)(2,1)}, bf16[192,1536]{1,0:T(8,128)(2,1)}, bf16[192,1536]{1,0:T(8,128)(2,1)}) custom-call(s32[3]{0:T(128)} %pad_add_fusion.place_ref.place, bf16[384,1536]{1,0:T(8,128)(2,1)} %get-tuple-element.141.fk, bf16[384,1536]{1,0:T(8,128)(2,1)} %copy-done.14, ...), custom_call_target="tpu_custom_call" | custom-call | bytes 7077888 | tf_op jit(solution)/shard_map/fold_pair/pallas_call | solution.py:352
  191.1 1.8 collective-permute-start.31
  194.8 6.7 %first_norm_backward.1 = (f32[768,768]{1,0:T(8,128)}, bf16[768,384]{1,0:T(8,128)(2,1)}, f32[8,768]{1,0:T(8,128)}) custom-call(f32[768,768]{1,0:T(8,128)} %get-tuple-element.115.d2, bf16[768,768]{1,0:T(8,128)(2,1)} %get-tuple-element.116.p, bf16[768,768]{1,0:T(8,128)(2,1)} %copy-done.13, f32[768,768]{1,0:T(8,128)} %get-tuple-element.108.n1, ...), custom_call_target="tpu_custom_call" | custom-call | flops 452984832 | bytes 11037696 | tf_op jit(solution)/shard_map/first_norm_backward/pallas_call | solution.py:573
  201.5 16.1 %attention_backward.1 = (bf16[6,256,1280]{2,1,0:T(8,128)(2,1)}, bf16[768,384]{1,0:T(8,128)(2,1)}, bf16[1280,384]{1,0:T(8,128)(2,1)}, bf16[1280,384]{1,0:T(8,128)(2,1)}) custom-call(bf16[768,384]{1,0:T(8,128)(2,1)} %fusion.4.q, bf16[1280,384]{1,0:T(8,128)(2,1)} %convolution_convert_fusion.k, bf16[1280,384]{1,0:T(8,128)(2,1)} %fusion.v, ...), custom_call_target="tpu_custom_call" | custom-call | flops 5234491392 | bytes 24379392 | tf_op jit(solution)/shard_map/attention_backward/pallas_call | solution.py:532
  217.6 2.5 fusion.17
  221.6 1.7 copy-done
  226.5 8.4 %weight_grads.1 = (bf16[384,768]{1,0:T(8,128)(2,1)}, bf16[384,768]{1,0:T(8,128)(2,1)}, bf16[384,896]{1,0:T(8,128)(2,1)}, bf16[384,896]{1,0:T(8,128)(2,1)}) custom-call(s32[3]{0:T(128)} %pad_add_fusion.place_ref.place, f32[768,768]{1,0:T(8,128)} %get-tuple-element.118.d1, bf16[768,384]{1,0:T(8,128)(2,1)} %get-tuple-element.99.o, ...), custom_call_target="tpu_custom_call" | custom-call | flops 2415919104 | bytes 11304960 | tf_op jit(solution)/shard_map/weight_grads/pallas_call | solution.py:624
  236.3 2.9 fold_line.3
  240.4 2.9 collective-permute-start.34
  243.3 3.5 %fusion.18 = f32[768,768]{1,0:T(8,128)} fusion(bf16[768,384]{1,0:T(8,128)(2,1)} %get-tuple-element.124.q, bf16[768,384]{1,0:T(8,128)(2,1)} %get-tuple-element.93), kind=kOutput, calls=%fused_computation.72 | convolution fusion | flops 452984832 | bytes 3538944 | tf_op jit(solution)/shard_map/dot_general | solution.py:27
  246.8 1.8 fusion.6
  248.6 2.6 collective-permute-done.21.fa
  253.0 3.8 %fold_pair.2 = (bf16[192,768]{1,0:T(8,128)(2,1)}, bf16[192,768]{1,0:T(8,128)(2,1)}, bf16[192,896]{1,0:T(8,128)(2,1)}, bf16[192,896]{1,0:T(8,128)(2,1)}) custom-call(s32[3]{0:T(128)} %pad_add_fusion.place_ref.place, bf16[384,768]{1,0:T(8,128)(2,1)} %get-tuple-element.129.fk, bf16[384,768]{1,0:T(8,128)(2,1)} %collective-permute-done.21.fa, ...), custom_call_target="tpu_custom_call" | custom-call | bytes 3833856 | tf_op jit(solution)/shard_map/fold_pair/pallas_call | solution.py:352
  258.3 5.3 %collective-permute-done.34 = bf16[48,3072]{1,0:T(8,128)(2,1)} collective-permute-done((bf16[48,3072]{1,0:T(8,128)(2,1)}, bf16[48,3072]{1,0:T(8,128)(2,1)}, u32[]{:S(2)}, u32[]{:S(2)}) %collective-permute-start.34) | collective-permute-done | bytes 294944 | tf_op jit(solution)/shard_map/ppermute | solution.py:46
  263.6 5.1 %collective-permute-done.35 = bf16[48,3072]{1,0:T(8,128)(2,1)} collective-permute-done((bf16[48,3072]{1,0:T(8,128)(2,1)}, bf16[48,3072]{1,0:T(8,128)(2,1)}, u32[]{:S(2)}, u32[]{:S(2)}) %collective-permute-start.35) | collective-permute-done | bytes 294944 | tf_op jit(solution)/shard_map/ppermute | solution.py:46
  268.7 2.1 add_convert_fusion
  270.8 1.6 collective-permute-start.36
  277.3 2.2 fold_line.2
  279.5 3.8 %collective-permute-start.26 = (bf16[48,1664]{1,0:T(8,128)(2,1)}, bf16[48,1664]{1,0:T(8,128)(2,1)S(1)}, u32[]{:S(2)}, u32[]{:S(2)}) collective-permute-start(bf16[48,1664]{1,0:T(8,128)(2,1)} %get-tuple-element.139), channel_id=1, source_target_pairs={{0,16},{4,20},{8,24},{12,28},{16,0},{20,4},{24,8},{28,12},{1,17},{... | collective-permute-start | bytes 479240 | tf_op jit(solution)/shard_map/ppermute | solution.py:46
  284.5 2.9 collective-permute-done.25
  287.4 7.6 %collective-permute-done.26 = bf16[48,1664]{1,0:T(8,128)(2,1)S(1)} collective-permute-done((bf16[48,1664]{1,0:T(8,128)(2,1)}, bf16[48,1664]{1,0:T(8,128)(2,1)S(1)}, u32[]{:S(2)}, u32[]{:S(2)}) %collective-permute-start.26) | collective-permute-done | bytes 159776 | tf_op jit(solution)/shard_map/ppermute | solution.py:46
  295.0 2.7 collective-permute-done.27
  299.6 3.6 %collective-permute-done.28 = bf16[48,1664]{1,0:T(8,128)(2,1)S(1)} collective-permute-done((bf16[48,1664]{1,0:T(8,128)(2,1)S(1)}, bf16[48,1664]{1,0:T(8,128)(2,1)S(1)}, u32[]{:S(2)}, u32[]{:S(2)}) %collective-permute-start.28) | collective-permute-done | bytes 159776 | tf_op jit(solution)/shard_map/ppermute | solution.py:49
  (167 shorter events, 56.2 us)
Async XLA Ops:
  0.7 38.0 %copy-start.19 = (bf16[1,512,768]{2,1,0:T(8,128)(2,1)S(1)}, bf16[1,512,768]{2,1,0:T(8,128)(2,1)}, u32[]{:S(2)}) copy-start(bf16[1,512,768]{2,1,0:T(8,128)(2,1)} %param.22) | copy-start | bytes 2359300
  8.0 5.5 %collective-permute-start = (bf16[48,1280]{1,0:T(8,128)(2,1)S(1)}, bf16[48,1280]{1,0:T(8,128)(2,1)S(1)}, u32[]{:S(2)}, u32[]{:S(2)}) collective-permute-start(bf16[48,1280]{1,0:T(8,128)(2,1)S(1)} %fusion.10), channel_id=1, source_target_pairs={{0,8},{4,12},{8,0},{12,4},{16,24},{20,28},{24,16},{28,20},{1,9},{5... | collective-permute-start | bytes 368648 | tf_op jit(solution)/shard_map/ppermute | solution.py:46
  8.0 11.8 %collective-permute-start.1 = (bf16[48,1280]{1,0:T(8,128)(2,1)S(1)}, bf16[48,1280]{1,0:T(8,128)(2,1)S(1)}, u32[]{:S(2)}, u32[]{:S(2)}) collective-permute-start(bf16[48,1280]{1,0:T(8,128)(2,1)S(1)} %fusion.10), channel_id=1, source_target_pairs={{0,16},{4,20},{8,24},{12,28},{16,0},{20,4},{24,8},{28,12},{1,17},{... | collective-permute-start | bytes 368648 | tf_op jit(solution)/shard_map/ppermute | solution.py:46
  11.1 11.2 %collective-permute-start.2 = (bf16[48,1280]{1,0:T(8,128)(2,1)S(1)}, bf16[48,1280]{1,0:T(8,128)(2,1)S(1)}, u32[]{:S(2)}, u32[]{:S(2)}) collective-permute-start(bf16[48,1280]{1,0:T(8,128)(2,1)S(1)} %fusion.10), channel_id=1, source_target_pairs={{0,24},{4,28},{8,16},{12,20},{16,8},{20,12},{24,0},{28,4},{1,25},{... | collective-permute-start | bytes 368648 | tf_op jit(solution)/shard_map/ppermute | solution.py:46
  22.3 14.7 %copy-start.12 = (bf16[4,48,1280]{2,1,0:T(8,128)(2,1)}, bf16[4,48,1280]{2,1,0:T(8,128)(2,1)S(1)}, u32[]{:S(2)}) copy-start(bf16[4,48,1280]{2,1,0:T(8,128)(2,1)S(1)} %pad_maximum_fusion.4.own_ref) | copy-start | bytes 1474564
  22.3 11.7 %collective-permute-start.3 = (bf16[4,48,1280]{2,1,0:T(8,128)(2,1)S(1)}, bf16[4,48,1280]{2,1,0:T(8,128)(2,1)S(1)}, u32[]{:S(2)}, u32[]{:S(2)}) collective-permute-start(bf16[4,48,1280]{2,1,0:T(8,128)(2,1)S(1)} %pad_maximum_fusion.4.own_ref), channel_id=1, source_target_pairs={{0,4},{4,0},{8,12},{12,8},{16,20},{20,16},{24,28},{28,24},{1,5},{5... | collective-permute-start | bytes 1474568 | tf_op jit(solution)/shard_map/ppermute | solution.py:43
  23.9 12.4 %collective-permute-start.4 = (bf16[4,48,1280]{2,1,0:T(8,128)(2,1)S(1)}, bf16[4,48,1280]{2,1,0:T(8,128)(2,1)S(1)}, u32[]{:S(2)}, u32[]{:S(2)}) collective-permute-start(bf16[4,48,1280]{2,1,0:T(8,128)(2,1)S(1)} %pad_maximum_fusion.4.own_ref), channel_id=1, source_target_pairs={{0,2},{2,0},{1,3},{3,1},{4,6},{6,4},{5,7},{7,5},{8,10},{10,8},{9,1... | collective-permute-start | bytes 1474568 | tf_op jit(solution)/shard_map/ppermute | solution.py:49
  25.4 13.5 %collective-permute-start.7 = (bf16[48,3456]{1,0:T(8,128)(2,1)S(1)}, bf16[48,3456]{1,0:T(8,128)(2,1)S(1)}, u32[]{:S(2)}, u32[]{:S(2)}) collective-permute-start(bf16[48,3456]{1,0:T(8,128)(2,1)S(1)} %fusion.8), channel_id=1, source_target_pairs={{0,8},{4,12},{8,0},{12,4},{16,24},{20,28},{24,16},{28,20},{1,9},{5... | collective-permute-start | bytes 995336 | tf_op jit(solution)/shard_map/ppermute | solution.py:46
  25.5 25.0 %collective-permute-start.8 = (bf16[48,3456]{1,0:T(8,128)(2,1)S(1)}, bf16[48,3456]{1,0:T(8,128)(2,1)S(1)}, u32[]{:S(2)}, u32[]{:S(2)}) collective-permute-start(bf16[48,3456]{1,0:T(8,128)(2,1)S(1)} %fusion.8), channel_id=1, source_target_pairs={{0,16},{4,20},{8,24},{12,28},{16,0},{20,4},{24,8},{28,12},{1,17},{... | collective-permute-start | bytes 995336 | tf_op jit(solution)/shard_map/ppermute | solution.py:46
  28.4 27.3 %collective-permute-start.9 = (bf16[48,3456]{1,0:T(8,128)(2,1)S(1)}, bf16[48,3456]{1,0:T(8,128)(2,1)}, u32[]{:S(2)}, u32[]{:S(2)}) collective-permute-start(bf16[48,3456]{1,0:T(8,128)(2,1)S(1)} %fusion.8), channel_id=1, source_target_pairs={{0,24},{4,28},{8,16},{12,20},{16,8},{20,12},{24,0},{28,4},{1,25},{... | collective-permute-start | bytes 995336 | tf_op jit(solution)/shard_map/ppermute | solution.py:46
  34.7 20.9 %collective-permute-start.5 = (bf16[2,48,1280]{2,1,0:T(8,128)(2,1)}, bf16[2,48,1280]{2,1,0:T(8,128)(2,1)S(1)}, u32[]{:S(2)}, u32[]{:S(2)}) collective-permute-start(bf16[2,48,1280]{2,1,0:T(8,128)(2,1)} %slice.133), channel_id=1, source_target_pairs={{0,2},{2,0},{1,3},{3,1},{4,6},{6,4},{5,7},{7,5},{8,10},{10,8},{9,1... | collective-permute-start | bytes 737288 | tf_op jit(solution)/shard_map/ppermute | solution.py:49
  37.1 21.1 %copy-start.24 = (bf16[1,1,256,768]{3,2,1,0:T(8,128)(2,1)S(1)}, bf16[1,1,256,768]{3,2,1,0:T(8,128)(2,1)}, u32[]{:S(2)}) copy-start(bf16[1,1,256,768]{3,2,1,0:T(8,128)(2,1)} %param.23) | copy-start | bytes 1179652
  37.1 18.6 %collective-permute-start.6 = (bf16[2,48,1280]{2,1,0:T(8,128)(2,1)}, bf16[2,48,1280]{2,1,0:T(8,128)(2,1)}, u32[]{:S(2)}, u32[]{:S(2)}) collective-permute-start(bf16[2,48,1280]{2,1,0:T(8,128)(2,1)} %slice.134), channel_id=1, source_target_pairs={{0,4},{4,0},{8,12},{12,8},{16,20},{20,16},{24,28},{28,24},{1,5},{5... | collective-permute-start | bytes 737288 | tf_op jit(solution)/shard_map/ppermute | solution.py:43
  38.9 20.7 %collective-permute-start.10 = (bf16[512,768]{0,1:T(8,128)(2,1)S(1)}, bf16[512,768]{0,1:T(8,128)(2,1)}, u32[]{:S(2)}, u32[]{:S(2)}) collective-permute-start(bf16[512,768]{0,1:T(8,128)(2,1)S(1)} %bitcast.81), channel_id=1, source_target_pairs={{0,2},{2,0},{1,3},{3,1},{4,6},{6,4},{5,7},{7,5},{8,10},{10,8},{9,1... | collective-permute-start | bytes 2359304 | tf_op jit(solution)/shard_map/ppermute | solution.py:49
  55.7 6.1 %copy-start.27 = (bf16[2,48,1280]{2,1,0:T(8,128)(2,1)}, bf16[2,48,1280]{2,1,0:T(8,128)(2,1)S(1)}, u32[]{:S(2)}) copy-start(bf16[2,48,1280]{2,1,0:T(8,128)(2,1)S(1)} %collective-permute-done.5.one_ref) | copy-start | bytes 737284
  57.1 28.2 %collective-permute-start.11 = (bf16[4,48,3456]{2,1,0:T(8,128)(2,1)S(1)}, bf16[4,48,3456]{2,1,0:T(8,128)(2,1)}, u32[]{:S(2)}, u32[]{:S(2)}) collective-permute-start(bf16[4,48,3456]{2,1,0:T(8,128)(2,1)S(1)} %pad_maximum_fusion.1.own_ref), channel_id=1, source_target_pairs={{0,4},{4,0},{8,12},{12,8},{16,20},{20,16},{24,28},{28,24},{1,5},{5... | collective-permute-start | bytes 3981320 | tf_op jit(solution)/shard_map/ppermute | solution.py:43
  57.7 30.1 %collective-permute-start.12 = (bf16[4,48,3456]{2,1,0:T(8,128)(2,1)S(1)}, bf16[4,48,3456]{2,1,0:T(8,128)(2,1)}, u32[]{:S(2)}, u32[]{:S(2)}) collective-permute-start(bf16[4,48,3456]{2,1,0:T(8,128)(2,1)S(1)} %pad_maximum_fusion.1.own_ref), channel_id=1, source_target_pairs={{0,2},{2,0},{1,3},{3,1},{4,6},{6,4},{5,7},{7,5},{8,10},{10,8},{9,1... | collective-permute-start | bytes 3981320 | tf_op jit(solution)/shard_map/ppermute | solution.py:49
  61.7 30.2 %copy-start.7 = (bf16[512,768]{0,1:T(8,128)(2,1)}, bf16[512,768]{0,1:T(8,128)(2,1)S(1)}, u32[]{:S(2)}) copy-start(bf16[512,768]{0,1:T(8,128)(2,1)S(1)} %get-tuple-element.153) | copy-start | bytes 2359300
  71.0 19.3 %copy-start.22 = (bf16[768,384]{1,0:T(8,128)(2,1)S(1)}, bf16[768,384]{1,0:T(8,128)(2,1)}, u32[]{:S(2)}) copy-start(bf16[768,384]{1,0:T(8,128)(2,1)} %get-tuple-element.93) | copy-start | bytes 1769476
  87.3 23.5 %collective-permute-start.13 = (bf16[2,48,3456]{2,1,0:T(8,128)(2,1)}, bf16[2,48,3456]{2,1,0:T(8,128)(2,1)}, u32[]{:S(2)}, u32[]{:S(2)}) collective-permute-start(bf16[2,48,3456]{2,1,0:T(8,128)(2,1)} %slice.135), channel_id=1, source_target_pairs={{0,2},{2,0},{1,3},{3,1},{4,6},{6,4},{5,7},{7,5},{8,10},{10,8},{9,1... | collective-permute-start | bytes 1990664 | tf_op jit(solution)/shard_map/ppermute | solution.py:49
  89.7 21.0 %collective-permute-start.14 = (bf16[2,48,3456]{2,1,0:T(8,128)(2,1)}, bf16[2,48,3456]{2,1,0:T(8,128)(2,1)}, u32[]{:S(2)}, u32[]{:S(2)}) collective-permute-start(bf16[2,48,3456]{2,1,0:T(8,128)(2,1)} %slice.136), channel_id=1, source_target_pairs={{0,4},{4,0},{8,12},{12,8},{16,20},{20,16},{24,28},{28,24},{1,5},{5... | collective-permute-start | bytes 1990664 | tf_op jit(solution)/shard_map/ppermute | solution.py:43
  110.8 5.4 %copy-start.23 = (bf16[768,384]{1,0:T(8,128)(2,1)S(1)}, bf16[768,384]{1,0:T(8,128)(2,1)}, u32[]{:S(2)}) copy-start(bf16[768,384]{1,0:T(8,128)(2,1)} %get-tuple-element.99.o) | copy-start | bytes 1769476
  118.1 3.5 %collective-permute-start.15 = (bf16[768,768]{1,0:T(8,128)(2,1)S(1)}, bf16[768,768]{1,0:T(8,128)(2,1)}, u32[]{:S(2)}, u32[]{:S(2)}) collective-permute-start(bf16[768,768]{1,0:T(8,128)(2,1)S(1)} %convolution_convert_fusion.1.p), channel_id=1, source_target_pairs={{0,1},{1,0},{2,3},{3,2},{4,5},{5,4},{6,7},{7,6},{8,9},{9,8},{10,11... | collective-permute-start | bytes 3538952 | tf_op jit(solution)/shard_map/ppermute | solution.py:52
  131.3 3.1 collective-permute-start.16
  156.9 28.5 %collective-permute-start.29 = (bf16[384,1536]{1,0:T(8,128)(2,1)}, bf16[384,1536]{1,0:T(8,128)(2,1)S(1)}, u32[]{:S(2)}, u32[]{:S(2)}) collective-permute-start(bf16[384,1536]{1,0:T(8,128)(2,1)} %get-tuple-element.142), channel_id=1, source_target_pairs={{0,4},{4,0},{8,12},{12,8},{16,20},{20,16},{24,28},{28,24},{1,5},{5... | collective-permute-start | bytes 3538952 | tf_op jit(solution)/shard_map/ppermute | solution.py:43
  158.4 28.3 %collective-permute-start.30 = (bf16[384,1536]{1,0:T(8,128)(2,1)}, bf16[384,1536]{1,0:T(8,128)(2,1)}, u32[]{:S(2)}, u32[]{:S(2)}) collective-permute-start(bf16[384,1536]{1,0:T(8,128)(2,1)} %get-tuple-element.144), channel_id=1, source_target_pairs={{0,2},{2,0},{1,3},{3,1},{4,6},{6,4},{5,7},{7,5},{8,10},{10,8},{9,1... | collective-permute-start | bytes 3538952 | tf_op jit(solution)/shard_map/ppermute | solution.py:49
  160.0 33.8 %collective-permute-start.17 = (bf16[768,768]{1,0:T(8,128)(2,1)}, bf16[768,768]{1,0:T(8,128)(2,1)S(1)}, u32[]{:S(2)}, u32[]{:S(2)}) collective-permute-start(bf16[768,768]{1,0:T(8,128)(2,1)} %get-tuple-element.116.p), channel_id=1, source_target_pairs={{0,1},{1,0},{2,3},{3,2},{4,5},{5,4},{6,7},{7,6},{8,9},{9,8},{10,11... | collective-permute-start | bytes 3538952 | tf_op jit(solution)/shard_map/ppermute | solution.py:52
  191.1 45.3 %collective-permute-start.31 = (bf16[192,1536]{1,0:T(8,128)(2,1)}, bf16[192,1536]{1,0:T(8,128)(2,1)}, u32[]{:S(2)}, u32[]{:S(2)}) collective-permute-start(bf16[192,1536]{1,0:T(8,128)(2,1)} %get-tuple-element.146), channel_id=1, source_target_pairs={{0,2},{2,0},{1,3},{3,1},{4,6},{6,4},{5,7},{7,5},{8,10},{10,8},{9,1... | collective-permute-start | bytes 1769480 | tf_op jit(solution)/shard_map/ppermute | solution.py:49
  192.8 43.5 %collective-permute-start.32 = (bf16[192,1536]{1,0:T(8,128)(2,1)}, bf16[192,1536]{1,0:T(8,128)(2,1)}, u32[]{:S(2)}, u32[]{:S(2)}) collective-permute-start(bf16[192,1536]{1,0:T(8,128)(2,1)} %get-tuple-element.148), channel_id=1, source_target_pairs={{0,4},{4,0},{8,12},{12,8},{16,20},{20,16},{24,28},{28,24},{1,5},{5... | collective-permute-start | bytes 1769480 | tf_op jit(solution)/shard_map/ppermute | solution.py:43
  201.5 16.1 %copy-start.21 = (bf16[768,384]{1,0:T(8,128)(2,1)S(1)}, bf16[768,384]{1,0:T(8,128)(2,1)}, u32[]{:S(2)}) copy-start(bf16[768,384]{1,0:T(8,128)(2,1)} %get-tuple-element.97) | copy-start | bytes 1769476
  225.1 18.2 %collective-permute-start.18 = (bf16[256,768]{1,0:T(8,128)(2,1)}, bf16[256,768]{1,0:T(8,128)(2,1)}, u32[]{:S(2)}, u32[]{:S(2)}) collective-permute-start(bf16[256,768]{1,0:T(8,128)(2,1)} %dynamic-slice_bitcast_fusion), channel_id=1, source_target_pairs={{0,1},{1,0},{2,3},{3,2},{4,5},{5,4},{6,7},{7,6},{8,9},{9,8},{10,11... | collective-permute-start | bytes 1179656 | tf_op jit(solution)/shard_map/ppermute | solution.py:52
  234.9 18.2 %collective-permute-start.22 = (bf16[384,896]{1,0:T(8,128)(2,1)}, bf16[384,896]{1,0:T(8,128)(2,1)}, u32[]{:S(2)}, u32[]{:S(2)}) collective-permute-start(bf16[384,896]{1,0:T(8,128)(2,1)} %get-tuple-element.132), channel_id=1, source_target_pairs={{0,2},{2,0},{1,3},{3,1},{4,6},{6,4},{5,7},{7,5},{8,10},{10,8},{9,1... | collective-permute-start | bytes 2064392 | tf_op jit(solution)/shard_map/ppermute | solution.py:49
  235.4 15.8 %collective-permute-start.21 = (bf16[384,768]{1,0:T(8,128)(2,1)}, bf16[384,768]{1,0:T(8,128)(2,1)}, u32[]{:S(2)}, u32[]{:S(2)}) collective-permute-start(bf16[384,768]{1,0:T(8,128)(2,1)} %get-tuple-element.130), channel_id=1, source_target_pairs={{0,4},{4,0},{8,12},{12,8},{16,20},{20,16},{24,28},{28,24},{1,5},{5... | collective-permute-start | bytes 1769480 | tf_op jit(solution)/shard_map/ppermute | solution.py:43
  239.2 7.6 %copy-start.6 = (bf16[1,512,768]{2,1,0:T(8,128)(2,1)S(1)}, bf16[1,512,768]{2,1,0:T(8,128)(2,1)}, u32[]{:S(2)}) copy-start(bf16[1,512,768]{2,1,0:T(8,128)(2,1)} %copy-done.5) | copy-start | bytes 2359300
  239.2 18.8 %collective-permute-start.33 = (bf16[48,3072]{1,0:T(8,128)(2,1)}, bf16[48,3072]{1,0:T(8,128)(2,1)S(1)}, u32[]{:S(2)}, u32[]{:S(2)}) collective-permute-start(bf16[48,3072]{1,0:T(8,128)(2,1)} %get-tuple-element.150), channel_id=1, source_target_pairs={{0,8},{4,12},{8,0},{12,4},{16,24},{20,28},{24,16},{28,20},{1,9},{5... | collective-permute-start | bytes 884744 | tf_op jit(solution)/shard_map/ppermute | solution.py:46
  240.4 23.2 %collective-permute-start.34 = (bf16[48,3072]{1,0:T(8,128)(2,1)}, bf16[48,3072]{1,0:T(8,128)(2,1)}, u32[]{:S(2)}, u32[]{:S(2)}) collective-permute-start(bf16[48,3072]{1,0:T(8,128)(2,1)} %get-tuple-element.151), channel_id=1, source_target_pairs={{0,16},{4,20},{8,24},{12,28},{16,0},{20,4},{24,8},{28,12},{1,17},{... | collective-permute-start | bytes 884744 | tf_op jit(solution)/shard_map/ppermute | solution.py:46
  243.3 25.4 %collective-permute-start.35 = (bf16[48,3072]{1,0:T(8,128)(2,1)}, bf16[48,3072]{1,0:T(8,128)(2,1)}, u32[]{:S(2)}, u32[]{:S(2)}) collective-permute-start(bf16[48,3072]{1,0:T(8,128)(2,1)} %get-tuple-element.152), channel_id=1, source_target_pairs={{0,24},{4,28},{8,16},{12,20},{16,8},{20,12},{24,0},{28,4},{1,25},{... | collective-permute-start | bytes 884744 | tf_op jit(solution)/shard_map/ppermute | solution.py:46
  251.2 22.7 %collective-permute-start.19 = (bf16[256,768]{1,0:T(8,128)(2,1)}, bf16[256,768]{1,0:T(8,128)(2,1)}, u32[]{:S(2)}, u32[]{:S(2)}) collective-permute-start(bf16[256,768]{1,0:T(8,128)(2,1)} %fusion.6), channel_id=1, source_target_pairs={{0,2},{2,0},{1,3},{3,1},{4,6},{6,4},{5,7},{7,5},{8,10},{10,8},{9,1... | collective-permute-start | bytes 1179656 | tf_op jit(solution)/shard_map/ppermute | solution.py:49
  256.9 20.4 %collective-permute-start.24 = (bf16[192,896]{1,0:T(8,128)(2,1)}, bf16[192,896]{1,0:T(8,128)(2,1)}, u32[]{:S(2)}, u32[]{:S(2)}) collective-permute-start(bf16[192,896]{1,0:T(8,128)(2,1)} %get-tuple-element.136), channel_id=1, source_target_pairs={{0,4},{4,0},{8,12},{12,8},{16,20},{20,16},{24,28},{28,24},{1,5},{5... | collective-permute-start | bytes 1032200 | tf_op jit(solution)/shard_map/ppermute | solution.py:43
  258.0 19.3 %collective-permute-start.23 = (bf16[192,768]{1,0:T(8,128)(2,1)}, bf16[192,768]{1,0:T(8,128)(2,1)}, u32[]{:S(2)}, u32[]{:S(2)}) collective-permute-start(bf16[192,768]{1,0:T(8,128)(2,1)} %get-tuple-element.134), channel_id=1, source_target_pairs={{0,2},{2,0},{1,3},{3,1},{4,6},{6,4},{5,7},{7,5},{8,10},{10,8},{9,1... | collective-permute-start | bytes 884744 | tf_op jit(solution)/shard_map/ppermute | solution.py:49
  270.8 12.6 %collective-permute-start.36 = (bf16[48,3072]{1,0:T(8,128)(2,1)}, bf16[48,3072]{1,0:T(8,128)(2,1)}, u32[]{:S(2)}, u32[]{:S(2)}) collective-permute-start(bf16[48,3072]{1,0:T(8,128)(2,1)} %add_convert_fusion), channel_id=1, source_target_pairs={{0,2},{2,0},{1,3},{3,1},{4,6},{6,4},{5,7},{7,5},{8,10},{10,8},{9,1... | collective-permute-start | bytes 884744 | tf_op jit(solution)/shard_map/ppermute | solution.py:49
  277.2 29.1 %collective-permute-start.20 = (bf16[768,768]{1,0:T(8,128)(2,1)}, bf16[768,768]{1,0:T(8,128)(2,1)S(1)}, u32[]{:S(2)}, u32[]{:S(2)}) collective-permute-start(bf16[768,768]{1,0:T(8,128)(2,1)} %pad_maximum_fusion.3), channel_id=1, source_target_pairs={{0,1},{1,0},{2,3},{3,2},{4,5},{5,4},{6,7},{7,6},{8,9},{9,8},{10,11... | collective-permute-start | bytes 3538952 | tf_op jit(solution)/shard_map/ppermute | solution.py:52
  279.5 18.2 %copy-start.26 = (f32[48,1664]{1,0:T(8,128)S(1)}, f32[48,1664]{1,0:T(8,128)}, u32[]{:S(2)}) copy-start(f32[48,1664]{1,0:T(8,128)} %get-tuple-element.137) | copy-start | bytes 958468
  279.5 7.9 %collective-permute-start.25 = (bf16[48,1664]{1,0:T(8,128)(2,1)}, bf16[48,1664]{1,0:T(8,128)(2,1)S(1)}, u32[]{:S(2)}, u32[]{:S(2)}) collective-permute-start(bf16[48,1664]{1,0:T(8,128)(2,1)} %get-tuple-element.138), channel_id=1, source_target_pairs={{0,8},{4,12},{8,0},{12,4},{16,24},{20,28},{24,16},{28,20},{1,9},{5... | collective-permute-start | bytes 479240 | tf_op jit(solution)/shard_map/ppermute | solution.py:46
  279.5 15.5 %collective-permute-start.26 = (bf16[48,1664]{1,0:T(8,128)(2,1)}, bf16[48,1664]{1,0:T(8,128)(2,1)S(1)}, u32[]{:S(2)}, u32[]{:S(2)}) collective-permute-start(bf16[48,1664]{1,0:T(8,128)(2,1)} %get-tuple-element.139), channel_id=1, source_target_pairs={{0,16},{4,20},{8,24},{12,28},{16,0},{20,4},{24,8},{28,12},{1,17},{... | collective-permute-start | bytes 479240 | tf_op jit(solution)/shard_map/ppermute | solution.py:46
  283.3 14.4 %collective-permute-start.27 = (bf16[48,1664]{1,0:T(8,128)(2,1)}, bf16[48,1664]{1,0:T(8,128)(2,1)S(1)}, u32[]{:S(2)}, u32[]{:S(2)}) collective-permute-start(bf16[48,1664]{1,0:T(8,128)(2,1)} %get-tuple-element.140), channel_id=1, source_target_pairs={{0,24},{4,28},{8,16},{12,20},{16,8},{20,12},{24,0},{28,4},{1,25},{... | collective-permute-start | bytes 479240 | tf_op jit(solution)/shard_map/ppermute | solution.py:46
  297.8 5.4 %collective-permute-start.28 = (bf16[48,1664]{1,0:T(8,128)(2,1)S(1)}, bf16[48,1664]{1,0:T(8,128)(2,1)S(1)}, u32[]{:S(2)}, u32[]{:S(2)}) collective-permute-start(bf16[48,1664]{1,0:T(8,128)(2,1)S(1)} %add_convert_fusion.1), channel_id=1, source_target_pairs={{0,2},{2,0},{1,3},{3,1},{4,6},{6,4},{5,7},{7,5},{8,10},{10,8},{9,1... | collective-permute-start | bytes 479240 | tf_op jit(solution)/shard_map/ppermute | solution.py:49
  299.6 6.7 %copy-start.3 = (bf16[512,768]{1,0:T(8,128)(2,1)S(1)}, bf16[512,768]{1,0:T(8,128)(2,1)}, u32[]{:S(2)}) copy-start(bf16[512,768]{1,0:T(8,128)(2,1)} %copy-done.2) | copy-start | bytes 2359300
  (20 other events, 44.1 us)

commit v2 on v1

--- a/solution.py
+++ b/solution.py
@@ -56,27 +56,114 @@
         return low.astype(f32) + self.over_tp(low).astype(f32)
 
 
-def assemble(place, cuts, own, across, along, far_one, far_two):
-    half = own.shape[1]
+def pack_early(grid, weights, vectors, tables):
+    rows = weights[0].shape[0]
+    edges = [sum(w.shape[1] for w in weights[:i]) for i in range(len(weights) + 1)]
+    cols = edges[-1] + LANES
+    count = len(weights)
+
+    def body(place, *refs):
+        out, half_out, lines = refs[-3:]
+        for ref, low, high in zip(refs, edges, edges[1:]):
+            out[:, low:high] = ref[...]
+        lines[...] = jnp.zeros_like(lines)
+        at = 0
+        for ref in refs[count:-3]:
+            height, width = ref.shape
+            lines[at : at + height, :width] = ref[...].astype(f32)
+            at += height
+        out[:, edges[-1] :] = lines[...].astype(bf16)
+        half_out[...] = out[pl.ds(pl.multiple_of(place[2] * (rows // 2), 16), rows // 2), :]
+
+    vmem = pl.BlockSpec(memory_space=pltpu.VMEM)
+    args = [*weights, *vectors, *tables]
+    outs = [like((rows, cols), bf16), like((rows // 2, cols), bf16)]
+    return pl.pallas_call(
+        body,
+        out_shape=outs,
+        in_specs=[pl.BlockSpec(memory_space=pltpu.SMEM)] + [vmem] * len(args),
+        out_specs=[vmem] * 2,
+        scratch_shapes=[pltpu.VMEM((rows, LANES), f32)],
+        cost_estimate=cost(0, *args, *outs),
+        name="pack_early",
+    )(grid.place, *args)
+
+
+def pack_late(grid, shard, late):
+    rows, head = shard.shape
+    cols = sum(w.shape[1] for w in late)
+
+    def body(place, early_ref, *refs):
+        out, half_out = refs[-2:]
+        out[:, :head] = early_ref[...]
+        here = pl.ds(pl.multiple_of(place[2] * (rows // 2), 16), rows // 2)
+        low = 0
+        for ref in refs[:-2]:
+            high = low + ref.shape[1]
+            out[:, head + low : head + high] = ref[...]
+            half_out[:, low:high] = ref[here, :]
+            low = high
+
+    vmem = pl.BlockSpec(memory_space=pltpu.VMEM)
+    outs = [like((rows, head + cols), bf16), like((rows // 2, cols), bf16)]
+    return pl.pallas_call(
+        body,
+        out_shape=outs,
+        in_specs=[pl.BlockSpec(memory_space=pltpu.SMEM)] + [vmem] * (1 + len(late)),
+        out_specs=[vmem] * 2,
+        cost_estimate=cost(0, shard, *late, *outs),
+        name="pack_late",
+    )(grid.place, shard, *late)
+
+
+def join(pieces):
+    height, cols = pieces[0].shape
+
+    def body(*refs):
+        for i, ref in enumerate(refs[:-1]):
+            refs[-1][i * height : (i + 1) * height, :] = ref[...]
+
+    vmem = pl.BlockSpec(memory_space=pltpu.VMEM)
+    out = like((len(pieces) * height, cols), pieces[0].dtype)
+    return pl.pallas_call(
+        body,
+        out_shape=out,
+        in_specs=[vmem] * len(pieces),
+        out_specs=vmem,
+        cost_estimate=cost(0, out, out),
+        name="join",
+    )(*pieces)
+
+
+def assemble(grid, cuts, base, own, side, came, across, along):
+    full = own.shape[0]
+    half = full // 2
     edges = [sum(cuts[:i]) for i in range(len(cuts) + 1)]
 
-    def body(place_ref, own_ref, across_ref, along_ref, one_ref, two_ref, *outs):
-        outer, inner, row = place_ref[0], place_ref[1], place_ref[2]
-
-        def put(piece, at_piece, step, swap_inner, swap_row):
-            at = ((outer ^ step) * 2 + (inner ^ swap_inner)) * 2 + (row ^ swap_row)
-            here = pl.ds(pl.multiple_of(at * half, 16), half)
+    def body(place, own_ref, side_ref, came_ref, across_ref, along_ref, *outs):
+        outer, inner, row = place[0], place[1], place[2]
+
+        def put(ref, start, length, step, swap_inner, swap_row, skip=0):
+            at = (outer ^ step) * 2 + (inner ^ swap_inner)
+            if length == half:
+                at = at * 2 + (row ^ swap_row)
+            here = pl.ds(pl.multiple_of(at * length, 16), length)
             for out, low, high in zip(outs, edges, edges[1:]):
-                out[here, :] = piece[at_piece, :, low:high]
-
-        for step in range(4):
-            put(own_ref, step, step, 0, 0)
-            put(across_ref, step, step, 1, 0)
-            put(along_ref, step, step, 0, 1)
-            put(one_ref if step < 2 else two_ref, step % 2, step, 1, 1)
+                out[here, :] = ref[start : start + length, skip + low : skip + high]
+
+        put(own_ref, 0, full, 0, 0, 0, base)
+        put(side_ref, 0, full, 0, 1, 0, base)
+        for step in (1, 2, 3):
+            start = (step - 1) * half
+            put(came_ref, start, half, step, 0, 0)
+            put(across_ref, start, half, step, 1, 0)
+            put(along_ref, start, half, step, 0, 1)
+            for out in outs:
+                at = (((outer ^ step) * 2 + (inner ^ 1)) * 2 + (row ^ 1)) * half
+                out[pl.ds(pl.multiple_of(at, 16), half), :] = jnp.zeros((half, out.shape[1]), bf16)
 
     vmem = pl.BlockSpec(memory_space=pltpu.VMEM)
-    outs = [like((16 * half, cols), own.dtype) for cols in cuts]
+    outs = [like((8 * full, cols), own.dtype) for cols in cuts]
     return pl.pallas_call(
         body,
         out_shape=outs,
@@ -85,42 +172,64 @@
         compiler_params=pltpu.CompilerParams(vmem_limit_bytes=VMEM_LIMIT),
         cost_estimate=cost(0, *outs, *outs),
         name="assemble",
-    )(place, own, across, along, far_one, far_two)
-
-
-def gather_rows(grid, early, late):
-    cuts = [[a.shape[1] for a in arrays] for arrays in (early, late)]
-    if not grid.staged:
-        return [[lax.all_gather(a, "fsdp", axis=0, tiled=True) for a in arrays] for arrays in (early, late)]
-    early, late = [jnp.concatenate(arrays, 1) for arrays in (early, late)]
-    half = early.shape[0] // 2
-
-    def lines(mine):
-        return [grid.over_outer(mine, step) for step in (1, 2, 3)]
-
-    def pairs(own):
-        return grid.over_inner(own), grid.over_ctx(own)
-
-    def corners(across, along):
-        return grid.over_ctx(across[:2]), grid.over_inner(along[2:])
-
-    mine, late_mine = [
-        lax.dynamic_slice_in_dim(a, grid.row * half, half, 0) for a in (early, late)
-    ]
-    came = lines(mine)
-    came, late_mine = lax.optimization_barrier((came, late_mine))
-    own = jnp.stack([mine] + came)
-    across, along = pairs(own)
-    far = corners(across, along)
-    late_came = lines(late_mine)
-    far, late_came = lax.optimization_barrier((far, late_came))
-    late_own = jnp.stack([late_mine] + late_came)
-    late_pairs = pairs(late_own)
-    late_far = corners(*late_pairs)
-    return (
-        assemble(grid.place, cuts[0], own, across, along, *far),
-        assemble(grid.place, cuts[1], late_own, *late_pairs, *late_far),
-    )
+    )(grid.place, own, side, came, across, along)
+
+
+def complete(grid, arrays, far_one, far_two):
+    half = far_one.shape[0] // 3
+    first = 0
+    while sum(a.shape[1] for a in arrays[: first + 1]) <= far_one.shape[1]:
+        first += 1
+    count = len(arrays)
+    copies = 3 * count
+
+    def body(place, one_ref, two_ref, *refs):
+        outs, sems = refs[count : 2 * count], refs[2 * count]
+        outer, inner, row = place[0], place[1], place[2]
+        started = []
+        low = 0
+        for i, out in enumerate(outs):
+            ref = one_ref if i < first else two_ref
+            if i == first:
+                low = 0
+            cols = out.shape[1]
+            for step in (1, 2, 3):
+                at = (((outer ^ step) * 2 + (inner ^ 1)) * 2 + (row ^ 1)) * half
+                copy = pltpu.make_async_copy(
+                    ref.at[(step - 1) * half : step * half, low : low + cols],
+                    out.at[pl.ds(pl.multiple_of(at, 16), half), :],
+                    sems.at[len(started)],
+                )
+                copy.start()
+                started.append(copy)
+            low += cols
+        for copy in started:
+            copy.wait()
+
+    vmem = pl.BlockSpec(memory_space=pltpu.VMEM)
+    anywhere = pl.BlockSpec(memory_space=pl.ANY)
+    return pl.pallas_call(
+        body,
+        out_shape=[like(a.shape, a.dtype) for a in arrays],
+        in_specs=[pl.BlockSpec(memory_space=pltpu.SMEM), vmem, vmem] + [anywhere] * count,
+        out_specs=[anywhere] * count,
+        scratch_shapes=[pltpu.SemaphoreType.DMA((copies,))],
+        input_output_aliases={3 + i: i for i in range(count)},
+        cost_estimate=cost(0, far_one, far_two, far_one, far_two),
+        name="complete",
+    )(grid.place, far_one, far_two, *arrays)
+
+
+def lines_of(grid, mine):
+    return [grid.over_outer(mine, step) for step in (1, 2, 3)]
+
+
+def pairs_of(grid, came):
+    return grid.over_inner(came), grid.over_ctx(came)
+
+
+def corners_of(grid, across, along, cut):
+    return grid.over_ctx(across[:, :cut]), grid.over_inner(along[:, cut:])
 
 
 def pick(array, at, axis):
@@ -173,18 +282,55 @@
     return 256 if rows % 256 == 0 else rows
 
 
-def ffn_forward(inputs, part, other, output_add, gain, shift, up_mat, up_add, down_turned):
-    rows, width = inputs.shape
+def first_norm(prompt, conts, part, other, output_add, gain, shift):
+    prompt_len, width = prompt.shape
+    rows = prompt_len + conts.shape[0]
+    tile = row_tile(prompt_len)
+    ahead = prompt_len // tile
+
+    def body(x, c, p, o, b, g, s, norm_out, inv_out, low_out, turned_out):
+        rows_in = jnp.where(pl.program_id(0) < ahead, x[...].astype(f32), c[...].astype(f32))
+        normed, inverse = norm_rows(rows_in + (p[...].astype(f32) + o[...].astype(f32)) + b[...])
+        norm_out[...] = normed
+        inv_out[...] = jnp.broadcast_to(inverse, inv_out.shape)
+        value = normed * g[...] + s[...]
+        low_out[...] = value.astype(bf16)
+        turned_out[...] = value.T.astype(bf16)
+
+    def tiled(array):
+        return pl.BlockSpec((tile, array.shape[1]), lambda i: (i, 0))
+
+    args = [prompt, conts, part, other, output_add, gain, shift]
+    outs = [
+        like((rows, width), f32),
+        like((rows, LANES), f32),
+        like((rows, width), bf16),
+        like((width, rows), bf16),
+    ]
+    return pl.pallas_call(
+        body,
+        grid=(rows // tile,),
+        out_shape=outs,
+        in_specs=[
+            pl.BlockSpec((tile, width), lambda i: (jnp.minimum(i, ahead - 1), 0)),
+            pl.BlockSpec((tile, width), lambda i: (jnp.maximum(i - ahead, 0), 0)),
+        ]
+        + [tiled(a) for a in args[2:4]]
+        + [whole_block(a) for a in args[4:]],
+        out_specs=[tiled(a) for a in outs[:3]] + [pl.BlockSpec((width, tile), lambda i: (0, i))],
+        compiler_params=pltpu.CompilerParams(vmem_limit_bytes=VMEM_LIMIT),
+        cost_estimate=cost(0, *args, *outs),
+        name="first_norm",
+    )(*args)
+
+
+def ffn_forward(low, up_mat, up_add, down_turned):
+    rows, width = low.shape
     hidden = up_mat.shape[1]
     tile = row_tile(rows)
 
-    def body(x, p, o, b, g, s, up, ub, dn, norm_out, inv_out, act_out, slope_out, part_out):
-        hidden_in = x[...].astype(f32) + (p[...].astype(f32) + o[...].astype(f32)) + b[...]
-        normed, inverse = norm_rows(hidden_in)
-        norm_out[...] = normed
-        inv_out[...] = jnp.broadcast_to(inverse, inv_out.shape)
-        low = (normed * g[...] + s[...]).astype(bf16)
-        inner = product(low, up[...]) + ub[...]
+    def body(x, up, ub, dn, act_out, slope_out, part_out):
+        inner = product(x[...], up[...]) + ub[...]
         normal_cdf = 0.5 * (1.0 + lax.erf(inner * math.sqrt(0.5)))
         act = (inner * normal_cdf).astype(bf16)
         act_out[...] = act
@@ -193,8 +339,6 @@
         part_out[...] = contract_cols(act, dn[...]).astype(bf16)
 
     outs = [
-        like((rows, width), f32),
-        like((rows, LANES), f32),
         like((rows, hidden), bf16),
         like((rows, hidden), bf16),
         like((rows, width), bf16),
@@ -203,12 +347,12 @@
     def tiled(array):
         return pl.BlockSpec((tile, array.shape[1]), lambda i: (i, 0))
 
-    args = [inputs, part, other, output_add, gain, shift, up_mat, up_add, down_turned]
+    args = [low, up_mat, up_add, down_turned]
     return pl.pallas_call(
         body,
         grid=(rows // tile,),
         out_shape=outs,
-        in_specs=[tiled(a) for a in args[:3]] + [whole_block(a) for a in args[3:]],
+        in_specs=[tiled(low)] + [whole_block(a) for a in args[1:]],
         out_specs=[tiled(a) for a in outs],
         compiler_params=pltpu.CompilerParams(vmem_limit_bytes=VMEM_LIMIT),
         cost_estimate=cost(4 * rows * width * hidden, *args, *outs, transcendentals=2 * rows * hidden),
@@ -238,7 +382,7 @@
                 out[half * block : half * (block + 1), :] = full_ref[pl.ds(at, half), :]
 
 
-def ffn_backward(grid, norm1, gain1, shift1, part, other, down_add, gain2, shift2, cots, act, slope, up_mat, down_turned):
+def ffn_backward(grid, norm1, turned1, gain1, shift1, part, other, down_add, gain2, shift2, cots, act, slope, up_mat, down_turned):
     rows, width = norm1.shape
     hidden = up_mat.shape[1]
     tile = 256
@@ -246,11 +390,11 @@
     prompt_len = cots[0].shape[0]
     count = 2 if grid.staged else 1
 
-    def body(place, n1, g1, s1, p, o, db, g2, s2, cp, cc, u, sl, up, dn, *rest):
-        outs, scratch = rest[:-6], rest[-6:]
+    def body(place, n1, x1_t, g1, s1, p, o, db, g2, s2, cp, cc, u, sl, up, dn, *rest):
+        outs, scratch = rest[:-5], rest[-5:]
         y_p, y_c, dh2, dx1, sums, up_sum = outs[:6]
         up_outs, down_outs = outs[6 : 6 + count], outs[6 + count :]
-        df, x1_t, df_t, acc, full_up, full_down = scratch
+        df, df_t, acc, full_up, full_down = scratch
         step = pl.program_id(0)
 
         @pl.when(step == 0)
@@ -275,7 +419,6 @@
                 df[here, :] = low
                 wide = low.astype(f32)
                 df_t[:, here] = wide.T.astype(bf16)
-                x1_t[:, here] = first.T.astype(bf16)
                 total[0] += column_sums(cot * normed)
                 total[1] += column_sums(cot)
                 total[2] += column_sums(wide)
@@ -299,7 +442,7 @@
     def tiled(array):
         return pl.BlockSpec((array.shape[0], tile), lambda j: (0, j))
 
-    fixed = [norm1, gain1, shift1, part, other, down_add, gain2, shift2, *cots]
+    fixed = [norm1, turned1, gain1, shift1, part, other, down_add, gain2, shift2, *cots]
     moving = [act, slope, up_mat, down_turned]
     outs = [
         like((prompt_len, width), bf16),
@@ -321,7 +464,6 @@
         scratch_shapes=[
             pltpu.VMEM((rows, width), bf16),
             pltpu.VMEM((width, rows), bf16),
-            pltpu.VMEM((width, rows), bf16),
             pltpu.VMEM((rows, width), f32),
             pltpu.VMEM((width, tile), bf16),
             pltpu.VMEM((width, tile), bf16),
@@ -384,13 +526,15 @@
     )(grid.place, *args)
 
 
-def scatter_split(grid, first, second):
+def scatter_split(grid, first, second, after=None):
     if not grid.staged:
         both = jnp.concatenate([first[0], second[0]], 1)
         both = lax.psum_scatter(both, "fsdp", scatter_dimension=0, tiled=True)
         return lax.psum(both, "ctx")
     came_first = grid.over_inner(first[1])
     came_second = grid.over_ctx(second[1])
+    if after is not None:
+        came_first, came_second, _ = lax.optimization_barrier((came_first, came_second, after))
     f_keep, f_send, s_keep, s_send = fold_pair(grid, (first[0], came_first), (second[0], came_second))
     came_first = grid.over_ctx(f_send)
     came_second = grid.over_inner(s_send)
@@ -409,7 +553,9 @@
     return (lane < LANES // 2) if index == 0 else (lane >= LANES // 2)
 
 
-def attention_forward(queries, keys, values, prev_logits, cont_len, prompt_len):
+def attention_forward(queries, keys, values, prev_logits, cont_len, prompt_len, pairs, held=()):
+    begin, end = pairs
+    kept = len(held)
     rows, width = queries.shape
     total = keys.shape[0]
     cont_size = rows - prompt_len
@@ -417,7 +563,9 @@
     heads = prev_logits.shape[0]
     chunk = row_tile(prompt_len)
 
-    def body(length, q, k, v, prev, logits, probs_p, probs_c, out):
+    def body(length, q, k, v, prev, *refs):
+        logits, probs_p, probs_c, out = refs[kept:]
+
         def soft(scores):
             weights = jnp.exp(scores - jnp.max(scores, axis=-1, keepdims=True))
             return (weights * (1.0 / jnp.sum(weights, axis=-1, keepdims=True))).astype(bf16)
@@ -451,25 +599,27 @@
     ]
 
     def columns(array):
-        return pl.BlockSpec((array.shape[0], LANES), lambda i: (0, i))
-
-    def pairs(array):
-        return pl.BlockSpec((2,) + array.shape[1:], lambda i: (i, 0, 0))
+        return pl.BlockSpec((array.shape[0], LANES), lambda i: (0, begin + i))
+
+    def pair_of(array):
+        return pl.BlockSpec((2,) + array.shape[1:], lambda i: (begin + i, 0, 0))
 
     args = [queries, keys, values, prev_logits]
     scores = heads * (prompt_len * full_len + cont_size * total)
     return pl.pallas_call(
         body,
-        grid=(heads // 2,),
+        grid=(end - begin,),
         out_shape=outs,
         in_specs=[pl.BlockSpec(memory_space=pltpu.SMEM)]
         + [columns(a) for a in args[:3]]
-        + [pairs(prev_logits)],
-        out_specs=[pairs(a) for a in outs[:3]] + [columns(outs[3])],
+        + [pair_of(prev_logits)]
+        + [pl.BlockSpec(memory_space=pl.ANY)] * kept,
+        out_specs=[pair_of(a) for a in outs[:3]] + [columns(outs[3])],
         compiler_params=pltpu.CompilerParams(vmem_limit_bytes=VMEM_LIMIT),
-        cost_estimate=cost(512 * scores, *args, *outs, transcendentals=scores),
+        input_output_aliases={5 + i: i for i in range(kept)},
+        cost_estimate=cost((end - begin) * 256 * scores, *args, transcendentals=scores),
         name="attention_forward",
-    )(cont_len, *args)
+    )(cont_len, *args, *held)
 
 
 def attention_backward(queries, keys, values, dout, attended, probs_p, probs_c, cots, scale):
@@ -721,54 +871,84 @@
     head_size = width // head_count
     scale = 1.0 / math.sqrt(head_size)
 
+    mine, conts = prompt[0], continuations[0, 0]
     lines = [v[None] for v in (output_bias, first_gain, first_shift, down_bias, second_gain, second_shift)]
-    lines += [query_bias, value_bias, up_bias]
-    small = jnp.concatenate([jnp.pad(v, ((0, 0), (0, LANES - v.shape[1]))) for v in lines], 0)
-    small = jnp.pad(small, ((0, rows - small.shape[0]), (0, 0)))
-    early, late = gather_rows(
-        grid,
-        [query_weight, key_weight, value_weight, small],
-        [output_weight.T, up_weight, down_weight.T],
-    )
-    query_mat, key_mat, value_mat, small = early
-    output_turned, up_mat, down_turned = late
+    tables = [query_bias, value_bias, up_bias]
+    early = [query_weight, key_weight, value_weight, output_weight.T]
+    late = [up_weight, down_weight.T]
+    shard, half_shard = pack_early(grid, early, lines, tables)
+    cuts = [width, width, width, width, LANES]
+    cut = 2 * width
+    if grid.staged:
+        came = lines_of(grid, half_shard)
+        sent, shard = lax.optimization_barrier((mine, shard))
+        theirs = grid.over_ctx(sent)
+        shards, late_half = pack_late(grid, shard, late)
+        side = grid.over_inner(shards)
+        came, late_half, theirs = lax.optimization_barrier((came, late_half, theirs))
+        came = join(came)
+        across, along = pairs_of(grid, came)
+        far = corners_of(grid, across, along, cut)
+        late_came = lines_of(grid, late_half)
+        far, late_came = lax.optimization_barrier((far, late_came))
+        early = complete(
+            grid, assemble(grid, cuts, 0, shards, side, came, across, along), *far
+        )
+        late_came = join(late_came)
+        late_across, late_along = pairs_of(grid, late_came)
+    else:
+        shards = [shard] + late
+        shards = [lax.all_gather(a, "fsdp", axis=0, tiled=True) for a in shards]
+        edges = [sum(cuts[:i]) for i in range(len(cuts) + 1)]
+        early = [shards[0][:, low:high] for low, high in zip(edges, edges[1:])]
+        late = shards[1:]
+    query_mat, key_mat, value_mat, output_turned, small = early
     vectors, query_add, value_add, up_line = unpack_small(
         grid, small, head_count, head_size, up_bias.shape[0]
     )
     output_line, gain1, shift1, down_line, gain2, shift2 = [vectors[i : i + 1] for i in range(6)]
 
-    mine = prompt[0]
-    inputs = jnp.concatenate([mine, continuations[0, 0]], 0)
+    inputs = jnp.concatenate([mine, conts], 0)
     if sizes[1] == 2:
-        theirs = grid.over_ctx(mine)
+        if not grid.staged:
+            theirs = grid.over_ctx(mine)
         whole = jnp.concatenate(
-            [
-                jnp.where(grid.row == 0, mine, theirs),
-                jnp.where(grid.row == 0, theirs, mine),
-                continuations[0, 0],
-            ],
-            0,
+            [jnp.where(grid.row == 0, mine, theirs), jnp.where(grid.row == 0, theirs, mine), conts], 0
         )
     else:
-        whole = jnp.concatenate(
-            [lax.all_gather(mine, "ctx", axis=0, tiled=True), continuations[0, 0]], 0
-        )
+        whole = jnp.concatenate([lax.all_gather(mine, "ctx", axis=0, tiled=True), conts], 0)
     full_len = whole.shape[0] - cont_size
     whole_t, inputs_t = whole.T, inputs.T
 
     queries = ((product(inputs, query_mat) + query_add) * scale).astype(bf16)
     keys = product(whole, key_mat).astype(bf16)
     values = (product(whole, value_mat) + value_add).astype(bf16)
+    queries, whole_t, inputs_t = lax.optimization_barrier((queries, whole_t, inputs_t))
+    attention = (queries, keys, values, prev_logits[0, 0], cont_len, prompt_len)
+    pair_count = head_count // 2
+    held = attention_forward(*attention, (0, pair_count - 1))
+    if grid.staged:
+        late_across, late_along, held = lax.optimization_barrier((late_across, late_along, held))
+        far = corners_of(grid, late_across, late_along, hidden)
     new_logits, probs_p, probs_c, attended = attention_forward(
-        queries, keys, values, prev_logits[0, 0], cont_len, prompt_len
+        *attention, (pair_count - 1, pair_count), held
     )
+    if grid.staged:
+        late = assemble(
+            grid, [hidden, hidden], sum(cuts), shards, side, late_came, late_across, late_along
+        )
     part = contract_cols(attended, output_turned).astype(bf16)
-    first_norm, first_inv, activated, slope, part2 = ffn_forward(
-        inputs, part, grid.over_tp(part), output_line, gain1, shift1, up_mat, up_line, down_turned
+    norm1, inv1, low1, turned1 = first_norm(
+        mine, conts, part, grid.over_tp(part), output_line, gain1, shift1
     )
+    if grid.staged:
+        late = complete(grid, late, *far)
+    up_mat, down_turned = late
+    activated, slope, part2 = ffn_forward(low1, up_mat, up_line, down_turned)
     results = ffn_backward(
         grid,
-        first_norm,
+        norm1,
+        turned1,
         gain1,
         shift1,
         part2,
@@ -785,16 +965,18 @@
     result_prompt, result_cont, grad_second, part3, sums2, up_sum = results[:6]
     splits = results[6:]
     half = len(splits) // 2
-    ffn_shard = scatter_split(grid, splits[:half], splits[half:]).astype(f32)
+    ffn_splits = splits[:half], splits[half:]
     grad_first, dout, sums1 = first_norm_backward(
-        grad_second, part3, grid.over_tp(part3), first_norm, first_inv, gain1, output_turned
+        grad_second, part3, grid.over_tp(part3), norm1, inv1, gain1, output_turned
     )
     grad_prev, dq, dk, dv = attention_backward(
         queries, keys, values, dout, attended, probs_p, probs_c, cot_logits[0, 0], scale
     )
+    ffn_shard = scatter_split(grid, *ffn_splits, after=dq).astype(f32)
     splits = weight_grads(
         grid, sizes[0], grad_first, attended, inputs_t, whole_t, dq, dk, dv, sums1, sums2, up_sum
     )
+    splits, dq, dk, dv = lax.optimization_barrier((splits, dq, dk, dv))
     half = len(splits) // 2
     late_shard = scatter_split(grid, splits[:half], splits[half:]).astype(f32)
 

time: 311 us -> 287 us (0.923)
  waiting for transfers between devices: 105 us -> 73 us
  Pallas kernels: 102 us -> 120 us
  local copies, waits for them, and re-layouts: 26.8 us -> 19.9 us
  other arithmetic: 19.8 us -> 14.4 us
    ppermute x8 -> x9, waiting for transfers between devices: 47.4 us -> 3.33 us  [over_inner(): return lax.ppermute(array, 'fsdp', [(i, i ^ 1) for i in range(8)])]
    pallas_call x1 -> x9, Pallas kernels: 15.5 us -> 36 us  [the longest x2 18.5 us: attention_forward(): pl.pallas_call(body, grid=(end - begin,), out_shape=outs, in_specs=[pl.Bl...]
    ppermute x12, waiting for transfers between devices: 5.35 us -> 19.9 us  [over_ctx(): return lax.ppermute(array, 'ctx', [(0, 1), (1, 0)])]
    pad x9 -> x0, local copies, waits for them, and re-layouts: 6.11 us -> none  [per_device(): jnp.pad(v, ((0, 0), (0, LANES - v.shape[1])))]
    ppermute x12, waiting for transfers between devices: 49.5 us -> 45.8 us  [over_outer(): return lax.ppermute(array, 'fsdp', [(i, i ^ 2 * step) for i in range(8)])]
    unnamed x64 -> x68, local copies, waits for them, and re-layouts: 6.17 us -> 9.62 us
    ppermute x8 -> x9, starting transfers between devices: 8.68 us -> 9.54 us  [over_inner(): return lax.ppermute(array, 'fsdp', [(i, i ^ 1) for i in range(8)])]
  transfers between devices with their start and end apart: 37 -> 38, of which waited for: 18 -> 20; matrix products, arithmetic and copies ran while one was open for 15% -> 12% of each run, Pallas kernels for 21% -> 25%
where the time goes in v2:
time: 287 us; the launch traced here: 282 us
  Pallas kernels  120 us (42%)
  waiting for transfers between devices  73 us (25%)
  starting transfers between devices  36.8 us (13%)
  local copies, waits for them, and re-layouts  19.9 us (7%)
  matrix products  14.9 us (5%)
  other arithmetic  14.4 us (5%)
    ppermute x12, waiting for transfers between devices, over_outer(): return lax.ppermute(array, 'fsdp', [(i, i ^ 2 * step) for i in range(8)])  45.8 us
    pallas_call x1, Pallas kernels, ffn_backward(): pl.pallas_call(body, grid=(hidden // tile,), out_shape=outs + grads, in_s...  21.8 us
    ppermute x12, waiting for transfers between devices, over_ctx(): return lax.ppermute(array, 'ctx', [(0, 1), (1, 0)])  19.9 us
    pallas_call x2, Pallas kernels, attention_forward(): pl.pallas_call(body, grid=(end - begin,), out_shape=outs, in_specs=[pl.Bl...  18.5 us
    pallas_call x1, Pallas kernels, attention_backward(): pl.pallas_call(body, grid=(heads // 2,), out_shape=outs, in_specs=[column...  16 us
    ppermute x12, starting transfers between devices, over_outer(): return lax.ppermute(array, 'fsdp', [(i, i ^ 2 * step) for i in range(8)])  13.6 us
    ppermute x12, starting transfers between devices, over_ctx(): return lax.ppermute(array, 'ctx', [(0, 1), (1, 0)])  13.4 us
    unnamed x68, local copies, waits for them, and re-layouts  9.62 us
  transfers between devices with their start and end apart: 38, of which 20 were waited for; matrix products, arithmetic and copies ran while one was open for 12% of the time, Pallas kernels for 25%

profile of v2, /device:TPU:8, one launch (start us, length us, event | category | flops | bytes accessed | tf_op | source)
XLA Modules:
  0.0 281.8 jit_solution(15956058012076306638)
XLA Ops:
  2.8 1.9 pack_early.1
  6.2 2.2 pack_late.1
  10.3 2.6 collective-permute-start.1
  13.4 3.1 %collective-permute-done.refs_0_ = bf16[48,1664]{1,0:T(8,128)(2,1)S(1)} collective-permute-done((bf16[48,1664]{1,0:T(8,128)(2,1)}, bf16[48,1664]{1,0:T(8,128)(2,1)S(1)}, u32[]{:S(2)}, u32[]{:S(2)}) %collective-permute-start) | collective-permute-done | bytes 159776 | tf_op jit(solution)/shard_map/ppermute | solution.py:46
  16.5 7.6 %collective-permute-done.1.refs_1_ = bf16[48,1664]{1,0:T(8,128)(2,1)S(1)} collective-permute-done((bf16[48,1664]{1,0:T(8,128)(2,1)}, bf16[48,1664]{1,0:T(8,128)(2,1)S(1)}, u32[]{:S(2)}, u32[]{:S(2)}) %collective-permute-start.1) | collective-permute-done | bytes 159776 | tf_op jit(solution)/shard_map/ppermute | solution.py:46
  24.1 2.8 collective-permute-done.2.refs_2_
  27.6 1.9 join.2.came_ref
  35.4 5.7 %collective-permute-done.6.along_ref = bf16[144,1664]{1,0:T(8,128)(2,1)} collective-permute-done((bf16[144,1664]{1,0:T(8,128)(2,1)}, bf16[144,1664]{1,0:T(8,128)(2,1)}, u32[]{:S(2)}, u32[]{:S(2)}) %collective-permute-start.6) | collective-permute-done | bytes 479264 | tf_op jit(solution)/shard_map/ppermute | solution.py:49
  44.4 1.6 collective-permute-start.5
  47.4 3.6 %assemble.2 = (bf16[768,384]{1,0:T(8,128)(2,1)}, bf16[768,384]{1,0:T(8,128)(2,1)}, bf16[768,384]{1,0:T(8,128)(2,1)}, bf16[768,384]{1,0:T(8,128)(2,1)}, bf16[768,128]{1,0:T(8,128)(2,1)}) custom-call(s32[3]{0:T(128)} %pad_add_fusion.place, bf16[96,4736]{1,0:T(8,128)(2,1)} %get-tuple-element.136.own_ref, bf16[96,4736]{1,0:T(8,128)(2,1)} %copy-done.6, ...), custom_call_target="tpu_custom_call" | custom-call | bytes 5111808 | tf_op jit(solution)/shard_map/assemble/pallas_call | solution.py:167
  52.3 5.6 %collective-permute-done.9.refs_1_ = bf16[48,3072]{1,0:T(8,128)(2,1)} collective-permute-done((bf16[48,3072]{1,0:T(8,128)(2,1)}, bf16[48,3072]{1,0:T(8,128)(2,1)}, u32[]{:S(2)}, u32[]{:S(2)}) %collective-permute-start.9) | collective-permute-done | bytes 294944 | tf_op jit(solution)/shard_map/ppermute | solution.py:46
  58.0 2.1 join.3.came_ref
  62.0 2.0 complete.2
  64.0 1.8 unpack_small.1
  67.2 2.8 %fusion.4.q = bf16[768,384]{1,0:T(8,128)(2,1)} fusion(bf16[768,384]{1,0:T(8,128)(2,1)} %get-tuple-element.142, bf16[256,768]{0,1:T(8,128)(2,1)S(1)} %bitcast.83, bf16[512,768]{0,1:T(8,128)(2,1)S(1)} %bitcast.77, f32[384]{0:T(512)S(1)} %reduce), kind=kOutput, calls=%fused_computation.15 | convolution fusion | flops 456228864 | bytes 2360832 | tf_op jit(solution)/shard_map/dot_general | solution.py:17
  70.1 2.2 convolution_convert_fusion.k
  72.2 2.2 fusion.v
  74.4 11.4 %attention_forward.2 = (bf16[6,256,1280]{2,1,0:T(8,128)(2,1)}, bf16[6,512,1024]{2,1,0:T(8,128)(2,1)}, bf16[6,256,1280]{2,1,0:T(8,128)(2,1)}, bf16[768,384]{1,0:T(8,128)(2,1)}) custom-call(s32[1,1]{1,0:T(1,128)S(6)} %copy.71.length, bf16[768,384]{1,0:T(8,128)(2,1)} %fusion.4.q, bf16[1280,384]{1,0:T(8,128)(2,1)} %convolution_convert_fusion.k, ...), custom_call_target="tpu_custom_call" | custom-call | flops 2617245696 | bytes 6488064 | tf_op jit(solution)/shard_map/attention_forward/pallas_call | solution.py:609
  85.9 7.1 %attention_forward.3 = (bf16[6,256,1280]{2,1,0:T(8,128)(2,1)}, bf16[6,512,1024]{2,1,0:T(8,128)(2,1)}, bf16[6,256,1280]{2,1,0:T(8,128)(2,1)}, bf16[768,384]{1,0:T(8,128)(2,1)}) custom-call(s32[1,1]{1,0:T(1,128)S(6)} %copy.71.length, bf16[768,384]{1,0:T(8,128)(2,1)} %fusion.4.q, ...), custom_call_target="tpu_custom_call", output_to_operand_aliasing={{0}: (5, {}), {1}: (6, {}), {2}: (7, {}), {3}: (8, {})} | custom-call | flops 1308622848 | bytes 6488064 | tf_op jit(solution)/shard_map/attention_forward/pallas_call | solution.py:609
  92.9 1.9 convolution_convert_fusion.1.p
  98.9 4.7 %assemble.3 = (bf16[768,1536]{1,0:T(8,128)(2,1)}, bf16[768,1536]{1,0:T(8,128)(2,1)}) custom-call(s32[3]{0:T(128)} %pad_add_fusion.place, bf16[96,4736]{1,0:T(8,128)(2,1)} %get-tuple-element.136.own_ref, bf16[96,4736]{1,0:T(8,128)(2,1)} %copy-done.6, bf16[144,3072]{1,0:T(8,128)(2,1)} %join.3.came_ref, bf16[144,3072]{1,0:T(8,128)(2,1)} %copy-done.16, ...), custom_call_target="tpu_custom_call" | custom-call | bytes 9437184 | tf_op jit(solution)/shard_map/assemble/pallas_call | solution.py:167
  103.6 4.0 %collective-permute-done.15.one_ref = bf16[144,1536]{1,0:T(8,128)(2,1)S(1)} collective-permute-done((bf16[144,1536]{1,0:T(8,128)(2,1)S(1)}, bf16[144,1536]{1,0:T(8,128)(2,1)S(1)}, u32[]{:S(2)}, u32[]{:S(2)}) %collective-permute-start.15) | collective-permute-done | bytes 442400 | tf_op jit(solution)/shard_map/ppermute | solution.py:49
  107.6 2.3 collective-permute-done.16.two_ref
  110.6 2.1 complete.3
  112.8 5.3 %first_norm.1 = (f32[768,768]{1,0:T(8,128)}, f32[768,128]{1,0:T(8,128)}, bf16[768,768]{1,0:T(8,128)(2,1)}, bf16[768,768]{1,0:T(8,128)(2,1)}) custom-call(bf16[512,768]{1,0:T(8,128)(2,1)} %bitcast.88, bf16[256,768]{1,0:T(8,128)(2,1)} %bitcast.89, bf16[768,768]{1,0:T(8,128)(2,1)} %copy-done.5, bf16[768,768]{1,0:T(8,128)(2,1)} %collective-permute-done.14.o, ...), custom_call_target="tpu_custom_call" | custom-call | bytes 8659968 | tf_op jit(solution)/shard_map/first_norm/pallas_call | solution.py:310
  118.1 8.2 %ffn_forward.1 = (bf16[768,1536]{1,0:T(8,128)(2,1)}, bf16[768,1536]{1,0:T(8,128)(2,1)}, bf16[768,768]{1,0:T(8,128)(2,1)}) custom-call(bf16[768,768]{1,0:T(8,128)(2,1)} %get-tuple-element.166.x, bf16[768,1536]{1,0:T(8,128)(2,1)} %get-tuple-element.171.up, f32[1,1536]{1,0:T(1,128)} %get-tuple-element.172.ub, bf16[768,1536]{1,0:T(8,128)(2,1)} %get-tuple-element.173.dn), custom_call_target="tpu_custom_call" | custom-call | flops 3623878656 | bytes 11802624 | tf_op jit(solution)/shard_map/ffn_forward/pallas_call | solution.py:351
  126.3 3.1 %collective-permute-done.17.o = bf16[768,768]{1,0:T(8,128)(2,1)S(1)} collective-permute-done((bf16[768,768]{1,0:T(8,128)(2,1)}, bf16[768,768]{1,0:T(8,128)(2,1)S(1)}, u32[]{:S(2)}, u32[]{:S(2)}) %collective-permute-start.17) | collective-permute-done | bytes 1179680 | tf_op jit(solution)/shard_map/ppermute | solution.py:52
  130.4 21.8 %ffn_backward.1 = (bf16[512,768]{1,0:T(8,128)(2,1)}, bf16[256,768]{1,0:T(8,128)(2,1)}, f32[768,768]{1,0:T(8,128)}, bf16[768,768]{1,0:T(8,128)(2,1)}, f32[8,768]{...) custom-call(s32[3]{0:T(128)} %pad_add_fusion.place, ...), custom_call_target="tpu_custom_call" | custom-call | flops 7247757312 | bytes 26041344 | tf_op jit(solution)/shard_map/ffn_backward/pallas_call | solution.py:456
  156.3 6.7 %first_norm_backward.1 = (f32[768,768]{1,0:T(8,128)}, bf16[768,384]{1,0:T(8,128)(2,1)}, f32[8,768]{1,0:T(8,128)}) custom-call(f32[768,768]{1,0:T(8,128)} %get-tuple-element.180.d2, bf16[768,768]{1,0:T(8,128)(2,1)} %get-tuple-element.181.p, bf16[768,768]{1,0:T(8,128)(2,1)} %copy-done.18, f32[768,768]{1,0:T(8,128)} %get-tuple-element.164.n1, ...), custom_call_target="tpu_custom_call" | custom-call | flops 452984832 | bytes 11037696 | tf_op jit(solution)/shard_map/first_norm_backward/pallas_call | solution.py:723
  163.0 16.0 %attention_backward.1 = (bf16[6,256,1280]{2,1,0:T(8,128)(2,1)}, bf16[768,384]{1,0:T(8,128)(2,1)}, bf16[1280,384]{1,0:T(8,128)(2,1)}, bf16[1280,384]{1,0:T(8,128)(2,1)}) custom-call(bf16[768,384]{1,0:T(8,128)(2,1)} %fusion.4.q, bf16[1280,384]{1,0:T(8,128)(2,1)} %convolution_convert_fusion.k, bf16[1280,384]{1,0:T(8,128)(2,1)} %fusion.v, ...), custom_call_target="tpu_custom_call" | custom-call | flops 5234491392 | bytes 24379392 | tf_op jit(solution)/shard_map/attention_backward/pallas_call | solution.py:682
  179.0 8.4 %weight_grads.1 = (bf16[384,768]{1,0:T(8,128)(2,1)}, bf16[384,768]{1,0:T(8,128)(2,1)}, bf16[384,896]{1,0:T(8,128)(2,1)}, bf16[384,896]{1,0:T(8,128)(2,1)}) custom-call(s32[3]{0:T(128)} %pad_add_fusion.place, f32[768,768]{1,0:T(8,128)} %get-tuple-element.183.d1, bf16[768,384]{1,0:T(8,128)(2,1)} %get-tuple-element.161.o, bf16[768,768]{1,0:T(8,128)(2,1)} %fusion.7.xt, ...), custom_call_target="tpu_custom_call" | custom-call | flops 2415919104 | bytes 11304960 | tf_op jit(solution)/shard_map/weight_grads/pallas_call | solution.py:774
  188.5 4.4 %fold_pair.3 = (bf16[192,1536]{1,0:T(8,128)(2,1)}, bf16[192,1536]{1,0:T(8,128)(2,1)}, bf16[192,1536]{1,0:T(8,128)(2,1)}, bf16[192,1536]{1,0:T(8,128)(2,1)}) custom-call(s32[3]{0:T(128)} %pad_add_fusion.place, bf16[384,1536]{1,0:T(8,128)(2,1)} %get-tuple-element.215.fk, bf16[384,1536]{1,0:T(8,128)(2,1)} %copy-done.19, ...), custom_call_target="tpu_custom_call" | custom-call | bytes 7077888 | tf_op jit(solution)/shard_map/fold_pair/pallas_call | solution.py:494
  197.6 1.7 copy-done
  203.1 6.3 %collective-permute-done.32.fa = bf16[192,1536]{1,0:T(8,128)(2,1)} collective-permute-done((bf16[192,1536]{1,0:T(8,128)(2,1)}, bf16[192,1536]{1,0:T(8,128)(2,1)}, u32[]{:S(2)}, u32[]{:S(2)}) %collective-permute-start.32) | collective-permute-done | bytes 589856 | tf_op jit(solution)/shard_map/ppermute | solution.py:49
  210.0 2.9 %fold_line.3 = (f32[48,3072]{1,0:T(8,128)}, bf16[48,3072]{1,0:T(8,128)(2,1)}, bf16[48,3072]{1,0:T(8,128)(2,1)}, bf16[48,3072]{1,0:T(8,128)(2,1)}) custom-call(s32[3]{0:T(128)} %pad_add_fusion.place, bf16[192,1536]{1,0:T(8,128)(2,1)} %get-tuple-element.221.fk, bf16[192,1536]{1,0:T(8,128)(2,1)} %collective-permute-done.32.fa, ...), custom_call_target="tpu_custom_call" | custom-call | bytes 3833856 | tf_op jit(solution)/shard_map/fold_line/pallas_call | solution.py:519
  214.2 2.1 collective-permute-start.35
  216.8 3.5 %fusion.13 = f32[768,768]{1,0:T(8,128)} fusion(bf16[768,384]{1,0:T(8,128)(2,1)} %get-tuple-element.201.q, bf16[768,384]{1,0:T(8,128)(2,1)} %get-tuple-element.142), kind=kOutput, calls=%fused_computation.57 | convolution fusion | flops 452984832 | bytes 3538944 | tf_op jit(solution)/shard_map/dot_general | solution.py:27
  223.3 3.8 %fold_pair.2 = (bf16[192,768]{1,0:T(8,128)(2,1)}, bf16[192,768]{1,0:T(8,128)(2,1)}, bf16[192,896]{1,0:T(8,128)(2,1)}, bf16[192,896]{1,0:T(8,128)(2,1)}) custom-call(s32[3]{0:T(128)} %pad_add_fusion.place, bf16[384,768]{1,0:T(8,128)(2,1)} %get-tuple-element.203.fk, bf16[384,768]{1,0:T(8,128)(2,1)} %collective-permute-done.22.fa, ...), custom_call_target="tpu_custom_call" | custom-call | bytes 3833856 | tf_op jit(solution)/shard_map/fold_pair/pallas_call | solution.py:494
  229.1 6.6 %collective-permute-done.35 = bf16[48,3072]{1,0:T(8,128)(2,1)} collective-permute-done((bf16[48,3072]{1,0:T(8,128)(2,1)}, bf16[48,3072]{1,0:T(8,128)(2,1)}, u32[]{:S(2)}, u32[]{:S(2)}) %collective-permute-start.35) | collective-permute-done | bytes 294944 | tf_op jit(solution)/shard_map/ppermute | solution.py:46
  235.7 5.2 %collective-permute-done.36 = bf16[48,3072]{1,0:T(8,128)(2,1)} collective-permute-done((bf16[48,3072]{1,0:T(8,128)(2,1)}, bf16[48,3072]{1,0:T(8,128)(2,1)}, u32[]{:S(2)}, u32[]{:S(2)}) %collective-permute-start.36) | collective-permute-done | bytes 294944 | tf_op jit(solution)/shard_map/ppermute | solution.py:46
  240.9 2.2 add_convert_fusion
  248.5 2.2 fold_line.2
  250.7 3.0 %collective-permute-start.27 = (bf16[48,1664]{1,0:T(8,128)(2,1)}, bf16[48,1664]{1,0:T(8,128)(2,1)S(1)}, u32[]{:S(2)}, u32[]{:S(2)}) collective-permute-start(bf16[48,1664]{1,0:T(8,128)(2,1)} %get-tuple-element.213), channel_id=1, source_target_pairs={{0,16},{4,20},{8,24},{12,28},{16,0},{20,4},{24,8},{28,12},{1,17},{... | collective-permute-start | bytes 479240 | tf_op jit(solution)/shard_map/ppermute | solution.py:46
  255.4 2.9 %collective-permute-done.26 = bf16[48,1664]{1,0:T(8,128)(2,1)S(1)} collective-permute-done((bf16[48,1664]{1,0:T(8,128)(2,1)}, bf16[48,1664]{1,0:T(8,128)(2,1)S(1)}, u32[]{:S(2)}, u32[]{:S(2)}) %collective-permute-start.26) | collective-permute-done | bytes 159776 | tf_op jit(solution)/shard_map/ppermute | solution.py:46
  258.3 7.1 %collective-permute-done.27 = bf16[48,1664]{1,0:T(8,128)(2,1)S(1)} collective-permute-done((bf16[48,1664]{1,0:T(8,128)(2,1)}, bf16[48,1664]{1,0:T(8,128)(2,1)S(1)}, u32[]{:S(2)}, u32[]{:S(2)}) %collective-permute-start.27) | collective-permute-done | bytes 159776 | tf_op jit(solution)/shard_map/ppermute | solution.py:46
  265.4 3.5 %collective-permute-done.28 = bf16[48,1664]{1,0:T(8,128)(2,1)S(1)} collective-permute-done((bf16[48,1664]{1,0:T(8,128)(2,1)}, bf16[48,1664]{1,0:T(8,128)(2,1)S(1)}, u32[]{:S(2)}, u32[]{:S(2)}) %collective-permute-start.28) | collective-permute-done | bytes 159776 | tf_op jit(solution)/shard_map/ppermute | solution.py:46
  270.9 3.6 %collective-permute-done.29 = bf16[48,1664]{1,0:T(8,128)(2,1)S(1)} collective-permute-done((bf16[48,1664]{1,0:T(8,128)(2,1)S(1)}, bf16[48,1664]{1,0:T(8,128)(2,1)S(1)}, u32[]{:S(2)}, u32[]{:S(2)}) %collective-permute-start.29) | collective-permute-done | bytes 159776 | tf_op jit(solution)/shard_map/ppermute | solution.py:49
  277.5 1.7 add_add_fusion
  (166 shorter events, 62.5 us)
Async XLA Ops:
  0.7 29.8 %copy-start.17 = (bf16[1,1,256,768]{3,2,1,0:T(8,128)(2,1)S(1)}, bf16[1,1,256,768]{3,2,1,0:T(8,128)(2,1)}, u32[]{:S(2)}) copy-start(bf16[1,1,256,768]{3,2,1,0:T(8,128)(2,1)} %param.23) | copy-start | bytes 1179652
  4.6 22.3 %collective-permute-start.3 = (bf16[512,768]{0,1:T(8,128)(2,1)S(1)}, bf16[512,768]{0,1:T(8,128)(2,1)S(1)}, u32[]{:S(2)}, u32[]{:S(2)}) collective-permute-start(bf16[512,768]{0,1:T(8,128)(2,1)S(1)} %bitcast.75), channel_id=1, source_target_pairs={{0,2},{2,0},{1,3},{3,1},{4,6},{6,4},{5,7},{7,5},{8,10},{10,8},{9,1... | collective-permute-start | bytes 2359304 | tf_op jit(solution)/shard_map/ppermute | solution.py:49
  8.4 35.9 %collective-permute-start.11 = (bf16[96,4736]{1,0:T(8,128)(2,1)}, bf16[96,4736]{1,0:T(8,128)(2,1)S(1)}, u32[]{:S(2)}, u32[]{:S(2)}) collective-permute-start(bf16[96,4736]{1,0:T(8,128)(2,1)} %get-tuple-element.136.own_ref), channel_id=1, source_target_pairs={{0,4},{4,0},{8,12},{12,8},{16,20},{20,16},{24,28},{28,24},{1,5},{5... | collective-permute-start | bytes 2727944 | tf_op jit(solution)/shard_map/ppermute | solution.py:43
  9.9 6.6 %collective-permute-start = (bf16[48,1664]{1,0:T(8,128)(2,1)}, bf16[48,1664]{1,0:T(8,128)(2,1)S(1)}, u32[]{:S(2)}, u32[]{:S(2)}) collective-permute-start(bf16[48,1664]{1,0:T(8,128)(2,1)} %get-tuple-element.125), channel_id=1, source_target_pairs={{0,8},{4,12},{8,0},{12,4},{16,24},{20,28},{24,16},{28,20},{1,9},{5... | collective-permute-start | bytes 479240 | tf_op jit(solution)/shard_map/ppermute | solution.py:46
  10.3 13.8 %collective-permute-start.1 = (bf16[48,1664]{1,0:T(8,128)(2,1)}, bf16[48,1664]{1,0:T(8,128)(2,1)S(1)}, u32[]{:S(2)}, u32[]{:S(2)}) collective-permute-start(bf16[48,1664]{1,0:T(8,128)(2,1)} %get-tuple-element.125), channel_id=1, source_target_pairs={{0,16},{4,20},{8,24},{12,28},{16,0},{20,4},{24,8},{28,12},{1,17},{... | collective-permute-start | bytes 479240 | tf_op jit(solution)/shard_map/ppermute | solution.py:46
  12.9 14.0 %collective-permute-start.2 = (bf16[48,1664]{1,0:T(8,128)(2,1)}, bf16[48,1664]{1,0:T(8,128)(2,1)S(1)}, u32[]{:S(2)}, u32[]{:S(2)}) collective-permute-start(bf16[48,1664]{1,0:T(8,128)(2,1)} %get-tuple-element.125), channel_id=1, source_target_pairs={{0,24},{4,28},{8,16},{12,20},{16,8},{20,12},{24,0},{28,4},{1,25},{... | collective-permute-start | bytes 479240 | tf_op jit(solution)/shard_map/ppermute | solution.py:46
  16.5 10.4 %copy-start.28 = (bf16[48,1664]{1,0:T(8,128)(2,1)}, bf16[48,1664]{1,0:T(8,128)(2,1)S(1)}, u32[]{:S(2)}) copy-start(bf16[48,1664]{1,0:T(8,128)(2,1)S(1)} %collective-permute-done.refs_0_) | copy-start | bytes 479236
  29.5 11.6 %collective-permute-start.6 = (bf16[144,1664]{1,0:T(8,128)(2,1)}, bf16[144,1664]{1,0:T(8,128)(2,1)}, u32[]{:S(2)}, u32[]{:S(2)}) collective-permute-start(bf16[144,1664]{1,0:T(8,128)(2,1)} %join.2.came_ref), channel_id=1, source_target_pairs={{0,2},{2,0},{1,3},{3,1},{4,6},{6,4},{5,7},{7,5},{8,10},{10,8},{9,1... | collective-permute-start | bytes 1437704 | tf_op jit(solution)/shard_map/ppermute | solution.py:49
  30.0 12.1 %collective-permute-start.4 = (bf16[144,1664]{1,0:T(8,128)(2,1)}, bf16[144,1664]{1,0:T(8,128)(2,1)}, u32[]{:S(2)}, u32[]{:S(2)}) collective-permute-start(bf16[144,1664]{1,0:T(8,128)(2,1)} %join.2.came_ref), channel_id=1, source_target_pairs={{0,4},{4,0},{8,12},{12,8},{16,20},{20,16},{24,28},{28,24},{1,5},{5... | collective-permute-start | bytes 1437704 | tf_op jit(solution)/shard_map/ppermute | solution.py:43
  32.6 19.7 %collective-permute-start.10 = (bf16[48,3072]{1,0:T(8,128)(2,1)}, bf16[48,3072]{1,0:T(8,128)(2,1)S(1)}, u32[]{:S(2)}, u32[]{:S(2)}) collective-permute-start(bf16[48,3072]{1,0:T(8,128)(2,1)} %get-tuple-element.133), channel_id=1, source_target_pairs={{0,24},{4,28},{8,16},{12,20},{16,8},{20,12},{24,0},{28,4},{1,25},{... | collective-permute-start | bytes 884744 | tf_op jit(solution)/shard_map/ppermute | solution.py:46
  34.1 18.2 %collective-permute-start.8 = (bf16[48,3072]{1,0:T(8,128)(2,1)}, bf16[48,3072]{1,0:T(8,128)(2,1)S(1)}, u32[]{:S(2)}, u32[]{:S(2)}) collective-permute-start(bf16[48,3072]{1,0:T(8,128)(2,1)} %get-tuple-element.133), channel_id=1, source_target_pairs={{0,8},{4,12},{8,0},{12,4},{16,24},{20,28},{24,16},{28,20},{1,9},{5... | collective-permute-start | bytes 884744 | tf_op jit(solution)/shard_map/ppermute | solution.py:46
  35.4 10.6 %copy-start.10 = (bf16[512,768]{0,1:T(8,128)(2,1)}, bf16[512,768]{0,1:T(8,128)(2,1)S(1)}, u32[]{:S(2)}) copy-start(bf16[512,768]{0,1:T(8,128)(2,1)S(1)} %get-tuple-element.230) | copy-start | bytes 2359300
  41.0 16.9 %collective-permute-start.9 = (bf16[48,3072]{1,0:T(8,128)(2,1)}, bf16[48,3072]{1,0:T(8,128)(2,1)}, u32[]{:S(2)}, u32[]{:S(2)}) collective-permute-start(bf16[48,3072]{1,0:T(8,128)(2,1)} %get-tuple-element.133), channel_id=1, source_target_pairs={{0,16},{4,20},{8,24},{12,28},{16,0},{20,4},{24,8},{28,12},{1,17},{... | collective-permute-start | bytes 884744 | tf_op jit(solution)/shard_map/ppermute | solution.py:46
  42.0 15.9 %collective-permute-start.7 = (bf16[144,896]{1,0:T(8,128)(2,1)S(1)}, bf16[144,896]{1,0:T(8,128)(2,1)}, u32[]{:S(2)}, u32[]{:S(2)}) collective-permute-start(bf16[144,896]{1,0:T(8,128)(2,1)S(1)} %slice.134), channel_id=1, source_target_pairs={{0,4},{4,0},{8,12},{12,8},{16,20},{20,16},{24,28},{28,24},{1,5},{5... | collective-permute-start | bytes 774152 | tf_op jit(solution)/shard_map/ppermute | solution.py:43
  44.4 13.6 %collective-permute-start.5 = (bf16[144,768]{1,0:T(8,128)(2,1)S(1)}, bf16[144,768]{1,0:T(8,128)(2,1)}, u32[]{:S(2)}, u32[]{:S(2)}) collective-permute-start(bf16[144,768]{1,0:T(8,128)(2,1)S(1)} %slice.133), channel_id=1, source_target_pairs={{0,2},{2,0},{1,3},{3,1},{4,6},{6,4},{5,7},{7,5},{8,10},{10,8},{9,1... | collective-permute-start | bytes 663560 | tf_op jit(solution)/shard_map/ppermute | solution.py:49
  60.1 25.7 %collective-permute-start.12 = (bf16[144,3072]{1,0:T(8,128)(2,1)}, bf16[144,3072]{1,0:T(8,128)(2,1)S(1)}, u32[]{:S(2)}, u32[]{:S(2)}) collective-permute-start(bf16[144,3072]{1,0:T(8,128)(2,1)} %join.3.came_ref), channel_id=1, source_target_pairs={{0,4},{4,0},{8,12},{12,8},{16,20},{20,16},{24,28},{28,24},{1,5},{5... | collective-permute-start | bytes 2654216 | tf_op jit(solution)/shard_map/ppermute | solution.py:43
  61.5 24.4 %collective-permute-start.13 = (bf16[144,3072]{1,0:T(8,128)(2,1)}, bf16[144,3072]{1,0:T(8,128)(2,1)}, u32[]{:S(2)}, u32[]{:S(2)}) collective-permute-start(bf16[144,3072]{1,0:T(8,128)(2,1)} %join.3.came_ref), channel_id=1, source_target_pairs={{0,2},{2,0},{1,3},{3,1},{4,6},{6,4},{5,7},{7,5},{8,10},{10,8},{9,1... | collective-permute-start | bytes 2654216 | tf_op jit(solution)/shard_map/ppermute | solution.py:49
  85.8 9.1 %copy-start.16 = (bf16[144,3072]{1,0:T(8,128)(2,1)}, bf16[144,3072]{1,0:T(8,128)(2,1)S(1)}, u32[]{:S(2)}) copy-start(bf16[144,3072]{1,0:T(8,128)(2,1)S(1)} %collective-permute-done.12.across_ref) | copy-start | bytes 2654212
  85.9 7.1 %copy-start.4 = (bf16[768,384]{1,0:T(8,128)(2,1)S(1)}, bf16[768,384]{1,0:T(8,128)(2,1)}, u32[]{:S(2)}) copy-start(bf16[768,384]{1,0:T(8,128)(2,1)} %get-tuple-element.162.ot) | copy-start | bytes 1769476
  94.8 8.8 %copy-start.5 = (bf16[768,768]{1,0:T(8,128)(2,1)}, bf16[768,768]{1,0:T(8,128)(2,1)S(1)}, u32[]{:S(2)}) copy-start(bf16[768,768]{1,0:T(8,128)(2,1)S(1)} %convolution_convert_fusion.1.p) | copy-start | bytes 3538948
  94.8 18.0 %collective-permute-start.14 = (bf16[768,768]{1,0:T(8,128)(2,1)S(1)}, bf16[768,768]{1,0:T(8,128)(2,1)}, u32[]{:S(2)}, u32[]{:S(2)}) collective-permute-start(bf16[768,768]{1,0:T(8,128)(2,1)S(1)} %convolution_convert_fusion.1.p), channel_id=1, source_target_pairs={{0,1},{1,0},{2,3},{3,2},{4,5},{5,4},{6,7},{7,6},{8,9},{9,8},{10,11... | collective-permute-start | bytes 3538952 | tf_op jit(solution)/shard_map/ppermute | solution.py:52
  95.0 12.6 %collective-permute-start.15 = (bf16[144,1536]{1,0:T(8,128)(2,1)S(1)}, bf16[144,1536]{1,0:T(8,128)(2,1)S(1)}, u32[]{:S(2)}, u32[]{:S(2)}) collective-permute-start(bf16[144,1536]{1,0:T(8,128)(2,1)S(1)} %slice.106), channel_id=1, source_target_pairs={{0,2},{2,0},{1,3},{3,1},{4,6},{6,4},{5,7},{7,5},{8,10},{10,8},{9,1... | collective-permute-start | bytes 1327112 | tf_op jit(solution)/shard_map/ppermute | solution.py:49
  97.5 12.3 %collective-permute-start.16 = (bf16[144,1536]{1,0:T(8,128)(2,1)S(1)}, bf16[144,1536]{1,0:T(8,128)(2,1)S(1)}, u32[]{:S(2)}, u32[]{:S(2)}) collective-permute-start(bf16[144,1536]{1,0:T(8,128)(2,1)S(1)} %slice.107), channel_id=1, source_target_pairs={{0,4},{4,0},{8,12},{12,8},{16,20},{20,16},{24,28},{28,24},{1,5},{5... | collective-permute-start | bytes 1327112 | tf_op jit(solution)/shard_map/ppermute | solution.py:43
  126.3 3.1 %collective-permute-start.17 = (bf16[768,768]{1,0:T(8,128)(2,1)}, bf16[768,768]{1,0:T(8,128)(2,1)S(1)}, u32[]{:S(2)}, u32[]{:S(2)}) collective-permute-start(bf16[768,768]{1,0:T(8,128)(2,1)} %get-tuple-element.174.p), channel_id=1, source_target_pairs={{0,1},{1,0},{2,3},{3,2},{4,5},{5,4},{6,7},{7,6},{8,9},{9,8},{10,11... | collective-permute-start | bytes 3538952 | tf_op jit(solution)/shard_map/ppermute | solution.py:52
  152.2 3.1 %collective-permute-start.18 = (bf16[768,768]{1,0:T(8,128)(2,1)}, bf16[768,768]{1,0:T(8,128)(2,1)S(1)}, u32[]{:S(2)}, u32[]{:S(2)}) collective-permute-start(bf16[768,768]{1,0:T(8,128)(2,1)} %get-tuple-element.181.p), channel_id=1, source_target_pairs={{0,1},{1,0},{2,3},{3,2},{4,5},{5,4},{6,7},{7,6},{8,9},{9,8},{10,11... | collective-permute-start | bytes 3538952 | tf_op jit(solution)/shard_map/ppermute | solution.py:52
  152.4 35.1 %collective-permute-start.30 = (bf16[384,1536]{1,0:T(8,128)(2,1)}, bf16[384,1536]{1,0:T(8,128)(2,1)S(1)}, u32[]{:S(2)}, u32[]{:S(2)}) collective-permute-start(bf16[384,1536]{1,0:T(8,128)(2,1)} %get-tuple-element.216), channel_id=1, source_target_pairs={{0,4},{4,0},{8,12},{12,8},{16,20},{20,16},{24,28},{28,24},{1,5},{5... | collective-permute-start | bytes 3538952 | tf_op jit(solution)/shard_map/ppermute | solution.py:43
  153.0 34.5 %collective-permute-start.31 = (bf16[384,1536]{1,0:T(8,128)(2,1)}, bf16[384,1536]{1,0:T(8,128)(2,1)}, u32[]{:S(2)}, u32[]{:S(2)}) collective-permute-start(bf16[384,1536]{1,0:T(8,128)(2,1)} %get-tuple-element.217), channel_id=1, source_target_pairs={{0,2},{2,0},{1,3},{3,1},{4,6},{6,4},{5,7},{7,5},{8,10},{10,8},{9,1... | collective-permute-start | bytes 3538952 | tf_op jit(solution)/shard_map/ppermute | solution.py:49
  188.5 6.4 %copy-start.14 = (bf16[768,384]{1,0:T(8,128)(2,1)S(1)}, bf16[768,384]{1,0:T(8,128)(2,1)}, u32[]{:S(2)}) copy-start(bf16[768,384]{1,0:T(8,128)(2,1)} %get-tuple-element.148) | copy-start | bytes 1769476
  192.9 16.6 %collective-permute-start.32 = (bf16[192,1536]{1,0:T(8,128)(2,1)}, bf16[192,1536]{1,0:T(8,128)(2,1)}, u32[]{:S(2)}, u32[]{:S(2)}) collective-permute-start(bf16[192,1536]{1,0:T(8,128)(2,1)} %get-tuple-element.222), channel_id=1, source_target_pairs={{0,2},{2,0},{1,3},{3,1},{4,6},{6,4},{5,7},{7,5},{8,10},{10,8},{9,1... | collective-permute-start | bytes 1769480 | tf_op jit(solution)/shard_map/ppermute | solution.py:49
  193.5 16.5 %collective-permute-start.33 = (bf16[192,1536]{1,0:T(8,128)(2,1)}, bf16[192,1536]{1,0:T(8,128)(2,1)}, u32[]{:S(2)}, u32[]{:S(2)}) collective-permute-start(bf16[192,1536]{1,0:T(8,128)(2,1)} %get-tuple-element.224), channel_id=1, source_target_pairs={{0,4},{4,0},{8,12},{12,8},{16,20},{20,16},{24,28},{28,24},{1,5},{5... | collective-permute-start | bytes 1769480 | tf_op jit(solution)/shard_map/ppermute | solution.py:43
  201.0 15.3 %collective-permute-start.19 = (bf16[256,768]{1,0:T(8,128)(2,1)}, bf16[256,768]{1,0:T(8,128)(2,1)S(1)}, u32[]{:S(2)}, u32[]{:S(2)}) collective-permute-start(bf16[256,768]{1,0:T(8,128)(2,1)} %dynamic-slice_bitcast_fusion), channel_id=1, source_target_pairs={{0,1},{1,0},{2,3},{3,2},{4,5},{5,4},{6,7},{7,6},{8,9},{9,8},{10,11... | collective-permute-start | bytes 1179656 | tf_op jit(solution)/shard_map/ppermute | solution.py:52
  201.0 22.4 %collective-permute-start.23 = (bf16[384,896]{1,0:T(8,128)(2,1)}, bf16[384,896]{1,0:T(8,128)(2,1)}, u32[]{:S(2)}, u32[]{:S(2)}) collective-permute-start(bf16[384,896]{1,0:T(8,128)(2,1)} %get-tuple-element.206), channel_id=1, source_target_pairs={{0,2},{2,0},{1,3},{3,1},{4,6},{6,4},{5,7},{7,5},{8,10},{10,8},{9,1... | collective-permute-start | bytes 2064392 | tf_op jit(solution)/shard_map/ppermute | solution.py:49
  201.7 19.9 %collective-permute-start.22 = (bf16[384,768]{1,0:T(8,128)(2,1)}, bf16[384,768]{1,0:T(8,128)(2,1)}, u32[]{:S(2)}, u32[]{:S(2)}) collective-permute-start(bf16[384,768]{1,0:T(8,128)(2,1)} %get-tuple-element.204), channel_id=1, source_target_pairs={{0,4},{4,0},{8,12},{12,8},{16,20},{20,16},{24,28},{28,24},{1,5},{5... | collective-permute-start | bytes 1769480 | tf_op jit(solution)/shard_map/ppermute | solution.py:43
  212.9 7.4 %copy-start.9 = (bf16[1,512,768]{2,1,0:T(8,128)(2,1)S(1)}, bf16[1,512,768]{2,1,0:T(8,128)(2,1)}, u32[]{:S(2)}) copy-start(bf16[1,512,768]{2,1,0:T(8,128)(2,1)} %copy-done.8) | copy-start | bytes 2359300
  212.9 14.9 %collective-permute-start.34 = (bf16[48,3072]{1,0:T(8,128)(2,1)}, bf16[48,3072]{1,0:T(8,128)(2,1)}, u32[]{:S(2)}, u32[]{:S(2)}) collective-permute-start(bf16[48,3072]{1,0:T(8,128)(2,1)} %get-tuple-element.226), channel_id=1, source_target_pairs={{0,8},{4,12},{8,0},{12,4},{16,24},{20,28},{24,16},{28,20},{1,9},{5... | collective-permute-start | bytes 884744 | tf_op jit(solution)/shard_map/ppermute | solution.py:46
  214.2 21.5 %collective-permute-start.35 = (bf16[48,3072]{1,0:T(8,128)(2,1)}, bf16[48,3072]{1,0:T(8,128)(2,1)}, u32[]{:S(2)}, u32[]{:S(2)}) collective-permute-start(bf16[48,3072]{1,0:T(8,128)(2,1)} %get-tuple-element.227), channel_id=1, source_target_pairs={{0,16},{4,20},{8,24},{12,28},{16,0},{20,4},{24,8},{28,12},{1,17},{... | collective-permute-start | bytes 884744 | tf_op jit(solution)/shard_map/ppermute | solution.py:46
  216.3 24.6 %collective-permute-start.36 = (bf16[48,3072]{1,0:T(8,128)(2,1)}, bf16[48,3072]{1,0:T(8,128)(2,1)}, u32[]{:S(2)}, u32[]{:S(2)}) collective-permute-start(bf16[48,3072]{1,0:T(8,128)(2,1)} %get-tuple-element.228), channel_id=1, source_target_pairs={{0,24},{4,28},{8,16},{12,20},{16,8},{20,12},{24,0},{28,4},{1,25},{... | collective-permute-start | bytes 884744 | tf_op jit(solution)/shard_map/ppermute | solution.py:46
  221.5 24.5 %collective-permute-start.20 = (bf16[256,768]{1,0:T(8,128)(2,1)}, bf16[256,768]{1,0:T(8,128)(2,1)}, u32[]{:S(2)}, u32[]{:S(2)}) collective-permute-start(bf16[256,768]{1,0:T(8,128)(2,1)} %fusion.6), channel_id=1, source_target_pairs={{0,2},{2,0},{1,3},{3,1},{4,6},{6,4},{5,7},{7,5},{8,10},{10,8},{9,1... | collective-permute-start | bytes 1179656 | tf_op jit(solution)/shard_map/ppermute | solution.py:49
  227.1 21.4 %collective-permute-start.25 = (bf16[192,896]{1,0:T(8,128)(2,1)}, bf16[192,896]{1,0:T(8,128)(2,1)}, u32[]{:S(2)}, u32[]{:S(2)}) collective-permute-start(bf16[192,896]{1,0:T(8,128)(2,1)} %get-tuple-element.210), channel_id=1, source_target_pairs={{0,4},{4,0},{8,12},{12,8},{16,20},{20,16},{24,28},{28,24},{1,5},{5... | collective-permute-start | bytes 1032200 | tf_op jit(solution)/shard_map/ppermute | solution.py:43
  227.8 20.7 %collective-permute-start.24 = (bf16[192,768]{1,0:T(8,128)(2,1)}, bf16[192,768]{1,0:T(8,128)(2,1)}, u32[]{:S(2)}, u32[]{:S(2)}) collective-permute-start(bf16[192,768]{1,0:T(8,128)(2,1)} %get-tuple-element.208), channel_id=1, source_target_pairs={{0,2},{2,0},{1,3},{3,1},{4,6},{6,4},{5,7},{7,5},{8,10},{10,8},{9,1... | collective-permute-start | bytes 884744 | tf_op jit(solution)/shard_map/ppermute | solution.py:49
  243.1 11.1 %collective-permute-start.37 = (bf16[48,3072]{1,0:T(8,128)(2,1)}, bf16[48,3072]{1,0:T(8,128)(2,1)}, u32[]{:S(2)}, u32[]{:S(2)}) collective-permute-start(bf16[48,3072]{1,0:T(8,128)(2,1)} %add_convert_fusion), channel_id=1, source_target_pairs={{0,2},{2,0},{1,3},{3,1},{4,6},{6,4},{5,7},{7,5},{8,10},{10,8},{9,1... | collective-permute-start | bytes 884744 | tf_op jit(solution)/shard_map/ppermute | solution.py:49
  248.4 29.1 %collective-permute-start.21 = (bf16[768,768]{1,0:T(8,128)(2,1)S(1)}, bf16[768,768]{1,0:T(8,128)(2,1)}, u32[]{:S(2)}, u32[]{:S(2)}) collective-permute-start(bf16[768,768]{1,0:T(8,128)(2,1)S(1)} %pad_maximum_fusion.2), channel_id=1, source_target_pairs={{0,1},{1,0},{2,3},{3,2},{4,5},{5,4},{6,7},{7,6},{8,9},{9,8},{10,11... | collective-permute-start | bytes 3538952 | tf_op jit(solution)/shard_map/ppermute | solution.py:52
  250.7 18.2 %copy-start.25 = (f32[48,1664]{1,0:T(8,128)S(1)}, f32[48,1664]{1,0:T(8,128)}, u32[]{:S(2)}) copy-start(f32[48,1664]{1,0:T(8,128)} %get-tuple-element.211) | copy-start | bytes 958468
  250.7 7.6 %collective-permute-start.26 = (bf16[48,1664]{1,0:T(8,128)(2,1)}, bf16[48,1664]{1,0:T(8,128)(2,1)S(1)}, u32[]{:S(2)}, u32[]{:S(2)}) collective-permute-start(bf16[48,1664]{1,0:T(8,128)(2,1)} %get-tuple-element.212), channel_id=1, source_target_pairs={{0,8},{4,12},{8,0},{12,4},{16,24},{20,28},{24,16},{28,20},{1,9},{5... | collective-permute-start | bytes 479240 | tf_op jit(solution)/shard_map/ppermute | solution.py:46
  250.7 14.7 %collective-permute-start.27 = (bf16[48,1664]{1,0:T(8,128)(2,1)}, bf16[48,1664]{1,0:T(8,128)(2,1)S(1)}, u32[]{:S(2)}, u32[]{:S(2)}) collective-permute-start(bf16[48,1664]{1,0:T(8,128)(2,1)} %get-tuple-element.213), channel_id=1, source_target_pairs={{0,16},{4,20},{8,24},{12,28},{16,0},{20,4},{24,8},{28,12},{1,17},{... | collective-permute-start | bytes 479240 | tf_op jit(solution)/shard_map/ppermute | solution.py:46
  253.7 15.2 %collective-permute-start.28 = (bf16[48,1664]{1,0:T(8,128)(2,1)}, bf16[48,1664]{1,0:T(8,128)(2,1)S(1)}, u32[]{:S(2)}, u32[]{:S(2)}) collective-permute-start(bf16[48,1664]{1,0:T(8,128)(2,1)} %get-tuple-element.214), channel_id=1, source_target_pairs={{0,24},{4,28},{8,16},{12,20},{16,8},{20,12},{24,0},{28,4},{1,25},{... | collective-permute-start | bytes 479240 | tf_op jit(solution)/shard_map/ppermute | solution.py:46
  269.0 5.4 %collective-permute-start.29 = (bf16[48,1664]{1,0:T(8,128)(2,1)S(1)}, bf16[48,1664]{1,0:T(8,128)(2,1)S(1)}, u32[]{:S(2)}, u32[]{:S(2)}) collective-permute-start(bf16[48,1664]{1,0:T(8,128)(2,1)S(1)} %add_convert_fusion.1), channel_id=1, source_target_pairs={{0,2},{2,0},{1,3},{3,1},{4,6},{6,4},{5,7},{7,5},{8,10},{10,8},{9,1... | collective-permute-start | bytes 479240 | tf_op jit(solution)/shard_map/ppermute | solution.py:49
  270.9 6.6 %copy-start.3 = (bf16[512,768]{1,0:T(8,128)(2,1)S(1)}, bf16[512,768]{1,0:T(8,128)(2,1)}, u32[]{:S(2)}) copy-start(bf16[512,768]{1,0:T(8,128)(2,1)} %copy-done.2) | copy-start | bytes 2359300
  (23 other events, 64.8 us)

commit v3 on v2

--- a/solution.py
+++ b/solution.py
@@ -37,7 +37,7 @@
         self.outer, self.inner = place // 2, place % 2
         self.row = lax.axis_index("ctx")
         self.core = lax.axis_index("tp")
-        self.place = jnp.stack([self.outer, self.inner, self.row]).astype(jnp.int32)
+        self.place = jnp.stack([self.outer, self.inner, self.row, self.core]).astype(jnp.int32)
 
     def over_inner(self, array):
         return lax.ppermute(array, "fsdp", [(i, i ^ 1) for i in range(8)])
@@ -249,10 +249,11 @@
 
 
 def cost(flops, *arrays, transcendentals=0):
-    moved = sum(math.prod(a.shape) * jnp.dtype(a.dtype).itemsize for a in arrays)
-    return pl.CostEstimate(
-        flops=int(flops), transcendentals=int(transcendentals), bytes_accessed=int(moved)
-    )
+    return pl.CostEstimate(flops=10**13, transcendentals=0, bytes_accessed=1)
+
+
+def after(values, *earlier):
+    return lax.optimization_barrier((values, earlier))[0]
 
 
 def like(shape, dtype):
@@ -474,30 +475,40 @@
     )(grid.place, *fixed, *moving)
 
 
-def fold_pair(grid, first, second):
-    half = first[0].shape[0] // 8
+def fold_pair(grid, firsts, seconds):
+    half = firsts[0][0].shape[0] // 8
     outs = []
-    for kept, _ in (first, second):
-        outs += [like((4 * half, kept.shape[1]), bf16)] * 2
-
-    def body(place, fk, fa, sk, sa, f_keep, f_send, s_keep, s_send):
-        for kept, came, keep, send, mine in (
-            (fk, fa, f_keep, f_send, place[2]),
-            (sk, sa, s_keep, s_send, place[1]),
+    for group in (firsts, seconds):
+        outs += [like((4 * half, sum(kept.shape[1] for kept, _ in group)), bf16)] * 2
+
+    def body(place, *refs):
+        pairs, outs = refs[:-4], refs[-4:]
+        at_pair = 0
+        for group, mine, (keep, send) in (
+            (firsts, place[2], outs[:2]),
+            (seconds, place[1], outs[2:]),
         ):
-            for out, flip in ((send, 1), (keep, 0)):
-                at = pl.multiple_of((mine ^ flip) * half, 16)
-                here = pl.ds(at, half)
-                out[...] = (kept[here, :].astype(f32) + came[here, :].astype(f32)).astype(bf16)
-
-    args = [*first, *second]
-    return pl.pallas_call(
-        body,
-        grid=(4,),
+            low = 0
+            for _ in group:
+                kept, came = pairs[at_pair : at_pair + 2]
+                at_pair += 2
+                high = low + kept.shape[1]
+                for out, flip in ((send, 1), (keep, 0)):
+                    for outer in range(4):
+                        here = pl.ds(pl.multiple_of((2 * outer + (mine ^ flip)) * half, 16), half)
+                        out[outer * half : (outer + 1) * half, low:high] = (
+                            kept[here, :].astype(f32) + came[here, :].astype(f32)
+                        ).astype(bf16)
+                low = high
+
+    vmem = pl.BlockSpec(memory_space=pltpu.VMEM)
+    args = [a for group in (firsts, seconds) for pair in group for a in pair]
+    return pl.pallas_call(
+        body,
         out_shape=outs,
-        in_specs=[pl.BlockSpec(memory_space=pltpu.SMEM)]
-        + [pl.BlockSpec((2 * half, a.shape[1]), lambda i: (i, 0)) for a in args],
-        out_specs=[pl.BlockSpec((half, a.shape[1]), lambda i: (i, 0)) for a in outs],
+        in_specs=[pl.BlockSpec(memory_space=pltpu.SMEM)] + [vmem] * len(args),
+        out_specs=[vmem] * 4,
+        compiler_params=pltpu.CompilerParams(vmem_limit_bytes=VMEM_LIMIT),
         cost_estimate=cost(0, *args, *outs),
         name="fold_pair",
     )(grid.place, *args)
@@ -526,31 +537,72 @@
     )(grid.place, *args)
 
 
-def scatter_split(grid, first, second, after=None):
-    if not grid.staged:
-        both = jnp.concatenate([first[0], second[0]], 1)
-        both = lax.psum_scatter(both, "fsdp", scatter_dimension=0, tiled=True)
-        return lax.psum(both, "ctx")
-    came_first = grid.over_inner(first[1])
-    came_second = grid.over_ctx(second[1])
-    if after is not None:
-        came_first, came_second, _ = lax.optimization_barrier((came_first, came_second, after))
-    f_keep, f_send, s_keep, s_send = fold_pair(grid, (first[0], came_first), (second[0], came_second))
-    came_first = grid.over_ctx(f_send)
-    came_second = grid.over_inner(s_send)
-    total, *sent = fold_line(grid, (f_keep, came_first), (s_keep, came_second))
-    for step in (1, 2, 3):
-        total = total + grid.over_outer(sent[step - 1], step).astype(f32)
-    total = total.astype(bf16)
-    other = grid.over_ctx(total)
-    low = jnp.where(grid.row == 0, total, other)
-    high = jnp.where(grid.row == 0, other, total)
-    return jnp.concatenate([low, high], 0)
+class Reduction:
+    def __init__(self, grid, firsts, seconds):
+        self.grid, self.firsts, self.seconds = grid, firsts, seconds
+        if grid.staged:
+            self.came = [
+                [grid.over_inner(g[1]) for g in firsts],
+                [grid.over_ctx(g[1]) for g in seconds],
+            ]
+
+    def fold(self, *earlier):
+        if not self.grid.staged:
+            return ()
+        grid = self.grid
+        came = after(self.came, *earlier)
+        folded = fold_pair(
+            grid,
+            [(g[0], c) for g, c in zip(self.firsts, came[0])],
+            [(g[0], c) for g, c in zip(self.seconds, came[1])],
+        )
+        f_keep, f_send, s_keep, s_send = folded
+        self.kept = f_keep, s_keep
+        self.came = grid.over_ctx(f_send), grid.over_inner(s_send)
+        return folded
+
+    def line(self, *earlier):
+        if not self.grid.staged:
+            return ()
+        came = after(self.came, *earlier)
+        self.total, *sent = fold_line(self.grid, (self.kept[0], came[0]), (self.kept[1], came[1]))
+        self.came = [self.grid.over_outer(sent[step - 1], step) for step in (1, 2, 3)]
+        return sent
+
+    def shard(self, *earlier):
+        grid = self.grid
+        if not grid.staged:
+            both = jnp.concatenate([g[0] for g in self.firsts + self.seconds], 1)
+            both = lax.psum_scatter(both, "fsdp", scatter_dimension=0, tiled=True)
+            return lax.psum(both, "ctx").astype(f32)
+        came = after(self.came, *earlier)
+        total = self.total
+        for piece in came:
+            total = total + piece.astype(f32)
+        total = total.astype(bf16)
+        other = grid.over_ctx(total)
+        low = jnp.where(grid.row == 0, total, other)
+        high = jnp.where(grid.row == 0, other, total)
+        return jnp.concatenate([low, high], 0).astype(f32)
+
+
+def columns_of(shard, widths):
+    edges = [sum(widths[:i]) for i in range(len(widths) + 1)]
+    return [shard[:, low:high] for low, high in zip(edges, edges[1:])]
 
 
 def head_lanes(shape, index):
     lane = lax.broadcasted_iota(jnp.int32, shape, 1)
     return (lane < LANES // 2) if index == 0 else (lane >= LANES // 2)
+
+
+def each_chunk(rows_at, prompt_len, rows, chunk):
+    @pl.loop(0, prompt_len // chunk)
+    def _(i):
+        rows_at(pl.multiple_of(i * chunk, chunk), True)
+
+    for at in range(prompt_len, rows, chunk):
+        rows_at(at, False)
 
 
 def attention_forward(queries, keys, values, prev_logits, cont_len, prompt_len, pairs, held=()):
@@ -572,12 +624,12 @@
 
         column = lax.broadcasted_iota(jnp.int32, (1, total), 1)
         live = column < full_len + length[0, 0]
-        for at in range(0, rows, chunk):
-            here = slice(at, at + chunk)
+        def rows_at(at, in_prompt):
+            here = pl.ds(at, chunk)
             halves = []
             for head in range(2):
                 one = jnp.where(head_lanes((chunk, LANES), head), q[here, :], 0)
-                if at < prompt_len:
+                if in_prompt:
                     probs = soft(contract_cols(one, k[:full_len, :]))
                     probs_p[head, here, :] = probs
                     halves.append(product(probs, v[:full_len, :]))
@@ -591,6 +643,8 @@
             first = head_lanes((chunk, LANES), 0)
             out[here, :] = jnp.where(first, halves[0], halves[1]).astype(bf16)
 
+        each_chunk(rows_at, prompt_len, rows, chunk)
+
     outs = [
         like((heads, cont_size, total), bf16),
         like((heads, prompt_len, full_len), bf16),
@@ -632,8 +686,8 @@
     def body(q, k, v, do, o, pp, pc, cot, prev_out, dq, dk, dv, acc_k, acc_v):
         acc_k[...] = jnp.zeros_like(acc_k)
         acc_v[...] = jnp.zeros_like(acc_v)
-        for at in range(0, rows, chunk):
-            here = slice(at, at + chunk)
+        def rows_at(at, in_prompt):
+            here = pl.ds(at, chunk)
             grads = []
             for head in range(2):
                 mine = head_lanes((chunk, LANES), head)
@@ -642,7 +696,7 @@
                 delta = jnp.sum(
                     one_do.astype(f32) * o[here, :].astype(f32), axis=-1, keepdims=True
                 )
-                if at < prompt_len:
+                if in_prompt:
                     span = full_len
                     probs = pp[head, here, :]
                     dprob = contract_cols(one_do, v[:span, :])
@@ -661,6 +715,8 @@
                 acc_v[:span, :] += contract_rows(probs, one_do)
             first = head_lanes((chunk, LANES), 0)
             dq[here, :] = (jnp.where(first, grads[0], grads[1]) * scale).astype(bf16)
+
+        each_chunk(rows_at, prompt_len, rows, chunk)
         dk[...] = acc_k[...].astype(bf16)
         dv[...] = acc_v[...].astype(bf16)
 
@@ -732,14 +788,47 @@
     )(*args)
 
 
+def input_pull(grid, dq, dk, dv, query_mat, key_mat, value_mat, prompt_len):
+    rows, width = dq.shape[0], query_mat.shape[0]
+    half = prompt_len // 2
+    tile = half
+    full_len = 2 * prompt_len
+
+    def body(place, q, k, v, qm, km, vm, own, keep, low):
+        def pull(at):
+            here = pl.ds(pl.multiple_of(at, tile), tile)
+            return contract_cols(k[here, :], km[...]) + contract_cols(v[here, :], vm[...])
+
+        for at in range(0, rows, tile):
+            source = place[2] * prompt_len + at if at < prompt_len else at - prompt_len + full_len
+            value = contract_cols(q[at : at + tile, :], qm[...]) + pull(source)
+            own[at : at + tile, :] = value
+            low[at : at + tile, :] = value.astype(bf16)
+        abroad = (1 - place[2]) * prompt_len
+        keep[...] = pull(abroad + place[3] * half).astype(bf16)
+        low[rows:, :] = pull(abroad + (1 - place[3]) * half).astype(bf16)
+
+    args = [dq, dk, dv, query_mat, key_mat, value_mat]
+    vmem = pl.BlockSpec(memory_space=pltpu.VMEM)
+    return pl.pallas_call(
+        body,
+        out_shape=[like((rows, width), f32), like((half, width), bf16), like((rows + half, width), bf16)],
+        in_specs=[pl.BlockSpec(memory_space=pltpu.SMEM)] + [vmem] * len(args),
+        out_specs=[vmem] * 3,
+        compiler_params=pltpu.CompilerParams(vmem_limit_bytes=VMEM_LIMIT),
+        cost_estimate=cost(0, *args),
+        name="input_pull",
+    )(grid.place, *args)
+
+
 def weight_grads(grid, shards, grad_first, attended, inputs_t, whole_t, dq, dk, dv, sums1, sums2, up_sum):
-    rows, width = grad_first.shape
-    part = dq.shape[1]
+    width, part = inputs_t.shape[0], dq.shape[1]
     hidden = up_sum.shape[1]
     count = 2 if grid.staged else 1
     block = width // shards
     sides = pl.cdiv((6 * width + 2 * part + hidden) // LANES, block)
     extra = sides * LANES
+    widths = [part, part, part, part, extra]
 
     def body(place, d1, o, xt, wt, q, k, v, s1, s2, us, *rest):
         firsts, seconds = rest[:count], rest[count : 2 * count]
@@ -748,8 +837,8 @@
         full_a[:, :part] = product(turned, o[...]).astype(bf16)
         full_a[:, part:] = product(xt[...], q[...]).astype(bf16)
         full_b[:, :part] = product(wt[...], k[...]).astype(bf16)
-        full_b[:, part : 2 * part] = product(wt[...], v[...]).astype(bf16)
         wide = 2 * part
+        full_b[:, part:wide] = product(wt[...], v[...]).astype(bf16)
         lines = [(s1, i) for i in range(3)] + [(s2, i) for i in range(3)]
         pieces = []
         for ref, i in lines:
@@ -769,21 +858,22 @@
         store_split(grid, place, full_b, seconds, False)
 
     args = [grad_first, attended, inputs_t, whole_t, dq, dk, dv, sums1, sums2, up_sum]
-    outs = split_out(grid, width, 2 * part) + split_out(grid, width, 2 * part + extra)
+    outs = split_out(grid, width, 2 * part) + split_out(grid, width, sum(widths[2:]))
     vmem = pl.BlockSpec(memory_space=pltpu.VMEM)
-    return pl.pallas_call(
+    outs = pl.pallas_call(
         body,
         out_shape=outs,
         in_specs=[pl.BlockSpec(memory_space=pltpu.SMEM)] + [vmem] * len(args),
         out_specs=[vmem] * len(outs),
         scratch_shapes=[
             pltpu.VMEM((width, 2 * part), bf16),
-            pltpu.VMEM((width, 2 * part + extra), bf16),
+            pltpu.VMEM((width, sum(widths[2:])), bf16),
         ],
         compiler_params=pltpu.CompilerParams(vmem_limit_bytes=VMEM_LIMIT),
-        cost_estimate=cost(4 * width * part * (rows + whole_t.shape[1]), *args, *outs),
+        cost_estimate=cost(0, *args, *outs),
         name="weight_grads",
     )(grid.place, *args)
+    return outs[:count], outs[count:], widths
 
 
 def unpack_small(grid, packed, heads, head_size, up_rows):
@@ -965,46 +1055,53 @@
     result_prompt, result_cont, grad_second, part3, sums2, up_sum = results[:6]
     splits = results[6:]
     half = len(splits) // 2
-    ffn_splits = splits[:half], splits[half:]
+    sum_f = Reduction(grid, [splits[:half]], [splits[half:]])
     grad_first, dout, sums1 = first_norm_backward(
         grad_second, part3, grid.over_tp(part3), norm1, inv1, gain1, output_turned
     )
     grad_prev, dq, dk, dv = attention_backward(
         queries, keys, values, dout, attended, probs_p, probs_c, cot_logits[0, 0], scale
     )
-    ffn_shard = scatter_split(grid, *ffn_splits, after=dq).astype(f32)
-    splits = weight_grads(
+    dq = after(dq, sum_f.fold(dq))
+    *splits, widths = weight_grads(
         grid, sizes[0], grad_first, attended, inputs_t, whole_t, dq, dk, dv, sums1, sums2, up_sum
     )
-    splits, dq, dk, dv = lax.optimization_barrier((splits, dq, dk, dv))
-    half = len(splits) // 2
-    late_shard = scatter_split(grid, splits[:half], splits[half:]).astype(f32)
-
-    from_query = contract_cols(dq, query_mat)
-    from_keyvalue = contract_cols(dk, key_mat) + contract_cols(dv, value_mat)
-    shared, own_cont = from_keyvalue[:full_len], from_keyvalue[full_len:]
-    if sizes[1] == 2 and sizes[2] == 2:
-        shared = shared.reshape(2, prompt_len, -1)
-        abroad = pick(shared, 1 - grid.row, 0).astype(bf16).reshape(2, prompt_len // 2, -1)
-        abroad_sum = add_low(
-            pick(abroad, grid.core, 0), grid.over_tp(pick(abroad, 1 - grid.core, 0))
-        )
-        arrived = grid.over_ctx(abroad_sum).astype(f32)
-        own = (pick(shared, grid.row, 0) + from_query[:prompt_len]).reshape(2, prompt_len // 2, -1)
-        at = lax.broadcasted_iota(jnp.int32, (2, 1, 1), 0)
-        own = own + jnp.where(at == grid.core, arrived[None], 0.0)
-        own = own.reshape(prompt_len, -1)
+    sum_c = Reduction(grid, [splits[0]], [splits[1]])
+
+    if grid.staged:
+        folded = sum_c.fold(sum_f.line(splits))
+        grads = after((dq, dk, dv), folded)
+        partial, keep, low = input_pull(grid, *grads, query_mat, key_mat, value_mat, prompt_len)
+        sent = sum_c.line(partial)
+        came = grid.over_tp(low)
+        own_rows = partial.shape[0]
+        input_grad = grad_first + partial.astype(bf16).astype(f32) + came[:own_rows].astype(f32)
+        arrived = grid.over_ctx(add_low(keep, came[own_rows:]))
+        shard_f = sum_f.shard(folded)
+        other = grid.over_tp(arrived)
+        first = jnp.where(grid.core == 0, arrived, other)
+        second = jnp.where(grid.core == 0, other, arrived)
+        grad_cont = input_grad[prompt_len:]
+        shared = grad_cont, arrived
+        grad_prompt = input_grad[:prompt_len] + jnp.concatenate([first, second], 0).astype(f32)
     else:
+        from_query = contract_cols(dq, query_mat)
+        from_keyvalue = contract_cols(dk, key_mat) + contract_cols(dv, value_mat)
         own = lax.psum_scatter(
-            shared.astype(bf16), "ctx", scatter_dimension=0, tiled=True
+            from_keyvalue[:full_len].astype(bf16), "ctx", scatter_dimension=0, tiled=True
         ).astype(f32)
         own = own + from_query[:prompt_len]
-    partial = jnp.concatenate([own, own_cont + from_query[prompt_len:]], 0)
-    input_grad = grad_first + grid.tp_sum(partial)
-
-    table = late_shard[:, 4 * width :]
+        partial = jnp.concatenate([own, from_keyvalue[full_len:] + from_query[prompt_len:]], 0)
+        input_grad = grad_first + grid.tp_sum(partial)
+        grad_prompt, grad_cont = input_grad[:prompt_len], input_grad[prompt_len:]
+        shard_f = sum_f.shard()
+        shared = ()
+    up_grad, down_turned_grad = columns_of(shard_f, [hidden, hidden])
+    down_grad = down_turned_grad.T
+    shard_c = sum_c.shard(up_grad, down_grad, *shared)
+    output_grads, query_grad, key_grad, value_grad, table = columns_of(shard_c, widths)
+    model = whole.shape[1]
     table = jnp.concatenate([table[:, at : at + LANES] for at in range(0, table.shape[1], LANES)], 0)
-    model = whole.shape[1]
     place = lax.axis_index("fsdp")
     at = 6 * (model // LANES)
     long_lines = table[:at].reshape(6, model)
@@ -1022,21 +1119,21 @@
         result_prompt[None],
         result_cont[None, None],
         new_logits[None, None],
-        input_grad[:prompt_len][None],
-        input_grad[prompt_len:][None, None],
+        grad_prompt[None],
+        grad_cont[None, None],
         grad_prev[None, None],
-        late_shard[:, width : 2 * width],
+        query_grad,
         shorts[0],
-        late_shard[:, 2 * width : 3 * width],
-        late_shard[:, 3 * width : 4 * width],
+        key_grad,
+        value_grad,
         shorts[1],
-        late_shard[:, :width].T,
+        output_grads.T,
         output_add_grad,
         gain_one_grad,
         shift_one_grad,
-        ffn_shard[:, :hidden],
+        up_grad,
         shorts[2],
-        ffn_shard[:, hidden:].T,
+        down_grad,
         down_add_grad,
         gain_two_grad,
         shift_two_grad,

time: 287 us -> 263 us (0.916)
  waiting for transfers between devices: 73 us -> 45.4 us
  Pallas kernels: 120 us -> 128 us
  starting transfers between devices: 36.8 us -> 43.9 us
  local copies, waits for them, and re-layouts: 19.9 us -> 13.6 us
  matrix products: 14.9 us -> 10.1 us
    ppermute x12, waiting for transfers between devices: 45.8 us -> 18.8 us  [over_outer(): return lax.ppermute(array, 'fsdp', [(i, i ^ 2 * step) for i in range(8)])]
    unnamed x68 -> x52, local copies, waits for them, and re-layouts: 9.62 us -> 3.67 us
    ppermute x12, starting transfers between devices: 13.6 us -> 19.4 us  [over_outer(): return lax.ppermute(array, 'fsdp', [(i, i ^ 2 * step) for i in range(8)])]
    pallas_call x2 -> x3, Pallas kernels: 8.18 us -> 13.4 us  [the longest x2 7.07 us: fold_pair(): pl.pallas_call(body, out_shape=outs, in_specs=[pl.BlockSpec(memory_space=...]
    dot_general x4 -> x1, matrix products: 7.76 us -> 2.87 us  [contract_cols(): lax.dot_general(left_mat, right_mat, (((1,), (1,)), ((), ())), preferred_...]
  transfers between devices with their start and end apart: 38 -> 38, of which waited for: 20 -> 20; matrix products, arithmetic and copies ran while one was open for 12% -> 13% of each run, Pallas kernels for 25% -> 33%
where the time goes in v3:
time: 263 us; the launch traced here: 259 us
  Pallas kernels  128 us (49%)
  waiting for transfers between devices  45.4 us (17%)
  starting transfers between devices  43.9 us (17%)
  other arithmetic  16 us (6%)
  local copies, waits for them, and re-layouts  13.6 us (5%)
  matrix products  10.1 us (4%)
    pallas_call x1, Pallas kernels, ffn_backward(): pl.pallas_call(body, grid=(hidden // tile,), out_shape=outs + grads, in_s...  21.8 us
    pallas_call x2, Pallas kernels, attention_forward(): pl.pallas_call(body, grid=(end - begin,), out_shape=outs, in_specs=[pl.Bl...  19.7 us
    ppermute x12, starting transfers between devices, over_outer(): return lax.ppermute(array, 'fsdp', [(i, i ^ 2 * step) for i in range(8)])  19.4 us
    ppermute x12, waiting for transfers between devices, over_outer(): return lax.ppermute(array, 'fsdp', [(i, i ^ 2 * step) for i in range(8)])  18.8 us
    ppermute x12, waiting for transfers between devices, over_ctx(): return lax.ppermute(array, 'ctx', [(0, 1), (1, 0)])  17.1 us
    pallas_call x1, Pallas kernels, attention_backward(): pl.pallas_call(body, grid=(heads // 2,), out_shape=outs, in_specs=[column...  17 us
    ppermute x12, starting transfers between devices, over_ctx(): return lax.ppermute(array, 'ctx', [(0, 1), (1, 0)])  14.2 us
    ppermute x9, starting transfers between devices, over_inner(): return lax.ppermute(array, 'fsdp', [(i, i ^ 1) for i in range(8)])  9.39 us
  transfers between devices with their start and end apart: 38, of which 20 were waited for; matrix products, arithmetic and copies ran while one was open for 13% of the time, Pallas kernels for 33%

profile of v3, /device:TPU:8, one launch (start us, length us, event | category | flops | bytes accessed | tf_op | source)
XLA Modules:
  0.0 258.8 jit_solution(9635608756511203855)
XLA Ops:
  1.3 2.0 pack_early.1
  3.2 3.0 %collective-permute-start.1 = (bf16[48,1664]{1,0:T(8,128)(2,1)}, bf16[48,1664]{1,0:T(8,128)(2,1)}, u32[]{:S(2)}, u32[]{:S(2)}) collective-permute-start(bf16[48,1664]{1,0:T(8,128)(2,1)} %get-tuple-element.137), channel_id=1, source_target_pairs={{0,16},{4,20},{8,24},{12,28},{16,0},{20,4},{24,8},{28,12},{1,17},{... | collective-permute-start | bytes 479240 | tf_op jit(solution)/shard_map/ppermute | solution.py:46
  9.4 2.3 pack_late.1
  14.1 2.3 fusion.4.xt
  17.7 3.2 %collective-permute-done.2.refs_2_ = bf16[48,1664]{1,0:T(8,128)(2,1)} collective-permute-done((bf16[48,1664]{1,0:T(8,128)(2,1)}, bf16[48,1664]{1,0:T(8,128)(2,1)}, u32[]{:S(2)}, u32[]{:S(2)}) %collective-permute-start.2) | collective-permute-done | bytes 159776 | tf_op jit(solution)/shard_map/ppermute | solution.py:46
  20.9 5.7 %collective-permute-done.3 = bf16[512,768]{0,1:T(8,128)(2,1)} collective-permute-done((bf16[512,768]{0,1:T(8,128)(2,1)}, bf16[512,768]{0,1:T(8,128)(2,1)}, u32[]{:S(2)}, u32[]{:S(2)}) %collective-permute-start.3) | collective-permute-done | bytes 786464 | tf_op jit(solution)/shard_map/ppermute | solution.py:49
  26.6 1.9 join.2.came_ref
  33.1 3.4 %collective-permute-start.8 = (bf16[48,3072]{1,0:T(8,128)(2,1)}, bf16[48,3072]{1,0:T(8,128)(2,1)}, u32[]{:S(2)}, u32[]{:S(2)}) collective-permute-start(bf16[48,3072]{1,0:T(8,128)(2,1)} %get-tuple-element.145), channel_id=1, source_target_pairs={{0,8},{4,12},{8,0},{12,4},{16,24},{20,28},{24,16},{28,20},{1,9},{5... | collective-permute-start | bytes 884744 | tf_op jit(solution)/shard_map/ppermute | solution.py:46
  40.9 3.5 %collective-permute-start.9 = (bf16[48,3072]{1,0:T(8,128)(2,1)}, bf16[48,3072]{1,0:T(8,128)(2,1)}, u32[]{:S(2)}, u32[]{:S(2)}) collective-permute-start(bf16[48,3072]{1,0:T(8,128)(2,1)} %get-tuple-element.145), channel_id=1, source_target_pairs={{0,16},{4,20},{8,24},{12,28},{16,0},{20,4},{24,8},{28,12},{1,17},{... | collective-permute-start | bytes 884744 | tf_op jit(solution)/shard_map/ppermute | solution.py:46
  47.9 3.6 %assemble.2 = (bf16[768,384]{1,0:T(8,128)(2,1)}, bf16[768,384]{1,0:T(8,128)(2,1)}, bf16[768,384]{1,0:T(8,128)(2,1)}, bf16[768,384]{1,0:T(8,128)(2,1)}, bf16[768,128]{1,0:T(8,128)(2,1)}) custom-call(s32[4]{0:T(128)} %pad_add_fusion.place, bf16[96,4736]{1,0:T(8,128)(2,1)} %get-tuple-element.148.own_ref, bf16[96,4736]{1,0:T(8,128)(2,1)} %collective-permute-done.11.side_ref, ...), custom_call_target="tpu_custom_call" | custom-call | flops 9999999827968 | bytes 1 | tf_op jit(solution)/shard_map/assemble/pallas_call | solution.py:167
  52.9 3.5 %collective-permute-done.9.refs_1_ = bf16[48,3072]{1,0:T(8,128)(2,1)} collective-permute-done((bf16[48,3072]{1,0:T(8,128)(2,1)}, bf16[48,3072]{1,0:T(8,128)(2,1)}, u32[]{:S(2)}, u32[]{:S(2)}) %collective-permute-start.9) | collective-permute-done | bytes 294944 | tf_op jit(solution)/shard_map/ppermute | solution.py:46
  56.4 2.1 join.3.came_ref
  59.6 2.0 complete.2
  61.6 1.9 unpack_small.1
  63.6 2.2 convolution_convert_fusion.k
  65.8 2.9 %fusion.3.q = bf16[768,384]{1,0:T(8,128)(2,1)} fusion(bf16[768,384]{1,0:T(8,128)(2,1)S(1)} %copy-done.22, bf16[256,768]{0,1:T(8,128)(2,1)S(1)} %bitcast.58, bf16[512,768]{0,1:T(8,128)(2,1)} %bitcast.4, f32[384]{0:T(512)S(1)} %reduce), kind=kOutput, calls=%fused_computation.10 | convolution fusion | flops 456228864 | bytes 2360832 | tf_op jit(solution)/shard_map/dot_general | solution.py:17
  68.7 2.2 fusion.v
  70.9 12.6 %attention_forward.2 = (bf16[6,256,1280]{2,1,0:T(8,128)(2,1)}, bf16[6,512,1024]{2,1,0:T(8,128)(2,1)}, bf16[6,256,1280]{2,1,0:T(8,128)(2,1)}, bf16[768,384]{1,0:T(8,128)(2,1)}) custom-call(s32[1,1]{1,0:T(1,128)S(6)} %copy.71.length, bf16[768,384]{1,0:T(8,128)(2,1)} %fusion.3.q, bf16[1280,384]{1,0:T(8,128)(2,1)} %convolution_convert_fusion.k, ...), custom_call_target="tpu_custom_call" | custom-call | flops 9999999827968 | bytes 1 | tf_op jit(solution)/shard_map/attention_forward/pallas_call | solution.py:663
  84.0 1.8 slice.100
  87.4 1.8 slice.101
  90.7 7.2 %attention_forward.3 = (bf16[6,256,1280]{2,1,0:T(8,128)(2,1)}, bf16[6,512,1024]{2,1,0:T(8,128)(2,1)}, bf16[6,256,1280]{2,1,0:T(8,128)(2,1)}, bf16[768,384]{1,0:T(8,128)(2,1)}) custom-call(s32[1,1]{1,0:T(1,128)S(6)} %copy.71.length, bf16[768,384]{1,0:T(8,128)(2,1)} %fusion.3.q, ...), custom_call_target="tpu_custom_call", output_to_operand_aliasing={{0}: (5, {}), {1}: (6, {}), {2}: (7, {}), {3}: (8, {})} | custom-call | flops 9999999827968 | bytes 1 | tf_op jit(solution)/shard_map/attention_forward/pallas_call | solution.py:663
  97.8 2.9 %convolution_convert_fusion.1.p = bf16[768,768]{1,0:T(8,128)(2,1)} fusion(bf16[768,384]{1,0:T(8,128)(2,1)} %get-tuple-element.173.o, bf16[768,384]{1,0:T(8,128)(2,1)S(1)} %copy-done.11), kind=kOutput, calls=%fused_computation.7 | convolution fusion | flops 453574656 | bytes 2359296 | tf_op jit(solution)/shard_map/dot_general | solution.py:27
  100.7 4.7 %assemble.3 = (bf16[768,1536]{1,0:T(8,128)(2,1)}, bf16[768,1536]{1,0:T(8,128)(2,1)}) custom-call(s32[4]{0:T(128)} %pad_add_fusion.place, bf16[96,4736]{1,0:T(8,128)(2,1)} %get-tuple-element.148.own_ref, bf16[96,4736]{1,0:T(8,128)(2,1)} %collective-permute-done.11.side_ref, bf16[144,3072]{1,0:T(8,128)(2,1)} %join.3.came_ref, ...), custom_call_target="tpu_custom_call" | custom-call | flops 9999999827968 | bytes 1 | tf_op jit(solution)/shard_map/assemble/pallas_call | solution.py:167
  105.5 2.1 complete.3
  107.6 5.3 %first_norm.1 = (f32[768,768]{1,0:T(8,128)}, f32[768,128]{1,0:T(8,128)}, bf16[768,768]{1,0:T(8,128)(2,1)}, bf16[768,768]{1,0:T(8,128)(2,1)}) custom-call(bf16[512,768]{1,0:T(8,128)(2,1)} %bitcast.60, bf16[256,768]{1,0:T(8,128)(2,1)} %bitcast.61, bf16[768,768]{1,0:T(8,128)(2,1)} %convolution_convert_fusion.1.p, bf16[768,768]{1,0:T(8,128)(2,1)} %collective-permute-done.14.o, ...), custom_call_target="tpu_custom_call" | custom-call | flops 9999999827968 | bytes 1 | tf_op jit(solution)/shard_map/first_norm/pallas_call | solution.py:311
  112.9 8.2 %ffn_forward.1 = (bf16[768,1536]{1,0:T(8,128)(2,1)}, bf16[768,1536]{1,0:T(8,128)(2,1)}, bf16[768,768]{1,0:T(8,128)(2,1)}) custom-call(bf16[768,768]{1,0:T(8,128)(2,1)} %get-tuple-element.178.x, bf16[768,1536]{1,0:T(8,128)(2,1)} %get-tuple-element.183.up, f32[1,1536]{1,0:T(1,128)} %get-tuple-element.184.ub, bf16[768,1536]{1,0:T(8,128)(2,1)} %get-tuple-element.185.dn), custom_call_target="tpu_custom_call" | custom-call | flops 9999999827968 | bytes 1 | tf_op jit(solution)/shard_map/ffn_forward/pallas_call | solution.py:352
  121.6 2.7 %collective-permute-done.17.o = bf16[768,768]{1,0:T(8,128)(2,1)S(1)} collective-permute-done((bf16[768,768]{1,0:T(8,128)(2,1)}, bf16[768,768]{1,0:T(8,128)(2,1)S(1)}, u32[]{:S(2)}, u32[]{:S(2)}) %collective-permute-start.17) | collective-permute-done | bytes 1179680 | tf_op jit(solution)/shard_map/ppermute | solution.py:52
  125.4 21.8 %ffn_backward.1 = (bf16[512,768]{1,0:T(8,128)(2,1)}, bf16[256,768]{1,0:T(8,128)(2,1)}, f32[768,768]{1,0:T(8,128)}, bf16[768,768]{1,0:T(8,128)(2,1)}, f32[8,768]{...) custom-call(s32[4]{0:T(128)} %pad_add_fusion.place, ...), custom_call_target="tpu_custom_call" | custom-call | flops 9999999827968 | bytes 1 | tf_op jit(solution)/shard_map/ffn_backward/pallas_call | solution.py:457
  151.3 6.6 %first_norm_backward.1 = (f32[768,768]{1,0:T(8,128)}, bf16[768,384]{1,0:T(8,128)(2,1)}, f32[8,768]{1,0:T(8,128)}) custom-call(f32[768,768]{1,0:T(8,128)} %get-tuple-element.192.d2, bf16[768,768]{1,0:T(8,128)(2,1)} %get-tuple-element.193.p, bf16[768,768]{1,0:T(8,128)(2,1)} %copy-done.20, f32[768,768]{1,0:T(8,128)} %get-tuple-element.176.n1, ...), custom_call_target="tpu_custom_call" | custom-call | flops 9999999827968 | bytes 1 | tf_op jit(solution)/shard_map/first_norm_backward/pallas_call | solution.py:779
  157.9 17.0 %attention_backward.1 = (bf16[6,256,1280]{2,1,0:T(8,128)(2,1)}, bf16[768,384]{1,0:T(8,128)(2,1)}, bf16[1280,384]{1,0:T(8,128)(2,1)}, bf16[1280,384]{1,0:T(8,128)(2,1)}) custom-call(bf16[768,384]{1,0:T(8,128)(2,1)} %fusion.3.q, bf16[1280,384]{1,0:T(8,128)(2,1)} %convolution_convert_fusion.k, bf16[1280,384]{1,0:T(8,128)(2,1)} %fusion.v, ...), custom_call_target="tpu_custom_call" | custom-call | flops 9999999827968 | bytes 1 | tf_op jit(solution)/shard_map/attention_backward/pallas_call | solution.py:738
  176.2 4.2 %fold_pair.2 = (bf16[192,1536]{1,0:T(8,128)(2,1)}, bf16[192,1536]{1,0:T(8,128)(2,1)}, bf16[192,1536]{1,0:T(8,128)(2,1)}, bf16[192,1536]{1,0:T(8,128)(2,1)}) custom-call(s32[4]{0:T(128)} %pad_add_fusion.place, bf16[384,1536]{1,0:T(8,128)(2,1)} %get-tuple-element.200.refs_0_, bf16[384,1536]{1,0:T(8,128)(2,1)} %collective-permute-done.19.refs_1_, ...), custom_call_target="tpu_custom_call" | custom-call | flops 9999999827968 | bytes 1 | tf_op jit(solution)/shard_map/fold_pair/pallas_call | solution.py:506
  182.4 8.3 %weight_grads.1 = (bf16[384,768]{1,0:T(8,128)(2,1)}, bf16[384,768]{1,0:T(8,128)(2,1)}, bf16[384,896]{1,0:T(8,128)(2,1)}, bf16[384,896]{1,0:T(8,128)(2,1)}) custom-call(s32[4]{0:T(128)} %pad_add_fusion.place, f32[768,768]{1,0:T(8,128)} %get-tuple-element.195.d1, bf16[768,384]{1,0:T(8,128)(2,1)} %get-tuple-element.173.o, bf16[768,768]{1,0:T(8,128)(2,1)} %fusion.4.xt, ...), custom_call_target="tpu_custom_call" | custom-call | flops 9999999827968 | bytes 1 | tf_op jit(solution)/shard_map/weight_grads/pallas_call | solution.py:863
  192.7 4.1 %collective-permute-done.23.fa = bf16[192,1536]{1,0:T(8,128)(2,1)} collective-permute-done((bf16[192,1536]{1,0:T(8,128)(2,1)}, bf16[192,1536]{1,0:T(8,128)(2,1)}, u32[]{:S(2)}, u32[]{:S(2)}) %collective-permute-start.23) | collective-permute-done | bytes 589856 | tf_op jit(solution)/shard_map/ppermute | solution.py:49
  197.3 2.9 %fold_line.2 = (f32[48,3072]{1,0:T(8,128)}, bf16[48,3072]{1,0:T(8,128)(2,1)}, bf16[48,3072]{1,0:T(8,128)(2,1)}, bf16[48,3072]{1,0:T(8,128)(2,1)}) custom-call(s32[4]{0:T(128)} %pad_add_fusion.place, bf16[192,1536]{1,0:T(8,128)(2,1)} %get-tuple-element.206.fk, bf16[192,1536]{1,0:T(8,128)(2,1)} %collective-permute-done.23.fa, ...), custom_call_target="tpu_custom_call" | custom-call | flops 9999999827968 | bytes 1 | tf_op jit(solution)/shard_map/fold_line/pallas_call | solution.py:530
  200.2 2.4 collective-permute-start.33
  204.2 3.7 %collective-permute-done.21.refs_1_ = bf16[384,768]{1,0:T(8,128)(2,1)} collective-permute-done((bf16[384,768]{1,0:T(8,128)(2,1)}, bf16[384,768]{1,0:T(8,128)(2,1)}, u32[]{:S(2)}, u32[]{:S(2)}) %collective-permute-start.21) | collective-permute-done | bytes 589856 | tf_op jit(solution)/shard_map/ppermute | solution.py:43
  207.9 1.9 collective-permute-done.22.refs_3_
  209.8 2.9 %fold_pair.3 = (bf16[192,768]{1,0:T(8,128)(2,1)}, bf16[192,768]{1,0:T(8,128)(2,1)}, bf16[192,896]{1,0:T(8,128)(2,1)}, bf16[192,896]{1,0:T(8,128)(2,1)}) custom-call(s32[4]{0:T(128)} %pad_add_fusion.place, bf16[384,768]{1,0:T(8,128)(2,1)} %get-tuple-element.218.refs_0_, bf16[384,768]{1,0:T(8,128)(2,1)} %collective-permute-done.21.refs_1_, ...), custom_call_target="tpu_custom_call" | custom-call | flops 9999999827968 | bytes 1 | tf_op jit(solution)/shard_map/fold_pair/pallas_call | solution.py:506
  214.5 6.4 %input_pull.1 = (f32[768,768]{1,0:T(8,128)}, bf16[256,768]{1,0:T(8,128)(2,1)}, bf16[1024,768]{1,0:T(8,128)(2,1)}) custom-call(s32[4]{0:T(128)} %pad_add_fusion.place, bf16[768,384]{1,0:T(8,128)(2,1)} %get-tuple-element.233.q, bf16[1280,384]{1,0:T(8,128)(2,1)} %get-tuple-element.234.k, bf16[1280,384]{1,0:T(8,128)(2,1)} %get-tuple-element.235.v, ...), custom_call_target="tpu_custom_call" | custom-call | flops 9999999827968 | bytes 1 | tf_op jit(solution)/shard_map/input_pull/pallas_call | solution.py:813
  221.8 4.8 %collective-permute-done.35 = bf16[48,3072]{1,0:T(8,128)(2,1)} collective-permute-done((bf16[48,3072]{1,0:T(8,128)(2,1)}, bf16[48,3072]{1,0:T(8,128)(2,1)}, u32[]{:S(2)}, u32[]{:S(2)}) %collective-permute-start.35) | collective-permute-done | bytes 294944 | tf_op jit(solution)/shard_map/ppermute | solution.py:46
  226.5 2.0 add_convert_fusion.1
  230.0 2.2 fold_line.3
  232.2 2.9 %collective-permute-start.31 = (bf16[48,1664]{1,0:T(8,128)(2,1)}, bf16[48,1664]{1,0:T(8,128)(2,1)S(1)}, u32[]{:S(2)}, u32[]{:S(2)}) collective-permute-start(bf16[48,1664]{1,0:T(8,128)(2,1)} %get-tuple-element.244), channel_id=1, source_target_pairs={{0,16},{4,20},{8,24},{12,28},{16,0},{20,4},{24,8},{28,12},{1,17},{... | collective-permute-start | bytes 479240 | tf_op jit(solution)/shard_map/ppermute | solution.py:46
  238.0 1.8 add_convert_fusion
  241.2 1.7 convert_add_fusion
  243.4 3.3 %collective-permute-done.32 = bf16[48,1664]{1,0:T(8,128)(2,1)S(1)} collective-permute-done((bf16[48,1664]{1,0:T(8,128)(2,1)}, bf16[48,1664]{1,0:T(8,128)(2,1)S(1)}, u32[]{:S(2)}, u32[]{:S(2)}) %collective-permute-start.32) | collective-permute-done | bytes 159776 | tf_op jit(solution)/shard_map/ppermute | solution.py:46
  247.9 1.7 collective-permute-start.37
  250.5 2.7 %collective-permute-done.37 = bf16[48,1664]{1,0:T(8,128)(2,1)S(1)} collective-permute-done((bf16[48,1664]{1,0:T(8,128)(2,1)S(1)}, bf16[48,1664]{1,0:T(8,128)(2,1)S(1)}, u32[]{:S(2)}, u32[]{:S(2)}) %collective-permute-start.37) | collective-permute-done | bytes 159776 | tf_op jit(solution)/shard_map/ppermute | solution.py:49
  (139 shorter events, 55.0 us)
Async XLA Ops:
  1.3 5.5 %copy-start.9 = (bf16[1,512,768]{2,1,0:T(8,128)(2,1)S(1)}, bf16[1,512,768]{2,1,0:T(8,128)(2,1)}, u32[]{:S(2)}) copy-start(bf16[1,512,768]{2,1,0:T(8,128)(2,1)} %param.22) | copy-start | bytes 2359300
  3.2 13.1 %collective-permute-start = (bf16[48,1664]{1,0:T(8,128)(2,1)}, bf16[48,1664]{1,0:T(8,128)(2,1)}, u32[]{:S(2)}, u32[]{:S(2)}) collective-permute-start(bf16[48,1664]{1,0:T(8,128)(2,1)} %get-tuple-element.137), channel_id=1, source_target_pairs={{0,8},{4,12},{8,0},{12,4},{16,24},{20,28},{24,16},{28,20},{1,9},{5... | collective-permute-start | bytes 479240 | tf_op jit(solution)/shard_map/ppermute | solution.py:46
  3.2 14.5 %collective-permute-start.1 = (bf16[48,1664]{1,0:T(8,128)(2,1)}, bf16[48,1664]{1,0:T(8,128)(2,1)}, u32[]{:S(2)}, u32[]{:S(2)}) collective-permute-start(bf16[48,1664]{1,0:T(8,128)(2,1)} %get-tuple-element.137), channel_id=1, source_target_pairs={{0,16},{4,20},{8,24},{12,28},{16,0},{20,4},{24,8},{28,12},{1,17},{... | collective-permute-start | bytes 479240 | tf_op jit(solution)/shard_map/ppermute | solution.py:46
  6.3 14.6 %collective-permute-start.2 = (bf16[48,1664]{1,0:T(8,128)(2,1)}, bf16[48,1664]{1,0:T(8,128)(2,1)}, u32[]{:S(2)}, u32[]{:S(2)}) collective-permute-start(bf16[48,1664]{1,0:T(8,128)(2,1)} %get-tuple-element.137), channel_id=1, source_target_pairs={{0,24},{4,28},{8,16},{12,20},{16,8},{20,12},{24,0},{28,4},{1,25},{... | collective-permute-start | bytes 479240 | tf_op jit(solution)/shard_map/ppermute | solution.py:46
  7.9 18.8 %collective-permute-start.3 = (bf16[512,768]{0,1:T(8,128)(2,1)}, bf16[512,768]{0,1:T(8,128)(2,1)}, u32[]{:S(2)}, u32[]{:S(2)}) collective-permute-start(bf16[512,768]{0,1:T(8,128)(2,1)} %bitcast.4), channel_id=1, source_target_pairs={{0,2},{2,0},{1,3},{3,1},{4,6},{6,4},{5,7},{7,5},{8,10},{10,8},{9,1... | collective-permute-start | bytes 2359304 | tf_op jit(solution)/shard_map/ppermute | solution.py:49
  11.7 34.7 %collective-permute-start.11 = (bf16[96,4736]{1,0:T(8,128)(2,1)}, bf16[96,4736]{1,0:T(8,128)(2,1)}, u32[]{:S(2)}, u32[]{:S(2)}) collective-permute-start(bf16[96,4736]{1,0:T(8,128)(2,1)} %get-tuple-element.148.own_ref), channel_id=1, source_target_pairs={{0,4},{4,0},{8,12},{12,8},{16,20},{20,16},{24,28},{28,24},{1,5},{5... | collective-permute-start | bytes 2727944 | tf_op jit(solution)/shard_map/ppermute | solution.py:43
  13.4 15.1 %copy-start = (bf16[1,1,256,768]{2,3,1,0:T(8,128)(2,1)}, bf16[1,1,256,768]{2,3,1,0:T(8,128)(2,1)S(1)}, u32[]{:S(2)}) copy-start(bf16[1,1,256,768]{2,3,1,0:T(8,128)(2,1)S(1)} %copy.55) | copy-start | bytes 1179652
  28.5 16.6 %collective-permute-start.4 = (bf16[144,1664]{1,0:T(8,128)(2,1)}, bf16[144,1664]{1,0:T(8,128)(2,1)S(1)}, u32[]{:S(2)}, u32[]{:S(2)}) collective-permute-start(bf16[144,1664]{1,0:T(8,128)(2,1)} %join.2.came_ref), channel_id=1, source_target_pairs={{0,4},{4,0},{8,12},{12,8},{16,20},{20,16},{24,28},{28,24},{1,5},{5... | collective-permute-start | bytes 1437704 | tf_op jit(solution)/shard_map/ppermute | solution.py:43
  30.0 8.0 %copy-start.1 = (bf16[1,1,256,768]{2,3,1,0:T(8,128)(2,1)S(1)}, bf16[1,1,256,768]{2,3,1,0:T(8,128)(2,1)}, u32[]{:S(2)}) copy-start(bf16[1,1,256,768]{2,3,1,0:T(8,128)(2,1)} %copy-done) | copy-start | bytes 1179652
  30.0 10.9 %collective-permute-start.6 = (bf16[144,1664]{1,0:T(8,128)(2,1)}, bf16[144,1664]{1,0:T(8,128)(2,1)S(1)}, u32[]{:S(2)}, u32[]{:S(2)}) collective-permute-start(bf16[144,1664]{1,0:T(8,128)(2,1)} %join.2.came_ref), channel_id=1, source_target_pairs={{0,2},{2,0},{1,3},{3,1},{4,6},{6,4},{5,7},{7,5},{8,10},{10,8},{9,1... | collective-permute-start | bytes 1437704 | tf_op jit(solution)/shard_map/ppermute | solution.py:49
  31.5 21.4 %collective-permute-start.10 = (bf16[48,3072]{1,0:T(8,128)(2,1)}, bf16[48,3072]{1,0:T(8,128)(2,1)}, u32[]{:S(2)}, u32[]{:S(2)}) collective-permute-start(bf16[48,3072]{1,0:T(8,128)(2,1)} %get-tuple-element.145), channel_id=1, source_target_pairs={{0,24},{4,28},{8,16},{12,20},{16,8},{20,12},{24,0},{28,4},{1,25},{... | collective-permute-start | bytes 884744 | tf_op jit(solution)/shard_map/ppermute | solution.py:46
  33.1 19.8 %collective-permute-start.8 = (bf16[48,3072]{1,0:T(8,128)(2,1)}, bf16[48,3072]{1,0:T(8,128)(2,1)}, u32[]{:S(2)}, u32[]{:S(2)}) collective-permute-start(bf16[48,3072]{1,0:T(8,128)(2,1)} %get-tuple-element.145), channel_id=1, source_target_pairs={{0,8},{4,12},{8,0},{12,4},{16,24},{20,28},{24,16},{28,20},{1,9},{5... | collective-permute-start | bytes 884744 | tf_op jit(solution)/shard_map/ppermute | solution.py:46
  40.9 7.0 %copy-start.15 = (bf16[144,1664]{1,0:T(8,128)(2,1)}, bf16[144,1664]{1,0:T(8,128)(2,1)S(1)}, u32[]{:S(2)}) copy-start(bf16[144,1664]{1,0:T(8,128)(2,1)S(1)} %collective-permute-done.6.along_ref) | copy-start | bytes 1437700
  40.9 15.4 %collective-permute-start.9 = (bf16[48,3072]{1,0:T(8,128)(2,1)}, bf16[48,3072]{1,0:T(8,128)(2,1)}, u32[]{:S(2)}, u32[]{:S(2)}) collective-permute-start(bf16[48,3072]{1,0:T(8,128)(2,1)} %get-tuple-element.145), channel_id=1, source_target_pairs={{0,16},{4,20},{8,24},{12,28},{16,0},{20,4},{24,8},{28,12},{1,17},{... | collective-permute-start | bytes 884744 | tf_op jit(solution)/shard_map/ppermute | solution.py:46
  45.2 11.2 %collective-permute-start.7 = (bf16[144,896]{1,0:T(8,128)(2,1)}, bf16[144,896]{1,0:T(8,128)(2,1)}, u32[]{:S(2)}, u32[]{:S(2)}) collective-permute-start(bf16[144,896]{1,0:T(8,128)(2,1)} %slice.126), channel_id=1, source_target_pairs={{0,4},{4,0},{8,12},{12,8},{16,20},{20,16},{24,28},{28,24},{1,5},{5... | collective-permute-start | bytes 774152 | tf_op jit(solution)/shard_map/ppermute | solution.py:43
  46.4 10.0 %collective-permute-start.5 = (bf16[144,768]{1,0:T(8,128)(2,1)}, bf16[144,768]{1,0:T(8,128)(2,1)}, u32[]{:S(2)}, u32[]{:S(2)}) collective-permute-start(bf16[144,768]{1,0:T(8,128)(2,1)} %slice.125), channel_id=1, source_target_pairs={{0,2},{2,0},{1,3},{3,1},{4,6},{6,4},{5,7},{7,5},{8,10},{10,8},{9,1... | collective-permute-start | bytes 663560 | tf_op jit(solution)/shard_map/ppermute | solution.py:49
  58.5 25.5 %collective-permute-start.12 = (bf16[144,3072]{1,0:T(8,128)(2,1)}, bf16[144,3072]{1,0:T(8,128)(2,1)}, u32[]{:S(2)}, u32[]{:S(2)}) collective-permute-start(bf16[144,3072]{1,0:T(8,128)(2,1)} %join.3.came_ref), channel_id=1, source_target_pairs={{0,4},{4,0},{8,12},{12,8},{16,20},{20,16},{24,28},{28,24},{1,5},{5... | collective-permute-start | bytes 2654216 | tf_op jit(solution)/shard_map/ppermute | solution.py:43
  59.0 25.0 %collective-permute-start.13 = (bf16[144,3072]{1,0:T(8,128)(2,1)}, bf16[144,3072]{1,0:T(8,128)(2,1)}, u32[]{:S(2)}, u32[]{:S(2)}) collective-permute-start(bf16[144,3072]{1,0:T(8,128)(2,1)} %join.3.came_ref), channel_id=1, source_target_pairs={{0,2},{2,0},{1,3},{3,1},{4,6},{6,4},{5,7},{7,5},{8,10},{10,8},{9,1... | collective-permute-start | bytes 2654216 | tf_op jit(solution)/shard_map/ppermute | solution.py:49
  70.9 12.6 %copy-start.17 = (f32[8,768]{1,0:T(8,128)S(1)}, f32[8,768]{1,0:T(8,128)}, u32[]{:S(2)}) copy-start(f32[8,768]{1,0:T(8,128)} %get-tuple-element.175) | copy-start | bytes 73732
  85.9 19.6 %collective-permute-start.15 = (bf16[144,1536]{1,0:T(8,128)(2,1)}, bf16[144,1536]{1,0:T(8,128)(2,1)}, u32[]{:S(2)}, u32[]{:S(2)}) collective-permute-start(bf16[144,1536]{1,0:T(8,128)(2,1)} %slice.100), channel_id=1, source_target_pairs={{0,2},{2,0},{1,3},{3,1},{4,6},{6,4},{5,7},{7,5},{8,10},{10,8},{9,1... | collective-permute-start | bytes 1327112 | tf_op jit(solution)/shard_map/ppermute | solution.py:49
  89.2 16.3 %collective-permute-start.16 = (bf16[144,1536]{1,0:T(8,128)(2,1)}, bf16[144,1536]{1,0:T(8,128)(2,1)}, u32[]{:S(2)}, u32[]{:S(2)}) collective-permute-start(bf16[144,1536]{1,0:T(8,128)(2,1)} %slice.101), channel_id=1, source_target_pairs={{0,4},{4,0},{8,12},{12,8},{16,20},{20,16},{24,28},{28,24},{1,5},{5... | collective-permute-start | bytes 1327112 | tf_op jit(solution)/shard_map/ppermute | solution.py:43
  90.7 7.2 %copy-start.11 = (bf16[768,384]{1,0:T(8,128)(2,1)S(1)}, bf16[768,384]{1,0:T(8,128)(2,1)}, u32[]{:S(2)}) copy-start(bf16[768,384]{1,0:T(8,128)(2,1)} %get-tuple-element.174.ot) | copy-start | bytes 1769476
  100.7 6.9 %collective-permute-start.14 = (bf16[768,768]{1,0:T(8,128)(2,1)}, bf16[768,768]{1,0:T(8,128)(2,1)}, u32[]{:S(2)}, u32[]{:S(2)}) collective-permute-start(bf16[768,768]{1,0:T(8,128)(2,1)} %convolution_convert_fusion.1.p), channel_id=1, source_target_pairs={{0,1},{1,0},{2,3},{3,2},{4,5},{5,4},{6,7},{7,6},{8,9},{9,8},{10,11... | collective-permute-start | bytes 3538952 | tf_op jit(solution)/shard_map/ppermute | solution.py:52
  121.1 3.2 %collective-permute-start.17 = (bf16[768,768]{1,0:T(8,128)(2,1)}, bf16[768,768]{1,0:T(8,128)(2,1)S(1)}, u32[]{:S(2)}, u32[]{:S(2)}) collective-permute-start(bf16[768,768]{1,0:T(8,128)(2,1)} %get-tuple-element.186.p), channel_id=1, source_target_pairs={{0,1},{1,0},{2,3},{3,2},{4,5},{5,4},{6,7},{7,6},{8,9},{9,8},{10,11... | collective-permute-start | bytes 3538952 | tf_op jit(solution)/shard_map/ppermute | solution.py:52
  147.1 3.1 %collective-permute-start.18 = (bf16[768,768]{1,0:T(8,128)(2,1)}, bf16[768,768]{1,0:T(8,128)(2,1)S(1)}, u32[]{:S(2)}, u32[]{:S(2)}) collective-permute-start(bf16[768,768]{1,0:T(8,128)(2,1)} %get-tuple-element.193.p), channel_id=1, source_target_pairs={{0,1},{1,0},{2,3},{3,2},{4,5},{5,4},{6,7},{7,6},{8,9},{9,8},{10,11... | collective-permute-start | bytes 3538952 | tf_op jit(solution)/shard_map/ppermute | solution.py:52
  147.6 28.3 %collective-permute-start.19 = (bf16[384,1536]{1,0:T(8,128)(2,1)}, bf16[384,1536]{1,0:T(8,128)(2,1)}, u32[]{:S(2)}, u32[]{:S(2)}) collective-permute-start(bf16[384,1536]{1,0:T(8,128)(2,1)} %get-tuple-element.201), channel_id=1, source_target_pairs={{0,4},{4,0},{8,12},{12,8},{16,20},{20,16},{24,28},{28,24},{1,5},{5... | collective-permute-start | bytes 3538952 | tf_op jit(solution)/shard_map/ppermute | solution.py:43
  148.1 28.0 %collective-permute-start.20 = (bf16[384,1536]{1,0:T(8,128)(2,1)}, bf16[384,1536]{1,0:T(8,128)(2,1)}, u32[]{:S(2)}, u32[]{:S(2)}) collective-permute-start(bf16[384,1536]{1,0:T(8,128)(2,1)} %get-tuple-element.202), channel_id=1, source_target_pairs={{0,2},{2,0},{1,3},{3,1},{4,6},{6,4},{5,7},{7,5},{8,10},{10,8},{9,1... | collective-permute-start | bytes 3538952 | tf_op jit(solution)/shard_map/ppermute | solution.py:49
  180.4 16.5 %collective-permute-start.23 = (bf16[192,1536]{1,0:T(8,128)(2,1)}, bf16[192,1536]{1,0:T(8,128)(2,1)}, u32[]{:S(2)}, u32[]{:S(2)}) collective-permute-start(bf16[192,1536]{1,0:T(8,128)(2,1)} %get-tuple-element.207), channel_id=1, source_target_pairs={{0,2},{2,0},{1,3},{3,1},{4,6},{6,4},{5,7},{7,5},{8,10},{10,8},{9,1... | collective-permute-start | bytes 1769480 | tf_op jit(solution)/shard_map/ppermute | solution.py:49
  180.9 16.4 %collective-permute-start.24 = (bf16[192,1536]{1,0:T(8,128)(2,1)}, bf16[192,1536]{1,0:T(8,128)(2,1)}, u32[]{:S(2)}, u32[]{:S(2)}) collective-permute-start(bf16[192,1536]{1,0:T(8,128)(2,1)} %get-tuple-element.209), channel_id=1, source_target_pairs={{0,4},{4,0},{8,12},{12,8},{16,20},{20,16},{24,28},{28,24},{1,5},{5... | collective-permute-start | bytes 1769480 | tf_op jit(solution)/shard_map/ppermute | solution.py:43
  190.7 19.2 %collective-permute-start.22 = (bf16[384,896]{1,0:T(8,128)(2,1)}, bf16[384,896]{1,0:T(8,128)(2,1)}, u32[]{:S(2)}, u32[]{:S(2)}) collective-permute-start(bf16[384,896]{1,0:T(8,128)(2,1)} %get-tuple-element.220), channel_id=1, source_target_pairs={{0,2},{2,0},{1,3},{3,1},{4,6},{6,4},{5,7},{7,5},{8,10},{10,8},{9,1... | collective-permute-start | bytes 2064392 | tf_op jit(solution)/shard_map/ppermute | solution.py:49
  192.2 15.7 %collective-permute-start.21 = (bf16[384,768]{1,0:T(8,128)(2,1)}, bf16[384,768]{1,0:T(8,128)(2,1)}, u32[]{:S(2)}, u32[]{:S(2)}) collective-permute-start(bf16[384,768]{1,0:T(8,128)(2,1)} %get-tuple-element.219), channel_id=1, source_target_pairs={{0,4},{4,0},{8,12},{12,8},{16,20},{20,16},{24,28},{28,24},{1,5},{5... | collective-permute-start | bytes 1769480 | tf_op jit(solution)/shard_map/ppermute | solution.py:43
  200.2 20.6 %collective-permute-start.33 = (bf16[48,3072]{1,0:T(8,128)(2,1)}, bf16[48,3072]{1,0:T(8,128)(2,1)}, u32[]{:S(2)}, u32[]{:S(2)}) collective-permute-start(bf16[48,3072]{1,0:T(8,128)(2,1)} %get-tuple-element.224), channel_id=1, source_target_pairs={{0,8},{4,12},{8,0},{12,4},{16,24},{20,28},{24,16},{28,20},{1,9},{5... | collective-permute-start | bytes 884744 | tf_op jit(solution)/shard_map/ppermute | solution.py:46
  202.6 19.1 %collective-permute-start.34 = (bf16[48,3072]{1,0:T(8,128)(2,1)}, bf16[48,3072]{1,0:T(8,128)(2,1)}, u32[]{:S(2)}, u32[]{:S(2)}) collective-permute-start(bf16[48,3072]{1,0:T(8,128)(2,1)} %get-tuple-element.225), channel_id=1, source_target_pairs={{0,16},{4,20},{8,24},{12,28},{16,0},{20,4},{24,8},{28,12},{1,17},{... | collective-permute-start | bytes 884744 | tf_op jit(solution)/shard_map/ppermute | solution.py:46
  203.6 22.9 %collective-permute-start.35 = (bf16[48,3072]{1,0:T(8,128)(2,1)}, bf16[48,3072]{1,0:T(8,128)(2,1)}, u32[]{:S(2)}, u32[]{:S(2)}) collective-permute-start(bf16[48,3072]{1,0:T(8,128)(2,1)} %get-tuple-element.226), channel_id=1, source_target_pairs={{0,24},{4,28},{8,16},{12,20},{16,8},{20,12},{24,0},{28,4},{1,25},{... | collective-permute-start | bytes 884744 | tf_op jit(solution)/shard_map/ppermute | solution.py:46
  212.7 17.3 %collective-permute-start.29 = (bf16[192,896]{1,0:T(8,128)(2,1)}, bf16[192,896]{1,0:T(8,128)(2,1)}, u32[]{:S(2)}, u32[]{:S(2)}) collective-permute-start(bf16[192,896]{1,0:T(8,128)(2,1)} %get-tuple-element.232), channel_id=1, source_target_pairs={{0,4},{4,0},{8,12},{12,8},{16,20},{20,16},{24,28},{28,24},{1,5},{5... | collective-permute-start | bytes 1032200 | tf_op jit(solution)/shard_map/ppermute | solution.py:43
  214.0 16.0 %collective-permute-start.28 = (bf16[192,768]{1,0:T(8,128)(2,1)}, bf16[192,768]{1,0:T(8,128)(2,1)}, u32[]{:S(2)}, u32[]{:S(2)}) collective-permute-start(bf16[192,768]{1,0:T(8,128)(2,1)} %get-tuple-element.230), channel_id=1, source_target_pairs={{0,2},{2,0},{1,3},{3,1},{4,6},{6,4},{5,7},{7,5},{8,10},{10,8},{9,1... | collective-permute-start | bytes 884744 | tf_op jit(solution)/shard_map/ppermute | solution.py:49
  214.5 12.0 %copy-start.10 = (f32[48,3072]{1,0:T(8,128)S(1)}, f32[48,3072]{1,0:T(8,128)}, u32[]{:S(2)}) copy-start(f32[48,3072]{1,0:T(8,128)} %get-tuple-element.246) | copy-start | bytes 1769476
  220.9 17.2 %collective-permute-start.25 = (bf16[1024,768]{1,0:T(8,128)(2,1)}, bf16[1024,768]{1,0:T(8,128)(2,1)}, u32[]{:S(2)}, u32[]{:S(2)}) collective-permute-start(bf16[1024,768]{1,0:T(8,128)(2,1)} %get-tuple-element.237), channel_id=1, source_target_pairs={{0,1},{1,0},{2,3},{3,2},{4,5},{5,4},{6,7},{7,6},{8,9},{9,8},{10,11... | collective-permute-start | bytes 4718600 | tf_op jit(solution)/shard_map/ppermute | solution.py:52
  228.5 7.2 %collective-permute-start.36 = (bf16[48,3072]{1,0:T(8,128)(2,1)}, bf16[48,3072]{1,0:T(8,128)(2,1)}, u32[]{:S(2)}, u32[]{:S(2)}) collective-permute-start(bf16[48,3072]{1,0:T(8,128)(2,1)} %add_convert_fusion.1), channel_id=1, source_target_pairs={{0,2},{2,0},{1,3},{3,1},{4,6},{6,4},{5,7},{7,5},{8,10},{10,8},{9,1... | collective-permute-start | bytes 884744 | tf_op jit(solution)/shard_map/ppermute | solution.py:49
  232.2 10.7 %collective-permute-start.30 = (bf16[48,1664]{1,0:T(8,128)(2,1)}, bf16[48,1664]{1,0:T(8,128)(2,1)S(1)}, u32[]{:S(2)}, u32[]{:S(2)}) collective-permute-start(bf16[48,1664]{1,0:T(8,128)(2,1)} %get-tuple-element.243), channel_id=1, source_target_pairs={{0,8},{4,12},{8,0},{12,4},{16,24},{20,28},{24,16},{28,20},{1,9},{5... | collective-permute-start | bytes 479240 | tf_op jit(solution)/shard_map/ppermute | solution.py:46
  232.2 11.2 %collective-permute-start.31 = (bf16[48,1664]{1,0:T(8,128)(2,1)}, bf16[48,1664]{1,0:T(8,128)(2,1)S(1)}, u32[]{:S(2)}, u32[]{:S(2)}) collective-permute-start(bf16[48,1664]{1,0:T(8,128)(2,1)} %get-tuple-element.244), channel_id=1, source_target_pairs={{0,16},{4,20},{8,24},{12,28},{16,0},{20,4},{24,8},{28,12},{1,17},{... | collective-permute-start | bytes 479240 | tf_op jit(solution)/shard_map/ppermute | solution.py:46
  235.1 11.5 %collective-permute-start.32 = (bf16[48,1664]{1,0:T(8,128)(2,1)}, bf16[48,1664]{1,0:T(8,128)(2,1)S(1)}, u32[]{:S(2)}, u32[]{:S(2)}) collective-permute-start(bf16[48,1664]{1,0:T(8,128)(2,1)} %get-tuple-element.245), channel_id=1, source_target_pairs={{0,24},{4,28},{8,16},{12,20},{16,8},{20,12},{24,0},{28,4},{1,25},{... | collective-permute-start | bytes 479240 | tf_op jit(solution)/shard_map/ppermute | solution.py:46
  236.8 4.4 %copy-start.8 = (f32[768,768]{1,0:T(8,128)S(1)}, f32[768,768]{1,0:T(8,128)}, u32[]{:S(2)}) copy-start(f32[768,768]{1,0:T(8,128)} %get-tuple-element.236) | copy-start | bytes 7077892
  236.9 4.3 %copy-start.7 = (f32[768,768]{1,0:T(8,128)S(1)}, f32[768,768]{1,0:T(8,128)}, u32[]{:S(2)}) copy-start(f32[768,768]{1,0:T(8,128)} %get-tuple-element.195.d1) | copy-start | bytes 7077892
  239.9 8.0 %copy-start.14 = (f32[48,1664]{1,0:T(8,128)S(1)}, f32[48,1664]{1,0:T(8,128)}, u32[]{:S(2)}) copy-start(f32[48,1664]{1,0:T(8,128)} %get-tuple-element.242) | copy-start | bytes 958468
  239.9 7.9 %collective-permute-start.26 = (bf16[256,768]{1,0:T(8,128)(2,1)S(1)}, bf16[256,768]{1,0:T(8,128)(2,1)}, u32[]{:S(2)}, u32[]{:S(2)}) collective-permute-start(bf16[256,768]{1,0:T(8,128)(2,1)S(1)} %add_convert_fusion), channel_id=1, source_target_pairs={{0,2},{2,0},{1,3},{3,1},{4,6},{6,4},{5,7},{7,5},{8,10},{10,8},{9,1... | collective-permute-start | bytes 1179656 | tf_op jit(solution)/shard_map/ppermute | solution.py:49
  247.9 5.3 %collective-permute-start.37 = (bf16[48,1664]{1,0:T(8,128)(2,1)S(1)}, bf16[48,1664]{1,0:T(8,128)(2,1)S(1)}, u32[]{:S(2)}, u32[]{:S(2)}) collective-permute-start(bf16[48,1664]{1,0:T(8,128)(2,1)S(1)} %add_convert_fusion.2), channel_id=1, source_target_pairs={{0,2},{2,0},{1,3},{3,1},{4,6},{6,4},{5,7},{7,5},{8,10},{10,8},{9,1... | collective-permute-start | bytes 479240 | tf_op jit(solution)/shard_map/ppermute | solution.py:49
  250.5 5.8 %collective-permute-start.27 = (bf16[256,768]{1,0:T(8,128)(2,1)}, bf16[256,768]{1,0:T(8,128)(2,1)}, u32[]{:S(2)}, u32[]{:S(2)}) collective-permute-start(bf16[256,768]{1,0:T(8,128)(2,1)} %collective-permute-done.26), channel_id=1, source_target_pairs={{0,1},{1,0},{2,3},{3,2},{4,5},{5,4},{6,7},{7,6},{8,9},{9,8},{10,11... | collective-permute-start | bytes 1179656 | tf_op jit(solution)/shard_map/ppermute | solution.py:52
  (15 other events, 31.0 us)

commit v4 on v3

--- a/solution.py
+++ b/solution.py
@@ -232,6 +232,24 @@
     return grid.over_ctx(across[:, :cut]), grid.over_inner(along[:, cut:])
 
 
+def halves_of(across, along):
+    rows, cols = across.shape[0], across.shape[1] // 2
+
+    def body(first, second, first_out, second_out):
+        first_out[...] = first[...]
+        second_out[...] = second[...]
+
+    return pl.pallas_call(
+        body,
+        grid=(1,),
+        out_shape=[like((rows, cols), across.dtype)] * 2,
+        in_specs=[pl.BlockSpec((rows, cols), lambda i: (0, 0)), pl.BlockSpec((rows, cols), lambda i: (0, 1))],
+        out_specs=[pl.BlockSpec((rows, cols), lambda i: (0, 0))] * 2,
+        cost_estimate=cost(0, across, along),
+        name="halves_of",
+    )(across, along)
+
+
 def pick(array, at, axis):
     return lax.dynamic_index_in_dim(array, at, axis, keepdims=False)
 
@@ -289,14 +307,12 @@
     tile = row_tile(prompt_len)
     ahead = prompt_len // tile
 
-    def body(x, c, p, o, b, g, s, norm_out, inv_out, low_out, turned_out):
+    def body(x, c, p, o, b, g, s, norm_out, inv_out, low_out):
         rows_in = jnp.where(pl.program_id(0) < ahead, x[...].astype(f32), c[...].astype(f32))
         normed, inverse = norm_rows(rows_in + (p[...].astype(f32) + o[...].astype(f32)) + b[...])
         norm_out[...] = normed
         inv_out[...] = jnp.broadcast_to(inverse, inv_out.shape)
-        value = normed * g[...] + s[...]
-        low_out[...] = value.astype(bf16)
-        turned_out[...] = value.T.astype(bf16)
+        low_out[...] = (normed * g[...] + s[...]).astype(bf16)
 
     def tiled(array):
         return pl.BlockSpec((tile, array.shape[1]), lambda i: (i, 0))
@@ -306,7 +322,6 @@
         like((rows, width), f32),
         like((rows, LANES), f32),
         like((rows, width), bf16),
-        like((width, rows), bf16),
     ]
     return pl.pallas_call(
         body,
@@ -318,11 +333,29 @@
         ]
         + [tiled(a) for a in args[2:4]]
         + [whole_block(a) for a in args[4:]],
-        out_specs=[tiled(a) for a in outs[:3]] + [pl.BlockSpec((width, tile), lambda i: (0, i))],
+        out_specs=[tiled(a) for a in outs],
         compiler_params=pltpu.CompilerParams(vmem_limit_bytes=VMEM_LIMIT),
         cost_estimate=cost(0, *args, *outs),
         name="first_norm",
     )(*args)
+
+
+def turn(array):
+    rows, cols = array.shape
+    tile = row_tile(rows)
+
+    def body(x, out):
+        out[...] = x[...].astype(f32).T.astype(bf16)
+
+    return pl.pallas_call(
+        body,
+        grid=(rows // tile,),
+        out_shape=like((cols, rows), bf16),
+        in_specs=[pl.BlockSpec((tile, cols), lambda i: (i, 0))],
+        out_specs=pl.BlockSpec((cols, tile), lambda i: (0, i)),
+        cost_estimate=cost(0, array),
+        name="turn",
+    )(array)
 
 
 def ffn_forward(low, up_mat, up_add, down_turned):
@@ -481,6 +514,8 @@
     for group in (firsts, seconds):
         outs += [like((4 * half, sum(kept.shape[1] for kept, _ in group)), bf16)] * 2
 
+    vmem = pl.BlockSpec(memory_space=pltpu.VMEM)
+
     def body(place, *refs):
         pairs, outs = refs[:-4], refs[-4:]
         at_pair = 0
@@ -501,7 +536,6 @@
                         ).astype(bf16)
                 low = high
 
-    vmem = pl.BlockSpec(memory_space=pltpu.VMEM)
     args = [a for group in (firsts, seconds) for pair in group for a in pair]
     return pl.pallas_call(
         body,
@@ -569,7 +603,7 @@
         self.came = [self.grid.over_outer(sent[step - 1], step) for step in (1, 2, 3)]
         return sent
 
-    def shard(self, *earlier):
+    def shard(self, *earlier, beside=()):
         grid = self.grid
         if not grid.staged:
             both = jnp.concatenate([g[0] for g in self.firsts + self.seconds], 1)
@@ -580,7 +614,7 @@
         for piece in came:
             total = total + piece.astype(f32)
         total = total.astype(bf16)
-        other = grid.over_ctx(total)
+        other = after(grid.over_ctx(total), *beside)
         low = jnp.where(grid.row == 0, total, other)
         high = jnp.where(grid.row == 0, other, total)
         return jnp.concatenate([low, high], 0).astype(f32)
@@ -980,12 +1014,9 @@
         across, along = pairs_of(grid, came)
         far = corners_of(grid, across, along, cut)
         late_came = lines_of(grid, late_half)
-        far, late_came = lax.optimization_barrier((far, late_came))
         early = complete(
             grid, assemble(grid, cuts, 0, shards, side, came, across, along), *far
         )
-        late_came = join(late_came)
-        late_across, late_along = pairs_of(grid, late_came)
     else:
         shards = [shard] + late
         shards = [lax.all_gather(a, "fsdp", axis=0, tiled=True) for a in shards]
@@ -996,6 +1027,10 @@
     vectors, query_add, value_add, up_line = unpack_small(
         grid, small, head_count, head_size, up_bias.shape[0]
     )
+    if grid.staged:
+        late_came = join(after(late_came, vectors))
+        late_across, late_along = pairs_of(grid, late_came)
+        query_mat, key_mat, value_mat = after((query_mat, key_mat, value_mat), late_came)
     output_line, gain1, shift1, down_line, gain2, shift2 = [vectors[i : i + 1] for i in range(6)]
 
     inputs = jnp.concatenate([mine, conts], 0)
@@ -1019,7 +1054,9 @@
     held = attention_forward(*attention, (0, pair_count - 1))
     if grid.staged:
         late_across, late_along, held = lax.optimization_barrier((late_across, late_along, held))
-        far = corners_of(grid, late_across, late_along, hidden)
+        first, second = halves_of(late_across, late_along)
+        held = after(held, first)
+        far = grid.over_ctx(first), grid.over_inner(second)
     new_logits, probs_p, probs_c, attended = attention_forward(
         *attention, (pair_count - 1, pair_count), held
     )
@@ -1028,13 +1065,14 @@
             grid, [hidden, hidden], sum(cuts), shards, side, late_came, late_across, late_along
         )
     part = contract_cols(attended, output_turned).astype(bf16)
-    norm1, inv1, low1, turned1 = first_norm(
+    norm1, inv1, low1 = first_norm(
         mine, conts, part, grid.over_tp(part), output_line, gain1, shift1
     )
     if grid.staged:
         late = complete(grid, late, *far)
     up_mat, down_turned = late
     activated, slope, part2 = ffn_forward(low1, up_mat, up_line, down_turned)
+    turned1 = turn(after(low1, part2))
     results = ffn_backward(
         grid,
         norm1,
@@ -1098,7 +1136,7 @@
         shared = ()
     up_grad, down_turned_grad = columns_of(shard_f, [hidden, hidden])
     down_grad = down_turned_grad.T
-    shard_c = sum_c.shard(up_grad, down_grad, *shared)
+    shard_c = sum_c.shard(up_grad, down_grad, *shared, beside=[grad_prompt])
     output_grads, query_grad, key_grad, value_grad, table = columns_of(shard_c, widths)
     model = whole.shape[1]
     table = jnp.concatenate([table[:, at : at + LANES] for at in range(0, table.shape[1], LANES)], 0)

time: 263 us -> 256 us (0.973)
  Pallas kernels: 128 us -> 133 us
  local copies, waits for them, and re-layouts: 13.6 us -> 8.94 us
  starting transfers between devices: 43.9 us -> 39.6 us
    pallas_call x0 -> x2, Pallas kernels: none -> 5.46 us  [the longest x1 3.37 us: turn(): pl.pallas_call(body, grid=(rows // tile,), out_shape=like((cols, rows), b...]
    ppermute x12, waiting for transfers between devices: 17.1 us -> 21.1 us  [over_ctx(): return lax.ppermute(array, 'ctx', [(0, 1), (1, 0)])]
    ppermute x12, starting transfers between devices: 19.4 us -> 15.4 us  [over_outer(): return lax.ppermute(array, 'fsdp', [(i, i ^ 2 * step) for i in range(8)])]
    slice x4 -> x2, local copies, waits for them, and re-layouts: 5.02 us -> 1.43 us  [corners_of(): return (grid.over_ctx(across[:, :cut]), grid.over_inner(along[:, cut:]))]
    ppermute x12, waiting for transfers between devices: 18.8 us -> 15.3 us  [over_outer(): return lax.ppermute(array, 'fsdp', [(i, i ^ 2 * step) for i in range(8)])]
  transfers between devices with their start and end apart: 38 -> 38, of which waited for: 20 -> 19; matrix products, arithmetic and copies ran while one was open for 13% -> 11% of each run, Pallas kernels for 33% -> 35%
where the time goes in v4:
time: 256 us; the launch traced here: 253 us
  Pallas kernels  133 us (52%)
  waiting for transfers between devices  44.4 us (17%)
  starting transfers between devices  39.6 us (15%)
  other arithmetic  14.9 us (6%)
  matrix products  10.1 us (4%)
  local copies, waits for them, and re-layouts  8.94 us (3%)
    pallas_call x1, Pallas kernels, ffn_backward(): pl.pallas_call(body, grid=(hidden // tile,), out_shape=outs + grads, in_s...  21.8 us
    ppermute x12, waiting for transfers between devices, over_ctx(): return lax.ppermute(array, 'ctx', [(0, 1), (1, 0)])  21.1 us
    pallas_call x2, Pallas kernels, attention_forward(): pl.pallas_call(body, grid=(end - begin,), out_shape=outs, in_specs=[pl.Bl...  19.7 us
    pallas_call x1, Pallas kernels, attention_backward(): pl.pallas_call(body, grid=(heads // 2,), out_shape=outs, in_specs=[column...  17 us
    ppermute x12, starting transfers between devices, over_outer(): return lax.ppermute(array, 'fsdp', [(i, i ^ 2 * step) for i in range(8)])  15.4 us
    ppermute x12, waiting for transfers between devices, over_outer(): return lax.ppermute(array, 'fsdp', [(i, i ^ 2 * step) for i in range(8)])  15.3 us
    ppermute x12, starting transfers between devices, over_ctx(): return lax.ppermute(array, 'ctx', [(0, 1), (1, 0)])  13.4 us
    ppermute x9, starting transfers between devices, over_inner(): return lax.ppermute(array, 'fsdp', [(i, i ^ 1) for i in range(8)])  10.1 us
  transfers between devices with their start and end apart: 38, of which 19 were waited for; matrix products, arithmetic and copies ran while one was open for 11% of the time, Pallas kernels for 35%

profile of v4, /device:TPU:8, one launch (start us, length us, event | category | flops | bytes accessed | tf_op | source)
XLA Modules:
  0.0 253.0 jit_solution(7575623372289818313)
XLA Ops:
  1.3 2.0 pack_early.1
  3.2 3.0 %collective-permute-start.1 = (bf16[48,1664]{1,0:T(8,128)(2,1)}, bf16[48,1664]{1,0:T(8,128)(2,1)}, u32[]{:S(2)}, u32[]{:S(2)}) collective-permute-start(bf16[48,1664]{1,0:T(8,128)(2,1)} %get-tuple-element.145), channel_id=1, source_target_pairs={{0,16},{4,20},{8,24},{12,28},{16,0},{20,4},{24,8},{28,12},{1,17},{... | collective-permute-start | bytes 479240 | tf_op jit(solution)/shard_map/ppermute | solution.py:46
  9.4 2.3 pack_late.1
  14.1 2.3 fusion.3.xt
  17.7 3.2 %collective-permute-done.2.refs_2_ = bf16[48,1664]{1,0:T(8,128)(2,1)} collective-permute-done((bf16[48,1664]{1,0:T(8,128)(2,1)}, bf16[48,1664]{1,0:T(8,128)(2,1)}, u32[]{:S(2)}, u32[]{:S(2)}) %collective-permute-start.2) | collective-permute-done | bytes 159776 | tf_op jit(solution)/shard_map/ppermute | solution.py:46
  20.9 5.7 %collective-permute-done.3 = bf16[512,768]{0,1:T(8,128)(2,1)} collective-permute-done((bf16[512,768]{0,1:T(8,128)(2,1)}, bf16[512,768]{0,1:T(8,128)(2,1)}, u32[]{:S(2)}, u32[]{:S(2)}) %collective-permute-start.3) | collective-permute-done | bytes 786464 | tf_op jit(solution)/shard_map/ppermute | solution.py:49
  26.6 1.9 join.2.came_ref
  31.5 3.5 %collective-permute-start.10 = (bf16[48,3072]{1,0:T(8,128)(2,1)}, bf16[48,3072]{1,0:T(8,128)(2,1)}, u32[]{:S(2)}, u32[]{:S(2)}) collective-permute-start(bf16[48,3072]{1,0:T(8,128)(2,1)} %get-tuple-element.162), channel_id=1, source_target_pairs={{0,16},{4,20},{8,24},{12,28},{16,0},{20,4},{24,8},{28,12},{1,17},{... | collective-permute-start | bytes 884744 | tf_op jit(solution)/shard_map/ppermute | solution.py:46
  38.3 2.7 %collective-permute-done.6.along_ref = bf16[144,1664]{1,0:T(8,128)(2,1)S(1)} collective-permute-done((bf16[144,1664]{1,0:T(8,128)(2,1)}, bf16[144,1664]{1,0:T(8,128)(2,1)S(1)}, u32[]{:S(2)}, u32[]{:S(2)}) %collective-permute-start.6) | collective-permute-done | bytes 479264 | tf_op jit(solution)/shard_map/ppermute | solution.py:49
  45.9 3.6 %assemble.2 = (bf16[768,384]{1,0:T(8,128)(2,1)}, bf16[768,384]{1,0:T(8,128)(2,1)}, bf16[768,384]{1,0:T(8,128)(2,1)}, bf16[768,384]{1,0:T(8,128)(2,1)}, bf16[768,128]{1,0:T(8,128)(2,1)}) custom-call(s32[4]{0:T(128)} %pad_add_fusion.place, bf16[96,4736]{1,0:T(8,128)(2,1)} %get-tuple-element.153.own_ref, bf16[96,4736]{1,0:T(8,128)(2,1)} %collective-permute-done.8.side_ref, ...), custom_call_target="tpu_custom_call" | custom-call | flops 9999999827968 | bytes 1 | tf_op jit(solution)/shard_map/assemble/pallas_call | solution.py:167
  49.5 2.0 collective-permute-done.5.one_ref
  51.5 2.0 complete.2
  53.4 1.8 unpack_small.1
  55.2 3.0 %collective-permute-done.11.refs_2_ = bf16[48,3072]{1,0:T(8,128)(2,1)} collective-permute-done((bf16[48,3072]{1,0:T(8,128)(2,1)}, bf16[48,3072]{1,0:T(8,128)(2,1)}, u32[]{:S(2)}, u32[]{:S(2)}) %collective-permute-start.11) | collective-permute-done | bytes 294944 | tf_op jit(solution)/shard_map/ppermute | solution.py:46
  58.3 2.3 join.3.came_ref
  61.8 2.2 convolution_convert_fusion.k
  64.1 2.9 %fusion.2.q = bf16[768,384]{1,0:T(8,128)(2,1)} fusion(bf16[768,384]{1,0:T(8,128)(2,1)S(1)} %copy-done.21, bf16[256,768]{0,1:T(8,128)(2,1)S(1)} %bitcast.57, bf16[512,768]{0,1:T(8,128)(2,1)} %bitcast.4, f32[384]{0:T(512)S(1)} %reduce), kind=kOutput, calls=%fused_computation.9 | convolution fusion | flops 456228864 | bytes 2360832 | tf_op jit(solution)/shard_map/dot_general | solution.py:17
  67.0 2.2 fusion.v
  69.1 12.6 %attention_forward.2 = (bf16[6,256,1280]{2,1,0:T(8,128)(2,1)}, bf16[6,512,1024]{2,1,0:T(8,128)(2,1)}, bf16[6,256,1280]{2,1,0:T(8,128)(2,1)}, bf16[768,384]{1,0:T(8,128)(2,1)}) custom-call(s32[1,1]{1,0:T(1,128)S(6)} %copy.71.length, bf16[768,384]{1,0:T(8,128)(2,1)} %fusion.2.q, bf16[1280,384]{1,0:T(8,128)(2,1)} %convolution_convert_fusion.k, ...), custom_call_target="tpu_custom_call" | custom-call | flops 9999999827968 | bytes 1 | tf_op jit(solution)/shard_map/attention_forward/pallas_call | solution.py:697
  82.3 2.1 halves_of.1
  87.2 7.2 %attention_forward.3 = (bf16[6,256,1280]{2,1,0:T(8,128)(2,1)}, bf16[6,512,1024]{2,1,0:T(8,128)(2,1)}, bf16[6,256,1280]{2,1,0:T(8,128)(2,1)}, bf16[768,384]{1,0:T(8,128)(2,1)}) custom-call(s32[1,1]{1,0:T(1,128)S(6)} %copy.71.length, bf16[768,384]{1,0:T(8,128)(2,1)} %fusion.2.q, ...), custom_call_target="tpu_custom_call", output_to_operand_aliasing={{0}: (5, {}), {1}: (6, {}), {2}: (7, {}), {3}: (8, {})} | custom-call | flops 9999999827968 | bytes 1 | tf_op jit(solution)/shard_map/attention_forward/pallas_call | solution.py:697
  94.4 2.9 %convolution_convert_fusion.1.p = bf16[768,768]{1,0:T(8,128)(2,1)} fusion(bf16[768,384]{1,0:T(8,128)(2,1)} %get-tuple-element.190.o, bf16[768,384]{1,0:T(8,128)(2,1)S(1)} %copy-done.11), kind=kOutput, calls=%fused_computation.6 | convolution fusion | flops 453574656 | bytes 2359296 | tf_op jit(solution)/shard_map/dot_general | solution.py:27
  97.3 4.7 %assemble.3 = (bf16[768,1536]{1,0:T(8,128)(2,1)}, bf16[768,1536]{1,0:T(8,128)(2,1)}) custom-call(s32[4]{0:T(128)} %pad_add_fusion.place, bf16[96,4736]{1,0:T(8,128)(2,1)} %get-tuple-element.153.own_ref, bf16[96,4736]{1,0:T(8,128)(2,1)} %collective-permute-done.8.side_ref, bf16[144,3072]{1,0:T(8,128)(2,1)} %join.3.came_ref, ...), custom_call_target="tpu_custom_call" | custom-call | flops 9999999827968 | bytes 1 | tf_op jit(solution)/shard_map/assemble/pallas_call | solution.py:167
  102.0 2.1 complete.3
  104.2 5.1 %first_norm.1 = (f32[768,768]{1,0:T(8,128)}, f32[768,128]{1,0:T(8,128)}, bf16[768,768]{1,0:T(8,128)(2,1)}) custom-call(bf16[512,768]{1,0:T(8,128)(2,1)} %bitcast.60, bf16[256,768]{1,0:T(8,128)(2,1)} %bitcast.61, bf16[768,768]{1,0:T(8,128)(2,1)} %convolution_convert_fusion.1.p, bf16[768,768]{1,0:T(8,128)(2,1)} %collective-permute-done.14.o, ...), custom_call_target="tpu_custom_call" | custom-call | flops 9999999827968 | bytes 1 | tf_op jit(solution)/shard_map/first_norm/pallas_call | solution.py:326
  109.2 8.2 %ffn_forward.1 = (bf16[768,1536]{1,0:T(8,128)(2,1)}, bf16[768,1536]{1,0:T(8,128)(2,1)}, bf16[768,768]{1,0:T(8,128)(2,1)}) custom-call(bf16[768,768]{1,0:T(8,128)(2,1)} %get-tuple-element.201.x, bf16[768,1536]{1,0:T(8,128)(2,1)} %get-tuple-element.197.up, f32[1,1536]{1,0:T(1,128)} %get-tuple-element.198.ub, bf16[768,1536]{1,0:T(8,128)(2,1)} %get-tuple-element.199.dn), custom_call_target="tpu_custom_call" | custom-call | flops 9999999827968 | bytes 1 | tf_op jit(solution)/shard_map/ffn_forward/pallas_call | solution.py:385
  118.0 3.4 %turn.1.x1_t = bf16[768,768]{1,0:T(8,128)(2,1)} custom-call(bf16[768,768]{1,0:T(8,128)(2,1)} %get-tuple-element.201.x), custom_call_target="tpu_custom_call" | custom-call | flops 9999999827968 | bytes 1 | tf_op jit(solution)/shard_map/turn/pallas_call | solution.py:350
  121.4 21.8 %ffn_backward.1 = (bf16[512,768]{1,0:T(8,128)(2,1)}, bf16[256,768]{1,0:T(8,128)(2,1)}, f32[768,768]{1,0:T(8,128)}, bf16[768,768]{1,0:T(8,128)(2,1)}, f32[8,768]{...) custom-call(s32[4]{0:T(128)} %pad_add_fusion.place, ...), custom_call_target="tpu_custom_call" | custom-call | flops 9999999827968 | bytes 1 | tf_op jit(solution)/shard_map/ffn_backward/pallas_call | solution.py:490
  144.6 1.7 collective-permute-done.18.o
  147.3 6.6 %first_norm_backward.1 = (f32[768,768]{1,0:T(8,128)}, bf16[768,384]{1,0:T(8,128)(2,1)}, f32[8,768]{1,0:T(8,128)}) custom-call(f32[768,768]{1,0:T(8,128)} %get-tuple-element.207.d2, bf16[768,768]{1,0:T(8,128)(2,1)} %get-tuple-element.208.p, bf16[768,768]{1,0:T(8,128)(2,1)} %copy-done.20, f32[768,768]{1,0:T(8,128)} %get-tuple-element.192.n1, ...), custom_call_target="tpu_custom_call" | custom-call | flops 9999999827968 | bytes 1 | tf_op jit(solution)/shard_map/first_norm_backward/pallas_call | solution.py:813
  153.9 17.0 %attention_backward.1 = (bf16[6,256,1280]{2,1,0:T(8,128)(2,1)}, bf16[768,384]{1,0:T(8,128)(2,1)}, bf16[1280,384]{1,0:T(8,128)(2,1)}, bf16[1280,384]{1,0:T(8,128)(2,1)}) custom-call(bf16[768,384]{1,0:T(8,128)(2,1)} %fusion.2.q, bf16[1280,384]{1,0:T(8,128)(2,1)} %convolution_convert_fusion.k, bf16[1280,384]{1,0:T(8,128)(2,1)} %fusion.v, ...), custom_call_target="tpu_custom_call" | custom-call | flops 9999999827968 | bytes 1 | tf_op jit(solution)/shard_map/attention_backward/pallas_call | solution.py:772
  172.1 4.2 %fold_pair.2 = (bf16[192,1536]{1,0:T(8,128)(2,1)}, bf16[192,1536]{1,0:T(8,128)(2,1)}, bf16[192,1536]{1,0:T(8,128)(2,1)}, bf16[192,1536]{1,0:T(8,128)(2,1)}) custom-call(s32[4]{0:T(128)} %pad_add_fusion.place, bf16[384,1536]{1,0:T(8,128)(2,1)} %get-tuple-element.215.refs_0_, bf16[384,1536]{1,0:T(8,128)(2,1)} %collective-permute-done.19.refs_1_, ...), custom_call_target="tpu_custom_call" | custom-call | flops 9999999827968 | bytes 1 | tf_op jit(solution)/shard_map/fold_pair/pallas_call | solution.py:540
  178.3 8.3 %weight_grads.1 = (bf16[384,768]{1,0:T(8,128)(2,1)}, bf16[384,768]{1,0:T(8,128)(2,1)}, bf16[384,896]{1,0:T(8,128)(2,1)}, bf16[384,896]{1,0:T(8,128)(2,1)}) custom-call(s32[4]{0:T(128)} %pad_add_fusion.place, f32[768,768]{1,0:T(8,128)} %get-tuple-element.210.d1, bf16[768,384]{1,0:T(8,128)(2,1)} %get-tuple-element.190.o, bf16[768,768]{1,0:T(8,128)(2,1)} %fusion.3.xt, ...), custom_call_target="tpu_custom_call" | custom-call | flops 9999999827968 | bytes 1 | tf_op jit(solution)/shard_map/weight_grads/pallas_call | solution.py:897
  188.7 4.1 %collective-permute-done.23.fa = bf16[192,1536]{1,0:T(8,128)(2,1)} collective-permute-done((bf16[192,1536]{1,0:T(8,128)(2,1)}, bf16[192,1536]{1,0:T(8,128)(2,1)}, u32[]{:S(2)}, u32[]{:S(2)}) %collective-permute-start.23) | collective-permute-done | bytes 589856 | tf_op jit(solution)/shard_map/ppermute | solution.py:49
  193.6 2.9 %fold_line.2 = (f32[48,3072]{1,0:T(8,128)}, bf16[48,3072]{1,0:T(8,128)(2,1)}, bf16[48,3072]{1,0:T(8,128)(2,1)}, bf16[48,3072]{1,0:T(8,128)(2,1)}) custom-call(s32[4]{0:T(128)} %pad_add_fusion.place, bf16[192,1536]{1,0:T(8,128)(2,1)} %get-tuple-element.221.fk, bf16[192,1536]{1,0:T(8,128)(2,1)} %collective-permute-done.23.fa, ...), custom_call_target="tpu_custom_call" | custom-call | flops 9999999827968 | bytes 1 | tf_op jit(solution)/shard_map/fold_line/pallas_call | solution.py:564
  197.3 2.6 %collective-permute-start.34 = (bf16[48,3072]{1,0:T(8,128)(2,1)}, bf16[48,3072]{1,0:T(8,128)(2,1)}, u32[]{:S(2)}, u32[]{:S(2)}) collective-permute-start(bf16[48,3072]{1,0:T(8,128)(2,1)} %get-tuple-element.240), channel_id=1, source_target_pairs={{0,16},{4,20},{8,24},{12,28},{16,0},{20,4},{24,8},{28,12},{1,17},{... | collective-permute-start | bytes 884744 | tf_op jit(solution)/shard_map/ppermute | solution.py:46
  200.0 4.3 %collective-permute-done.21.refs_1_ = bf16[384,768]{1,0:T(8,128)(2,1)} collective-permute-done((bf16[384,768]{1,0:T(8,128)(2,1)}, bf16[384,768]{1,0:T(8,128)(2,1)}, u32[]{:S(2)}, u32[]{:S(2)}) %collective-permute-start.21) | collective-permute-done | bytes 589856 | tf_op jit(solution)/shard_map/ppermute | solution.py:43
  204.3 1.7 collective-permute-done.22.refs_3_
  206.0 2.9 %fold_pair.3 = (bf16[192,768]{1,0:T(8,128)(2,1)}, bf16[192,768]{1,0:T(8,128)(2,1)}, bf16[192,896]{1,0:T(8,128)(2,1)}, bf16[192,896]{1,0:T(8,128)(2,1)}) custom-call(s32[4]{0:T(128)} %pad_add_fusion.place, bf16[384,768]{1,0:T(8,128)(2,1)} %get-tuple-element.233.refs_0_, bf16[384,768]{1,0:T(8,128)(2,1)} %collective-permute-done.21.refs_1_, ...), custom_call_target="tpu_custom_call" | custom-call | flops 9999999827968 | bytes 1 | tf_op jit(solution)/shard_map/fold_pair/pallas_call | solution.py:540
  210.8 6.4 %input_pull.1 = (f32[768,768]{1,0:T(8,128)}, bf16[256,768]{1,0:T(8,128)(2,1)}, bf16[1024,768]{1,0:T(8,128)(2,1)}) custom-call(s32[4]{0:T(128)} %pad_add_fusion.place, bf16[768,384]{1,0:T(8,128)(2,1)} %get-tuple-element.248.q, bf16[1280,384]{1,0:T(8,128)(2,1)} %get-tuple-element.249.k, bf16[1280,384]{1,0:T(8,128)(2,1)} %get-tuple-element.250.v, ...), custom_call_target="tpu_custom_call" | custom-call | flops 9999999827968 | bytes 1 | tf_op jit(solution)/shard_map/input_pull/pallas_call | solution.py:847
  217.8 4.4 %collective-permute-done.35 = bf16[48,3072]{1,0:T(8,128)(2,1)} collective-permute-done((bf16[48,3072]{1,0:T(8,128)(2,1)}, bf16[48,3072]{1,0:T(8,128)(2,1)}, u32[]{:S(2)}, u32[]{:S(2)}) %collective-permute-start.35) | collective-permute-done | bytes 294944 | tf_op jit(solution)/shard_map/ppermute | solution.py:46
  222.1 2.0 add_convert_fusion.1
  225.5 2.3 fold_line.3
  227.7 3.0 %collective-permute-start.31 = (bf16[48,1664]{1,0:T(8,128)(2,1)}, bf16[48,1664]{1,0:T(8,128)(2,1)S(1)}, u32[]{:S(2)}, u32[]{:S(2)}) collective-permute-start(bf16[48,1664]{1,0:T(8,128)(2,1)} %get-tuple-element.259), channel_id=1, source_target_pairs={{0,16},{4,20},{8,24},{12,28},{16,0},{20,4},{24,8},{28,12},{1,17},{... | collective-permute-start | bytes 479240 | tf_op jit(solution)/shard_map/ppermute | solution.py:46
  233.6 1.8 add_convert_fusion
  236.8 1.7 convert_add_fusion
  239.4 2.7 %collective-permute-done.32 = bf16[48,1664]{1,0:T(8,128)(2,1)S(1)} collective-permute-done((bf16[48,1664]{1,0:T(8,128)(2,1)}, bf16[48,1664]{1,0:T(8,128)(2,1)S(1)}, u32[]{:S(2)}, u32[]{:S(2)}) %collective-permute-start.32) | collective-permute-done | bytes 159776 | tf_op jit(solution)/shard_map/ppermute | solution.py:46
  246.3 3.6 %collective-permute-done.37 = bf16[48,1664]{1,0:T(8,128)(2,1)S(1)} collective-permute-done((bf16[48,1664]{1,0:T(8,128)(2,1)S(1)}, bf16[48,1664]{1,0:T(8,128)(2,1)S(1)}, u32[]{:S(2)}, u32[]{:S(2)}) %collective-permute-start.37) | collective-permute-done | bytes 159776 | tf_op jit(solution)/shard_map/ppermute | solution.py:49
  (137 shorter events, 48.8 us)
Async XLA Ops:
  1.3 5.5 %copy-start.9 = (bf16[1,512,768]{2,1,0:T(8,128)(2,1)S(1)}, bf16[1,512,768]{2,1,0:T(8,128)(2,1)}, u32[]{:S(2)}) copy-start(bf16[1,512,768]{2,1,0:T(8,128)(2,1)} %param.22) | copy-start | bytes 2359300
  3.2 13.1 %collective-permute-start = (bf16[48,1664]{1,0:T(8,128)(2,1)}, bf16[48,1664]{1,0:T(8,128)(2,1)}, u32[]{:S(2)}, u32[]{:S(2)}) collective-permute-start(bf16[48,1664]{1,0:T(8,128)(2,1)} %get-tuple-element.145), channel_id=1, source_target_pairs={{0,8},{4,12},{8,0},{12,4},{16,24},{20,28},{24,16},{28,20},{1,9},{5... | collective-permute-start | bytes 479240 | tf_op jit(solution)/shard_map/ppermute | solution.py:46
  3.2 14.5 %collective-permute-start.1 = (bf16[48,1664]{1,0:T(8,128)(2,1)}, bf16[48,1664]{1,0:T(8,128)(2,1)}, u32[]{:S(2)}, u32[]{:S(2)}) collective-permute-start(bf16[48,1664]{1,0:T(8,128)(2,1)} %get-tuple-element.145), channel_id=1, source_target_pairs={{0,16},{4,20},{8,24},{12,28},{16,0},{20,4},{24,8},{28,12},{1,17},{... | collective-permute-start | bytes 479240 | tf_op jit(solution)/shard_map/ppermute | solution.py:46
  6.3 14.6 %collective-permute-start.2 = (bf16[48,1664]{1,0:T(8,128)(2,1)}, bf16[48,1664]{1,0:T(8,128)(2,1)}, u32[]{:S(2)}, u32[]{:S(2)}) collective-permute-start(bf16[48,1664]{1,0:T(8,128)(2,1)} %get-tuple-element.145), channel_id=1, source_target_pairs={{0,24},{4,28},{8,16},{12,20},{16,8},{20,12},{24,0},{28,4},{1,25},{... | collective-permute-start | bytes 479240 | tf_op jit(solution)/shard_map/ppermute | solution.py:46
  7.9 18.8 %collective-permute-start.3 = (bf16[512,768]{0,1:T(8,128)(2,1)}, bf16[512,768]{0,1:T(8,128)(2,1)}, u32[]{:S(2)}, u32[]{:S(2)}) collective-permute-start(bf16[512,768]{0,1:T(8,128)(2,1)} %bitcast.4), channel_id=1, source_target_pairs={{0,2},{2,0},{1,3},{3,1},{4,6},{6,4},{5,7},{7,5},{8,10},{10,8},{9,1... | collective-permute-start | bytes 2359304 | tf_op jit(solution)/shard_map/ppermute | solution.py:49
  11.7 33.5 %collective-permute-start.8 = (bf16[96,4736]{1,0:T(8,128)(2,1)}, bf16[96,4736]{1,0:T(8,128)(2,1)}, u32[]{:S(2)}, u32[]{:S(2)}) collective-permute-start(bf16[96,4736]{1,0:T(8,128)(2,1)} %get-tuple-element.153.own_ref), channel_id=1, source_target_pairs={{0,4},{4,0},{8,12},{12,8},{16,20},{20,16},{24,28},{28,24},{1,5},{5... | collective-permute-start | bytes 2727944 | tf_op jit(solution)/shard_map/ppermute | solution.py:43
  13.4 15.1 %copy-start = (bf16[1,1,256,768]{2,3,1,0:T(8,128)(2,1)}, bf16[1,1,256,768]{2,3,1,0:T(8,128)(2,1)S(1)}, u32[]{:S(2)}) copy-start(bf16[1,1,256,768]{2,3,1,0:T(8,128)(2,1)S(1)} %copy.55) | copy-start | bytes 1179652
  28.5 14.6 %collective-permute-start.4 = (bf16[144,1664]{1,0:T(8,128)(2,1)}, bf16[144,1664]{1,0:T(8,128)(2,1)S(1)}, u32[]{:S(2)}, u32[]{:S(2)}) collective-permute-start(bf16[144,1664]{1,0:T(8,128)(2,1)} %join.2.came_ref), channel_id=1, source_target_pairs={{0,4},{4,0},{8,12},{12,8},{16,20},{20,16},{24,28},{28,24},{1,5},{5... | collective-permute-start | bytes 1437704 | tf_op jit(solution)/shard_map/ppermute | solution.py:43
  30.0 6.5 %copy-start.1 = (bf16[1,1,256,768]{2,3,1,0:T(8,128)(2,1)S(1)}, bf16[1,1,256,768]{2,3,1,0:T(8,128)(2,1)}, u32[]{:S(2)}) copy-start(bf16[1,1,256,768]{2,3,1,0:T(8,128)(2,1)} %copy-done) | copy-start | bytes 1179652
  30.0 10.9 %collective-permute-start.6 = (bf16[144,1664]{1,0:T(8,128)(2,1)}, bf16[144,1664]{1,0:T(8,128)(2,1)S(1)}, u32[]{:S(2)}, u32[]{:S(2)}) collective-permute-start(bf16[144,1664]{1,0:T(8,128)(2,1)} %join.2.came_ref), channel_id=1, source_target_pairs={{0,2},{2,0},{1,3},{3,1},{4,6},{6,4},{5,7},{7,5},{8,10},{10,8},{9,1... | collective-permute-start | bytes 1437704 | tf_op jit(solution)/shard_map/ppermute | solution.py:49
  31.5 23.7 %collective-permute-start.10 = (bf16[48,3072]{1,0:T(8,128)(2,1)}, bf16[48,3072]{1,0:T(8,128)(2,1)}, u32[]{:S(2)}, u32[]{:S(2)}) collective-permute-start(bf16[48,3072]{1,0:T(8,128)(2,1)} %get-tuple-element.162), channel_id=1, source_target_pairs={{0,16},{4,20},{8,24},{12,28},{16,0},{20,4},{24,8},{28,12},{1,17},{... | collective-permute-start | bytes 884744 | tf_op jit(solution)/shard_map/ppermute | solution.py:46
  35.0 23.2 %collective-permute-start.11 = (bf16[48,3072]{1,0:T(8,128)(2,1)}, bf16[48,3072]{1,0:T(8,128)(2,1)}, u32[]{:S(2)}, u32[]{:S(2)}) collective-permute-start(bf16[48,3072]{1,0:T(8,128)(2,1)} %get-tuple-element.162), channel_id=1, source_target_pairs={{0,24},{4,28},{8,16},{12,20},{16,8},{20,12},{24,0},{28,4},{1,25},{... | collective-permute-start | bytes 884744 | tf_op jit(solution)/shard_map/ppermute | solution.py:46
  40.9 5.0 %copy-start.15 = (bf16[144,1664]{1,0:T(8,128)(2,1)}, bf16[144,1664]{1,0:T(8,128)(2,1)S(1)}, u32[]{:S(2)}) copy-start(bf16[144,1664]{1,0:T(8,128)(2,1)S(1)} %collective-permute-done.6.along_ref) | copy-start | bytes 1437700
  40.9 17.3 %collective-permute-start.9 = (bf16[48,3072]{1,0:T(8,128)(2,1)}, bf16[48,3072]{1,0:T(8,128)(2,1)}, u32[]{:S(2)}, u32[]{:S(2)}) collective-permute-start(bf16[48,3072]{1,0:T(8,128)(2,1)} %get-tuple-element.162), channel_id=1, source_target_pairs={{0,8},{4,12},{8,0},{12,4},{16,24},{20,28},{24,16},{28,20},{1,9},{5... | collective-permute-start | bytes 884744 | tf_op jit(solution)/shard_map/ppermute | solution.py:46
  43.1 8.3 %collective-permute-start.7 = (bf16[144,896]{1,0:T(8,128)(2,1)}, bf16[144,896]{1,0:T(8,128)(2,1)}, u32[]{:S(2)}, u32[]{:S(2)}) collective-permute-start(bf16[144,896]{1,0:T(8,128)(2,1)} %slice.118), channel_id=1, source_target_pairs={{0,4},{4,0},{8,12},{12,8},{16,20},{20,16},{24,28},{28,24},{1,5},{5... | collective-permute-start | bytes 774152 | tf_op jit(solution)/shard_map/ppermute | solution.py:43
  45.2 6.2 %collective-permute-start.5 = (bf16[144,768]{1,0:T(8,128)(2,1)}, bf16[144,768]{1,0:T(8,128)(2,1)}, u32[]{:S(2)}, u32[]{:S(2)}) collective-permute-start(bf16[144,768]{1,0:T(8,128)(2,1)} %slice.117), channel_id=1, source_target_pairs={{0,2},{2,0},{1,3},{3,1},{4,6},{6,4},{5,7},{7,5},{8,10},{10,8},{9,1... | collective-permute-start | bytes 663560 | tf_op jit(solution)/shard_map/ppermute | solution.py:49
  60.6 21.7 %collective-permute-start.12 = (bf16[144,3072]{1,0:T(8,128)(2,1)}, bf16[144,3072]{1,0:T(8,128)(2,1)}, u32[]{:S(2)}, u32[]{:S(2)}) collective-permute-start(bf16[144,3072]{1,0:T(8,128)(2,1)} %join.3.came_ref), channel_id=1, source_target_pairs={{0,4},{4,0},{8,12},{12,8},{16,20},{20,16},{24,28},{28,24},{1,5},{5... | collective-permute-start | bytes 2654216 | tf_op jit(solution)/shard_map/ppermute | solution.py:43
  61.1 21.2 %collective-permute-start.13 = (bf16[144,3072]{1,0:T(8,128)(2,1)}, bf16[144,3072]{1,0:T(8,128)(2,1)}, u32[]{:S(2)}, u32[]{:S(2)}) collective-permute-start(bf16[144,3072]{1,0:T(8,128)(2,1)} %join.3.came_ref), channel_id=1, source_target_pairs={{0,2},{2,0},{1,3},{3,1},{4,6},{6,4},{5,7},{7,5},{8,10},{10,8},{9,1... | collective-permute-start | bytes 2654216 | tf_op jit(solution)/shard_map/ppermute | solution.py:49
  69.1 12.6 %copy-start.17 = (f32[8,768]{1,0:T(8,128)S(1)}, f32[8,768]{1,0:T(8,128)}, u32[]{:S(2)}) copy-start(f32[8,768]{1,0:T(8,128)} %get-tuple-element.164) | copy-start | bytes 73732
  84.4 17.6 %collective-permute-start.15 = (bf16[144,1536]{1,0:T(8,128)(2,1)}, bf16[144,1536]{1,0:T(8,128)(2,1)}, u32[]{:S(2)}, u32[]{:S(2)}) collective-permute-start(bf16[144,1536]{1,0:T(8,128)(2,1)} %get-tuple-element.185), channel_id=1, source_target_pairs={{0,2},{2,0},{1,3},{3,1},{4,6},{6,4},{5,7},{7,5},{8,10},{10,8},{9,1... | collective-permute-start | bytes 1327112 | tf_op jit(solution)/shard_map/ppermute | solution.py:49
  85.7 16.3 %collective-permute-start.16 = (bf16[144,1536]{1,0:T(8,128)(2,1)}, bf16[144,1536]{1,0:T(8,128)(2,1)}, u32[]{:S(2)}, u32[]{:S(2)}) collective-permute-start(bf16[144,1536]{1,0:T(8,128)(2,1)} %get-tuple-element.194), channel_id=1, source_target_pairs={{0,4},{4,0},{8,12},{12,8},{16,20},{20,16},{24,28},{28,24},{1,5},{5... | collective-permute-start | bytes 1327112 | tf_op jit(solution)/shard_map/ppermute | solution.py:43
  87.2 7.2 %copy-start.11 = (bf16[768,384]{1,0:T(8,128)(2,1)S(1)}, bf16[768,384]{1,0:T(8,128)(2,1)}, u32[]{:S(2)}) copy-start(bf16[768,384]{1,0:T(8,128)(2,1)} %get-tuple-element.191.ot) | copy-start | bytes 1769476
  97.2 6.9 %collective-permute-start.14 = (bf16[768,768]{1,0:T(8,128)(2,1)}, bf16[768,768]{1,0:T(8,128)(2,1)}, u32[]{:S(2)}, u32[]{:S(2)}) collective-permute-start(bf16[768,768]{1,0:T(8,128)(2,1)} %convolution_convert_fusion.1.p), channel_id=1, source_target_pairs={{0,1},{1,0},{2,3},{3,2},{4,5},{5,4},{6,7},{7,6},{8,9},{9,8},{10,11... | collective-permute-start | bytes 3538952 | tf_op jit(solution)/shard_map/ppermute | solution.py:52
  117.5 3.9 %collective-permute-start.17 = (bf16[768,768]{1,0:T(8,128)(2,1)}, bf16[768,768]{1,0:T(8,128)(2,1)}, u32[]{:S(2)}, u32[]{:S(2)}) collective-permute-start(bf16[768,768]{1,0:T(8,128)(2,1)} %get-tuple-element.200.p), channel_id=1, source_target_pairs={{0,1},{1,0},{2,3},{3,2},{4,5},{5,4},{6,7},{7,6},{8,9},{9,8},{10,11... | collective-permute-start | bytes 3538952 | tf_op jit(solution)/shard_map/ppermute | solution.py:52
  143.1 3.1 %collective-permute-start.18 = (bf16[768,768]{1,0:T(8,128)(2,1)}, bf16[768,768]{1,0:T(8,128)(2,1)S(1)}, u32[]{:S(2)}, u32[]{:S(2)}) collective-permute-start(bf16[768,768]{1,0:T(8,128)(2,1)} %get-tuple-element.208.p), channel_id=1, source_target_pairs={{0,1},{1,0},{2,3},{3,2},{4,5},{5,4},{6,7},{7,6},{8,9},{9,8},{10,11... | collective-permute-start | bytes 3538952 | tf_op jit(solution)/shard_map/ppermute | solution.py:52
  143.2 28.7 %collective-permute-start.19 = (bf16[384,1536]{1,0:T(8,128)(2,1)}, bf16[384,1536]{1,0:T(8,128)(2,1)}, u32[]{:S(2)}, u32[]{:S(2)}) collective-permute-start(bf16[384,1536]{1,0:T(8,128)(2,1)} %get-tuple-element.216), channel_id=1, source_target_pairs={{0,4},{4,0},{8,12},{12,8},{16,20},{20,16},{24,28},{28,24},{1,5},{5... | collective-permute-start | bytes 3538952 | tf_op jit(solution)/shard_map/ppermute | solution.py:43
  143.8 28.3 %collective-permute-start.20 = (bf16[384,1536]{1,0:T(8,128)(2,1)}, bf16[384,1536]{1,0:T(8,128)(2,1)}, u32[]{:S(2)}, u32[]{:S(2)}) collective-permute-start(bf16[384,1536]{1,0:T(8,128)(2,1)} %get-tuple-element.217), channel_id=1, source_target_pairs={{0,2},{2,0},{1,3},{3,1},{4,6},{6,4},{5,7},{7,5},{8,10},{10,8},{9,1... | collective-permute-start | bytes 3538952 | tf_op jit(solution)/shard_map/ppermute | solution.py:49
  176.3 16.5 %collective-permute-start.23 = (bf16[192,1536]{1,0:T(8,128)(2,1)}, bf16[192,1536]{1,0:T(8,128)(2,1)}, u32[]{:S(2)}, u32[]{:S(2)}) collective-permute-start(bf16[192,1536]{1,0:T(8,128)(2,1)} %get-tuple-element.222), channel_id=1, source_target_pairs={{0,2},{2,0},{1,3},{3,1},{4,6},{6,4},{5,7},{7,5},{8,10},{10,8},{9,1... | collective-permute-start | bytes 1769480 | tf_op jit(solution)/shard_map/ppermute | solution.py:49
  177.1 16.5 %collective-permute-start.24 = (bf16[192,1536]{1,0:T(8,128)(2,1)}, bf16[192,1536]{1,0:T(8,128)(2,1)}, u32[]{:S(2)}, u32[]{:S(2)}) collective-permute-start(bf16[192,1536]{1,0:T(8,128)(2,1)} %get-tuple-element.224), channel_id=1, source_target_pairs={{0,4},{4,0},{8,12},{12,8},{16,20},{20,16},{24,28},{28,24},{1,5},{5... | collective-permute-start | bytes 1769480 | tf_op jit(solution)/shard_map/ppermute | solution.py:43
  186.7 19.3 %collective-permute-start.22 = (bf16[384,896]{1,0:T(8,128)(2,1)}, bf16[384,896]{1,0:T(8,128)(2,1)}, u32[]{:S(2)}, u32[]{:S(2)}) collective-permute-start(bf16[384,896]{1,0:T(8,128)(2,1)} %get-tuple-element.235), channel_id=1, source_target_pairs={{0,2},{2,0},{1,3},{3,1},{4,6},{6,4},{5,7},{7,5},{8,10},{10,8},{9,1... | collective-permute-start | bytes 2064392 | tf_op jit(solution)/shard_map/ppermute | solution.py:49
  188.2 16.1 %collective-permute-start.21 = (bf16[384,768]{1,0:T(8,128)(2,1)}, bf16[384,768]{1,0:T(8,128)(2,1)}, u32[]{:S(2)}, u32[]{:S(2)}) collective-permute-start(bf16[384,768]{1,0:T(8,128)(2,1)} %get-tuple-element.234), channel_id=1, source_target_pairs={{0,4},{4,0},{8,12},{12,8},{16,20},{20,16},{24,28},{28,24},{1,5},{5... | collective-permute-start | bytes 1769480 | tf_op jit(solution)/shard_map/ppermute | solution.py:43
  196.5 20.6 %collective-permute-start.33 = (bf16[48,3072]{1,0:T(8,128)(2,1)}, bf16[48,3072]{1,0:T(8,128)(2,1)}, u32[]{:S(2)}, u32[]{:S(2)}) collective-permute-start(bf16[48,3072]{1,0:T(8,128)(2,1)} %get-tuple-element.239), channel_id=1, source_target_pairs={{0,8},{4,12},{8,0},{12,4},{16,24},{20,28},{24,16},{28,20},{1,9},{5... | collective-permute-start | bytes 884744 | tf_op jit(solution)/shard_map/ppermute | solution.py:46
  197.3 20.5 %collective-permute-start.34 = (bf16[48,3072]{1,0:T(8,128)(2,1)}, bf16[48,3072]{1,0:T(8,128)(2,1)}, u32[]{:S(2)}, u32[]{:S(2)}) collective-permute-start(bf16[48,3072]{1,0:T(8,128)(2,1)} %get-tuple-element.240), channel_id=1, source_target_pairs={{0,16},{4,20},{8,24},{12,28},{16,0},{20,4},{24,8},{28,12},{1,17},{... | collective-permute-start | bytes 884744 | tf_op jit(solution)/shard_map/ppermute | solution.py:46
  199.9 22.3 %collective-permute-start.35 = (bf16[48,3072]{1,0:T(8,128)(2,1)}, bf16[48,3072]{1,0:T(8,128)(2,1)}, u32[]{:S(2)}, u32[]{:S(2)}) collective-permute-start(bf16[48,3072]{1,0:T(8,128)(2,1)} %get-tuple-element.241), channel_id=1, source_target_pairs={{0,24},{4,28},{8,16},{12,20},{16,8},{20,12},{24,0},{28,4},{1,25},{... | collective-permute-start | bytes 884744 | tf_op jit(solution)/shard_map/ppermute | solution.py:46
  208.8 16.6 %collective-permute-start.29 = (bf16[192,896]{1,0:T(8,128)(2,1)}, bf16[192,896]{1,0:T(8,128)(2,1)}, u32[]{:S(2)}, u32[]{:S(2)}) collective-permute-start(bf16[192,896]{1,0:T(8,128)(2,1)} %get-tuple-element.247), channel_id=1, source_target_pairs={{0,4},{4,0},{8,12},{12,8},{16,20},{20,16},{24,28},{28,24},{1,5},{5... | collective-permute-start | bytes 1032200 | tf_op jit(solution)/shard_map/ppermute | solution.py:43
  210.3 15.2 %collective-permute-start.28 = (bf16[192,768]{1,0:T(8,128)(2,1)}, bf16[192,768]{1,0:T(8,128)(2,1)}, u32[]{:S(2)}, u32[]{:S(2)}) collective-permute-start(bf16[192,768]{1,0:T(8,128)(2,1)} %get-tuple-element.245), channel_id=1, source_target_pairs={{0,2},{2,0},{1,3},{3,1},{4,6},{6,4},{5,7},{7,5},{8,10},{10,8},{9,1... | collective-permute-start | bytes 884744 | tf_op jit(solution)/shard_map/ppermute | solution.py:49
  210.8 11.4 %copy-start.10 = (f32[48,3072]{1,0:T(8,128)S(1)}, f32[48,3072]{1,0:T(8,128)}, u32[]{:S(2)}) copy-start(f32[48,3072]{1,0:T(8,128)} %get-tuple-element.261) | copy-start | bytes 1769476
  217.2 16.4 %collective-permute-start.25 = (bf16[1024,768]{1,0:T(8,128)(2,1)}, bf16[1024,768]{1,0:T(8,128)(2,1)}, u32[]{:S(2)}, u32[]{:S(2)}) collective-permute-start(bf16[1024,768]{1,0:T(8,128)(2,1)} %get-tuple-element.252), channel_id=1, source_target_pairs={{0,1},{1,0},{2,3},{3,2},{4,5},{5,4},{6,7},{7,6},{8,9},{9,8},{10,11... | collective-permute-start | bytes 4718600 | tf_op jit(solution)/shard_map/ppermute | solution.py:52
  224.1 7.1 %collective-permute-start.36 = (bf16[48,3072]{1,0:T(8,128)(2,1)}, bf16[48,3072]{1,0:T(8,128)(2,1)}, u32[]{:S(2)}, u32[]{:S(2)}) collective-permute-start(bf16[48,3072]{1,0:T(8,128)(2,1)} %add_convert_fusion.1), channel_id=1, source_target_pairs={{0,2},{2,0},{1,3},{3,1},{4,6},{6,4},{5,7},{7,5},{8,10},{10,8},{9,1... | collective-permute-start | bytes 884744 | tf_op jit(solution)/shard_map/ppermute | solution.py:49
  227.7 11.7 %collective-permute-start.30 = (bf16[48,1664]{1,0:T(8,128)(2,1)}, bf16[48,1664]{1,0:T(8,128)(2,1)S(1)}, u32[]{:S(2)}, u32[]{:S(2)}) collective-permute-start(bf16[48,1664]{1,0:T(8,128)(2,1)} %get-tuple-element.258), channel_id=1, source_target_pairs={{0,8},{4,12},{8,0},{12,4},{16,24},{20,28},{24,16},{28,20},{1,9},{5... | collective-permute-start | bytes 479240 | tf_op jit(solution)/shard_map/ppermute | solution.py:46
  227.7 11.7 %collective-permute-start.31 = (bf16[48,1664]{1,0:T(8,128)(2,1)}, bf16[48,1664]{1,0:T(8,128)(2,1)S(1)}, u32[]{:S(2)}, u32[]{:S(2)}) collective-permute-start(bf16[48,1664]{1,0:T(8,128)(2,1)} %get-tuple-element.259), channel_id=1, source_target_pairs={{0,16},{4,20},{8,24},{12,28},{16,0},{20,4},{24,8},{28,12},{1,17},{... | collective-permute-start | bytes 479240 | tf_op jit(solution)/shard_map/ppermute | solution.py:46
  230.7 11.4 %collective-permute-start.32 = (bf16[48,1664]{1,0:T(8,128)(2,1)}, bf16[48,1664]{1,0:T(8,128)(2,1)S(1)}, u32[]{:S(2)}, u32[]{:S(2)}) collective-permute-start(bf16[48,1664]{1,0:T(8,128)(2,1)} %get-tuple-element.260), channel_id=1, source_target_pairs={{0,24},{4,28},{8,16},{12,20},{16,8},{20,12},{24,0},{28,4},{1,25},{... | collective-permute-start | bytes 479240 | tf_op jit(solution)/shard_map/ppermute | solution.py:46
  232.3 4.4 %copy-start.8 = (f32[768,768]{1,0:T(8,128)S(1)}, f32[768,768]{1,0:T(8,128)}, u32[]{:S(2)}) copy-start(f32[768,768]{1,0:T(8,128)} %get-tuple-element.251) | copy-start | bytes 7077892
  232.5 4.3 %copy-start.7 = (f32[768,768]{1,0:T(8,128)S(1)}, f32[768,768]{1,0:T(8,128)}, u32[]{:S(2)}) copy-start(f32[768,768]{1,0:T(8,128)} %get-tuple-element.210.d1) | copy-start | bytes 7077892
  235.4 7.9 %copy-start.14 = (f32[48,1664]{1,0:T(8,128)S(1)}, f32[48,1664]{1,0:T(8,128)}, u32[]{:S(2)}) copy-start(f32[48,1664]{1,0:T(8,128)} %get-tuple-element.257) | copy-start | bytes 958468
  235.4 7.8 %collective-permute-start.26 = (bf16[256,768]{1,0:T(8,128)(2,1)S(1)}, bf16[256,768]{1,0:T(8,128)(2,1)S(1)}, u32[]{:S(2)}, u32[]{:S(2)}) collective-permute-start(bf16[256,768]{1,0:T(8,128)(2,1)S(1)} %add_convert_fusion), channel_id=1, source_target_pairs={{0,2},{2,0},{1,3},{3,1},{4,6},{6,4},{5,7},{7,5},{8,10},{10,8},{9,1... | collective-permute-start | bytes 1179656 | tf_op jit(solution)/shard_map/ppermute | solution.py:49
  243.2 1.7 collective-permute-start.27
  243.3 6.6 %collective-permute-start.37 = (bf16[48,1664]{1,0:T(8,128)(2,1)S(1)}, bf16[48,1664]{1,0:T(8,128)(2,1)S(1)}, u32[]{:S(2)}, u32[]{:S(2)}) collective-permute-start(bf16[48,1664]{1,0:T(8,128)(2,1)S(1)} %add_convert_fusion.2), channel_id=1, source_target_pairs={{0,2},{2,0},{1,3},{3,1},{4,6},{6,4},{5,7},{7,5},{8,10},{10,8},{9,1... | collective-permute-start | bytes 479240 | tf_op jit(solution)/shard_map/ppermute | solution.py:49
  (14 other events, 39.9 us)

commit v5 on v4

--- a/solution.py
+++ b/solution.py
@@ -259,6 +259,7 @@
 
 
 VMEM_LIMIT = 60 * 1024 * 1024
+SMALL_VMEM_LIMIT = 30 * 1024 * 1024
 
 
 def whole_block(array):
@@ -334,7 +335,7 @@
         + [tiled(a) for a in args[2:4]]
         + [whole_block(a) for a in args[4:]],
         out_specs=[tiled(a) for a in outs],
-        compiler_params=pltpu.CompilerParams(vmem_limit_bytes=VMEM_LIMIT),
+        compiler_params=pltpu.CompilerParams(vmem_limit_bytes=SMALL_VMEM_LIMIT),
         cost_estimate=cost(0, *args, *outs),
         name="first_norm",
     )(*args)
@@ -353,6 +354,7 @@
         out_shape=like((cols, rows), bf16),
         in_specs=[pl.BlockSpec((tile, cols), lambda i: (i, 0))],
         out_specs=pl.BlockSpec((cols, tile), lambda i: (0, i)),
+        compiler_params=pltpu.CompilerParams(vmem_limit_bytes=SMALL_VMEM_LIMIT),
         cost_estimate=cost(0, array),
         name="turn",
     )(array)
@@ -388,7 +390,7 @@
         out_shape=outs,
         in_specs=[tiled(low)] + [whole_block(a) for a in args[1:]],
         out_specs=[tiled(a) for a in outs],
-        compiler_params=pltpu.CompilerParams(vmem_limit_bytes=VMEM_LIMIT),
+        compiler_params=pltpu.CompilerParams(vmem_limit_bytes=SMALL_VMEM_LIMIT),
         cost_estimate=cost(4 * rows * width * hidden, *args, *outs, transcendentals=2 * rows * hidden),
         name="ffn_forward",
     )(*args)
@@ -915,7 +917,8 @@
     shards = grid.fsdp
     block, per_head, per_up = width // shards, head_size // shards, LANES // shards
 
-    def body(packed_ref, lines, query_out, value_out, up_out):
+    def body(packed_ref, *refs):
+        lines, (query_out, value_out, up_out) = refs[:6], refs[6:]
         source = lax.broadcasted_iota(jnp.int32, (LANES, width), 0)
         target = lax.broadcasted_iota(jnp.int32, (LANES, width), 1)
         whole = jnp.zeros((32, width), f32)
@@ -932,7 +935,8 @@
             by_head += product(piece, put.astype(bf16))
             put = (shift == shard * per_up) & (near < per_up)
             by_up += product(piece, put.astype(bf16))
-        lines[...] = whole[:8, :]
+        for i, out in enumerate(lines):
+            out[...] = whole[i : i + 1, :]
         low = lax.broadcasted_iota(jnp.int32, (1, LANES), 1) < head_size
         for pair in range(heads // 2):
             at = slice(pair * LANES, (pair + 1) * LANES)
@@ -943,8 +947,7 @@
             row = 6 + 2 * heads + i
             up_out[:, i * LANES : (i + 1) * LANES] = by_up[row : row + 1, :]
 
-    outs = [
-        like((8, width), f32),
+    outs = [like((1, width), f32)] * 6 + [
         like((1, heads * head_size), f32),
         like((1, heads * head_size), f32),
         like((1, up_rows * LANES), f32),
@@ -954,7 +957,7 @@
         body,
         out_shape=outs,
         in_specs=[vmem],
-        out_specs=[vmem] * 4,
+        out_specs=[vmem] * 9,
         cost_estimate=cost(0, packed, *outs),
         name="unpack_small",
     )(packed)
@@ -1024,14 +1027,14 @@
         early = [shards[0][:, low:high] for low, high in zip(edges, edges[1:])]
         late = shards[1:]
     query_mat, key_mat, value_mat, output_turned, small = early
-    vectors, query_add, value_add, up_line = unpack_small(
+    *vectors, query_add, value_add, up_line = unpack_small(
         grid, small, head_count, head_size, up_bias.shape[0]
     )
     if grid.staged:
         late_came = join(after(late_came, vectors))
         late_across, late_along = pairs_of(grid, late_came)
         query_mat, key_mat, value_mat = after((query_mat, key_mat, value_mat), late_came)
-    output_line, gain1, shift1, down_line, gain2, shift2 = [vectors[i : i + 1] for i in range(6)]
+    output_line, gain1, shift1, down_line, gain2, shift2 = vectors
 
     inputs = jnp.concatenate([mine, conts], 0)
     if sizes[1] == 2:

time: 256 us -> 253 us (0.988)
  Pallas kernels: 133 us -> 126 us
  local copies, waits for them, and re-layouts: 8.94 us -> 11.9 us
    unnamed x50 -> x66, local copies, waits for them, and re-layouts: 2.64 us -> 6.26 us
    pallas_call x1, Pallas kernels: 3.37 us -> 0.62 us  [turn(): pl.pallas_call(body, grid=(rows // tile,), out_shape=like((cols, rows), b...]
    pallas_call x1, Pallas kernels: 8.23 us -> 5.65 us  [ffn_forward(): pl.pallas_call(body, grid=(rows // tile,), out_shape=outs, in_specs=[tile...]
  transfers between devices with their start and end apart: 38 -> 38, of which waited for: 19 -> 19; matrix products, arithmetic and copies ran while one was open for 11% -> 12% of each run, Pallas kernels for 35% -> 34%
where the time goes in v5:
time: 253 us; the launch traced here: 250 us
  Pallas kernels  126 us (50%)
  waiting for transfers between devices  44.1 us (17%)
  starting transfers between devices  39.8 us (16%)
  other arithmetic  14.9 us (6%)
  local copies, waits for them, and re-layouts  11.9 us (5%)
  matrix products  11.3 us (4%)
    pallas_call x1, Pallas kernels, ffn_backward(): pl.pallas_call(body, grid=(hidden // tile,), out_shape=outs + grads, in_s...  21.8 us
    ppermute x12, waiting for transfers between devices, over_ctx(): return lax.ppermute(array, 'ctx', [(0, 1), (1, 0)])  21.4 us
    pallas_call x2, Pallas kernels, attention_forward(): pl.pallas_call(body, grid=(end - begin,), out_shape=outs, in_specs=[pl.Bl...  19.5 us
    pallas_call x1, Pallas kernels, attention_backward(): pl.pallas_call(body, grid=(heads // 2,), out_shape=outs, in_specs=[column...  17 us
    ppermute x12, starting transfers between devices, over_outer(): return lax.ppermute(array, 'fsdp', [(i, i ^ 2 * step) for i in range(8)])  15.4 us
    ppermute x12, waiting for transfers between devices, over_outer(): return lax.ppermute(array, 'fsdp', [(i, i ^ 2 * step) for i in range(8)])  15.3 us
    ppermute x12, starting transfers between devices, over_ctx(): return lax.ppermute(array, 'ctx', [(0, 1), (1, 0)])  13.3 us
    ppermute x9, starting transfers between devices, over_inner(): return lax.ppermute(array, 'fsdp', [(i, i ^ 1) for i in range(8)])  9.91 us
  transfers between devices with their start and end apart: 38, of which 19 were waited for; matrix products, arithmetic and copies ran while one was open for 12% of the time, Pallas kernels for 34%

profile of v5, /device:TPU:8, one launch (start us, length us, event | category | flops | bytes accessed | tf_op | source)
XLA Modules:
  0.0 250.1 jit_solution(1561182325684215954)
XLA Ops:
  1.3 2.0 pack_early.1
  3.2 3.0 %collective-permute-start.1 = (bf16[48,1664]{1,0:T(8,128)(2,1)}, bf16[48,1664]{1,0:T(8,128)(2,1)}, u32[]{:S(2)}, u32[]{:S(2)}) collective-permute-start(bf16[48,1664]{1,0:T(8,128)(2,1)} %get-tuple-element.150), channel_id=1, source_target_pairs={{0,16},{4,20},{8,24},{12,28},{16,0},{20,4},{24,8},{28,12},{1,17},{... | collective-permute-start | bytes 479240 | tf_op jit(solution)/shard_map/ppermute | solution.py:46
  7.9 1.5 collective-permute-start.3
  9.4 2.3 pack_late.1
  14.0 2.3 fusion.3.xt
  17.7 3.2 %collective-permute-done.2.refs_2_ = bf16[48,1664]{1,0:T(8,128)(2,1)} collective-permute-done((bf16[48,1664]{1,0:T(8,128)(2,1)}, bf16[48,1664]{1,0:T(8,128)(2,1)}, u32[]{:S(2)}, u32[]{:S(2)}) %collective-permute-start.2) | collective-permute-done | bytes 159776 | tf_op jit(solution)/shard_map/ppermute | solution.py:46
  20.9 5.7 %collective-permute-done.3 = bf16[512,768]{0,1:T(8,128)(2,1)} collective-permute-done((bf16[512,768]{0,1:T(8,128)(2,1)}, bf16[512,768]{0,1:T(8,128)(2,1)}, u32[]{:S(2)}, u32[]{:S(2)}) %collective-permute-start.3) | collective-permute-done | bytes 786464 | tf_op jit(solution)/shard_map/ppermute | solution.py:49
  26.6 1.9 join.2.came_ref
  31.5 3.5 %collective-permute-start.10 = (bf16[48,3072]{1,0:T(8,128)(2,1)}, bf16[48,3072]{1,0:T(8,128)(2,1)}, u32[]{:S(2)}, u32[]{:S(2)}) collective-permute-start(bf16[48,3072]{1,0:T(8,128)(2,1)} %get-tuple-element.167), channel_id=1, source_target_pairs={{0,16},{4,20},{8,24},{12,28},{16,0},{20,4},{24,8},{28,12},{1,17},{... | collective-permute-start | bytes 884744 | tf_op jit(solution)/shard_map/ppermute | solution.py:46
  36.5 1.6 fusion.6.wt
  38.3 2.7 %collective-permute-done.6.along_ref = bf16[144,1664]{1,0:T(8,128)(2,1)S(1)} collective-permute-done((bf16[144,1664]{1,0:T(8,128)(2,1)}, bf16[144,1664]{1,0:T(8,128)(2,1)S(1)}, u32[]{:S(2)}, u32[]{:S(2)}) %collective-permute-start.6) | collective-permute-done | bytes 479264 | tf_op jit(solution)/shard_map/ppermute | solution.py:49
  45.9 3.6 %assemble.2 = (bf16[768,384]{1,0:T(8,128)(2,1)}, bf16[768,384]{1,0:T(8,128)(2,1)}, bf16[768,384]{1,0:T(8,128)(2,1)}, bf16[768,384]{1,0:T(8,128)(2,1)}, bf16[768,128]{1,0:T(8,128)(2,1)}) custom-call(s32[4]{0:T(128)} %pad_add_fusion.place, bf16[96,4736]{1,0:T(8,128)(2,1)} %get-tuple-element.158.own_ref, bf16[96,4736]{1,0:T(8,128)(2,1)} %collective-permute-done.8.side_ref, ...), custom_call_target="tpu_custom_call" | custom-call | flops 9999999827968 | bytes 1 | tf_op jit(solution)/shard_map/assemble/pallas_call | solution.py:167
  49.5 1.9 collective-permute-done.5.one_ref
  51.4 2.0 complete.2
  53.4 1.8 unpack_small.1
  55.2 3.0 %collective-permute-done.11.refs_2_ = bf16[48,3072]{1,0:T(8,128)(2,1)} collective-permute-done((bf16[48,3072]{1,0:T(8,128)(2,1)}, bf16[48,3072]{1,0:T(8,128)(2,1)}, u32[]{:S(2)}, u32[]{:S(2)}) %collective-permute-start.11) | collective-permute-done | bytes 294944 | tf_op jit(solution)/shard_map/ppermute | solution.py:46
  58.3 2.3 join.3.came_ref
  61.8 3.2 %convolution_convert_fusion.k = bf16[1280,384]{1,0:T(8,128)(2,1)} fusion(bf16[768,384]{1,0:T(8,128)(2,1)} %get-tuple-element.182.km, bf16[256,768]{0,1:T(8,128)(2,1)S(1)} %bitcast.58, bf16[512,768]{0,1:T(8,128)(2,1)S(1)} %copy-done.19, bf16[512,768]{0,1:T(8,128)(2,1)S(1)} %copy-done.17), kind=kOutput, calls=%fused_computation.2 | convolution fusion | flops 761364480 | bytes 3538944 | tf_op jit(solution)/shard_map/dot_general | solution.py:17
  65.1 3.0 %fusion.2.q = bf16[768,384]{1,0:T(8,128)(2,1)} fusion(bf16[768,384]{1,0:T(8,128)(2,1)} %get-tuple-element.178.qm, bf16[256,768]{0,1:T(8,128)(2,1)S(1)} %bitcast.59, bf16[512,768]{0,1:T(8,128)(2,1)} %bitcast.4, f32[384]{0:T(512)S(1)} %reduce), kind=kOutput, calls=%fused_computation.9 | convolution fusion | flops 456228864 | bytes 2360832 | tf_op jit(solution)/shard_map/dot_general | solution.py:17
  68.1 2.2 fusion.v
  70.3 12.4 %attention_forward.2 = (bf16[6,256,1280]{2,1,0:T(8,128)(2,1)}, bf16[6,512,1024]{2,1,0:T(8,128)(2,1)}, bf16[6,256,1280]{2,1,0:T(8,128)(2,1)}, bf16[768,384]{1,0:T(8,128)(2,1)}) custom-call(s32[1,1]{1,0:T(1,128)S(6)} %copy.71.length, bf16[768,384]{1,0:T(8,128)(2,1)} %fusion.2.q, bf16[1280,384]{1,0:T(8,128)(2,1)} %convolution_convert_fusion.k, ...), custom_call_target="tpu_custom_call" | custom-call | flops 9999999827968 | bytes 1 | tf_op jit(solution)/shard_map/attention_forward/pallas_call | solution.py:699
  82.6 2.1 halves_of.1
  87.5 7.2 %attention_forward.3 = (bf16[6,256,1280]{2,1,0:T(8,128)(2,1)}, bf16[6,512,1024]{2,1,0:T(8,128)(2,1)}, bf16[6,256,1280]{2,1,0:T(8,128)(2,1)}, bf16[768,384]{1,0:T(8,128)(2,1)}) custom-call(s32[1,1]{1,0:T(1,128)S(6)} %copy.71.length, bf16[768,384]{1,0:T(8,128)(2,1)} %fusion.2.q, ...), custom_call_target="tpu_custom_call", output_to_operand_aliasing={{0}: (5, {}), {1}: (6, {}), {2}: (7, {}), {3}: (8, {})} | custom-call | flops 9999999827968 | bytes 1 | tf_op jit(solution)/shard_map/attention_forward/pallas_call | solution.py:699
  94.7 2.9 %convolution_convert_fusion.1.p = bf16[768,768]{1,0:T(8,128)(2,1)} fusion(bf16[768,384]{1,0:T(8,128)(2,1)} %get-tuple-element.200.o, bf16[768,384]{1,0:T(8,128)(2,1)S(1)} %copy-done.23), kind=kOutput, calls=%fused_computation.6 | convolution fusion | flops 453574656 | bytes 2359296 | tf_op jit(solution)/shard_map/dot_general | solution.py:27
  97.6 4.7 %assemble.3 = (bf16[768,1536]{1,0:T(8,128)(2,1)}, bf16[768,1536]{1,0:T(8,128)(2,1)}) custom-call(s32[4]{0:T(128)} %pad_add_fusion.place, bf16[96,4736]{1,0:T(8,128)(2,1)} %get-tuple-element.158.own_ref, bf16[96,4736]{1,0:T(8,128)(2,1)} %collective-permute-done.8.side_ref, bf16[144,3072]{1,0:T(8,128)(2,1)} %join.3.came_ref, ...), custom_call_target="tpu_custom_call" | custom-call | flops 9999999827968 | bytes 1 | tf_op jit(solution)/shard_map/assemble/pallas_call | solution.py:167
  102.3 2.2 complete.3
  104.6 3.5 %first_norm.1 = (f32[768,768]{1,0:T(8,128)S(1)}, f32[768,128]{1,0:T(8,128)S(1)}, bf16[768,768]{1,0:T(8,128)(2,1)S(1)}) custom-call(bf16[512,768]{1,0:T(8,128)(2,1)S(1)} %bitcast.54, bf16[256,768]{1,0:T(8,128)(2,1)S(1)} %bitcast.55, bf16[768,768]{1,0:T(8,128)(2,1)} %convolution_convert_fusion.1.p, bf16[768,768]{1,0:T(8,128)(2,1)} %collective-permute-done.14.o, ...), custom_call_target="tpu_custom_call" | custom-call | flops 9999999827968 | bytes 1 | tf_op jit(solution)/shard_map/first_norm/pallas_call | solution.py:327
  109.5 5.7 %ffn_forward.1 = (bf16[768,1536]{1,0:T(8,128)(2,1)S(1)}, bf16[768,1536]{1,0:T(8,128)(2,1)S(1)}, bf16[768,768]{1,0:T(8,128)(2,1)}) custom-call(bf16[768,768]{1,0:T(8,128)(2,1)S(1)} %get-tuple-element.211.x, bf16[768,1536]{1,0:T(8,128)(2,1)S(1)} %copy-done.5, f32[1,1536]{1,0:T(1,128)S(1)} %copy-done.9, bf16[768,1536]{1,0:T(8,128)(2,1)S(1)} %copy-done.6), custom_call_target="tpu_custom_call" | custom-call | flops 9999999827968 | bytes 1 | tf_op jit(solution)/shard_map/ffn_forward/pallas_call | solution.py:387
  118.5 21.8 %ffn_backward.1 = (bf16[512,768]{1,0:T(8,128)(2,1)}, bf16[256,768]{1,0:T(8,128)(2,1)}, f32[768,768]{1,0:T(8,128)}, bf16[768,768]{1,0:T(8,128)(2,1)}, f32[8,768]{...) custom-call(s32[4]{0:T(128)} %pad_add_fusion.place, ...), custom_call_target="tpu_custom_call" | custom-call | flops 9999999827968 | bytes 1 | tf_op jit(solution)/shard_map/ffn_backward/pallas_call | solution.py:492
  144.5 6.7 %first_norm_backward.1 = (f32[768,768]{1,0:T(8,128)}, bf16[768,384]{1,0:T(8,128)(2,1)}, f32[8,768]{1,0:T(8,128)}) custom-call(f32[768,768]{1,0:T(8,128)} %get-tuple-element.217.d2, bf16[768,768]{1,0:T(8,128)(2,1)} %get-tuple-element.218.p, bf16[768,768]{1,0:T(8,128)(2,1)} %copy-done.30, f32[768,768]{1,0:T(8,128)} %copy-done.2, f32[768,128]{1,0:T(8,128)} %copy-done.8, ...), custom_call_target="tpu_custom_call" | custom-call | flops 9999999827968 | bytes 1 | tf_op jit(solution)/shard_map/first_norm_backward/pallas_call | solution.py:815
  151.2 17.0 %attention_backward.1 = (bf16[6,256,1280]{2,1,0:T(8,128)(2,1)}, bf16[768,384]{1,0:T(8,128)(2,1)}, bf16[1280,384]{1,0:T(8,128)(2,1)}, bf16[1280,384]{1,0:T(8,128)(2,1)}) custom-call(bf16[768,384]{1,0:T(8,128)(2,1)} %fusion.2.q, bf16[1280,384]{1,0:T(8,128)(2,1)} %convolution_convert_fusion.k, bf16[1280,384]{1,0:T(8,128)(2,1)} %fusion.v, ...), custom_call_target="tpu_custom_call" | custom-call | flops 9999999827968 | bytes 1 | tf_op jit(solution)/shard_map/attention_backward/pallas_call | solution.py:774
  169.3 4.2 %fold_pair.2 = (bf16[192,1536]{1,0:T(8,128)(2,1)}, bf16[192,1536]{1,0:T(8,128)(2,1)}, bf16[192,1536]{1,0:T(8,128)(2,1)}, bf16[192,1536]{1,0:T(8,128)(2,1)}) custom-call(s32[4]{0:T(128)} %pad_add_fusion.place, bf16[384,1536]{1,0:T(8,128)(2,1)} %get-tuple-element.225.refs_0_, bf16[384,1536]{1,0:T(8,128)(2,1)} %collective-permute-done.19.refs_1_, ...), custom_call_target="tpu_custom_call" | custom-call | flops 9999999827968 | bytes 1 | tf_op jit(solution)/shard_map/fold_pair/pallas_call | solution.py:542
  175.6 8.3 %weight_grads.1 = (bf16[384,768]{1,0:T(8,128)(2,1)}, bf16[384,768]{1,0:T(8,128)(2,1)}, bf16[384,896]{1,0:T(8,128)(2,1)}, bf16[384,896]{1,0:T(8,128)(2,1)}) custom-call(s32[4]{0:T(128)} %pad_add_fusion.place, f32[768,768]{1,0:T(8,128)} %get-tuple-element.220.d1, bf16[768,384]{1,0:T(8,128)(2,1)} %get-tuple-element.200.o, bf16[768,768]{1,0:T(8,128)(2,1)} %fusion.3.xt, ...), custom_call_target="tpu_custom_call" | custom-call | flops 9999999827968 | bytes 1 | tf_op jit(solution)/shard_map/weight_grads/pallas_call | solution.py:899
  185.9 4.1 %collective-permute-done.23.fa = bf16[192,1536]{1,0:T(8,128)(2,1)} collective-permute-done((bf16[192,1536]{1,0:T(8,128)(2,1)}, bf16[192,1536]{1,0:T(8,128)(2,1)}, u32[]{:S(2)}, u32[]{:S(2)}) %collective-permute-start.23) | collective-permute-done | bytes 589856 | tf_op jit(solution)/shard_map/ppermute | solution.py:49
  190.7 2.9 %fold_line.2 = (f32[48,3072]{1,0:T(8,128)}, bf16[48,3072]{1,0:T(8,128)(2,1)}, bf16[48,3072]{1,0:T(8,128)(2,1)}, bf16[48,3072]{1,0:T(8,128)(2,1)}) custom-call(s32[4]{0:T(128)} %pad_add_fusion.place, bf16[192,1536]{1,0:T(8,128)(2,1)} %get-tuple-element.231.fk, bf16[192,1536]{1,0:T(8,128)(2,1)} %collective-permute-done.23.fa, ...), custom_call_target="tpu_custom_call" | custom-call | flops 9999999827968 | bytes 1 | tf_op jit(solution)/shard_map/fold_line/pallas_call | solution.py:566
  194.4 2.3 collective-permute-start.34
  197.1 4.1 %collective-permute-done.21.refs_1_ = bf16[384,768]{1,0:T(8,128)(2,1)} collective-permute-done((bf16[384,768]{1,0:T(8,128)(2,1)}, bf16[384,768]{1,0:T(8,128)(2,1)}, u32[]{:S(2)}, u32[]{:S(2)}) %collective-permute-start.21) | collective-permute-done | bytes 589856 | tf_op jit(solution)/shard_map/ppermute | solution.py:43
  201.2 1.9 collective-permute-done.22.refs_3_
  203.1 2.9 %fold_pair.3 = (bf16[192,768]{1,0:T(8,128)(2,1)}, bf16[192,768]{1,0:T(8,128)(2,1)}, bf16[192,896]{1,0:T(8,128)(2,1)}, bf16[192,896]{1,0:T(8,128)(2,1)}) custom-call(s32[4]{0:T(128)} %pad_add_fusion.place, bf16[384,768]{1,0:T(8,128)(2,1)} %get-tuple-element.243.refs_0_, bf16[384,768]{1,0:T(8,128)(2,1)} %collective-permute-done.21.refs_1_, ...), custom_call_target="tpu_custom_call" | custom-call | flops 9999999827968 | bytes 1 | tf_op jit(solution)/shard_map/fold_pair/pallas_call | solution.py:542
  207.7 6.4 %input_pull.1 = (f32[768,768]{1,0:T(8,128)}, bf16[256,768]{1,0:T(8,128)(2,1)}, bf16[1024,768]{1,0:T(8,128)(2,1)}) custom-call(s32[4]{0:T(128)} %pad_add_fusion.place, bf16[768,384]{1,0:T(8,128)(2,1)} %get-tuple-element.258.q, bf16[1280,384]{1,0:T(8,128)(2,1)} %get-tuple-element.259.k, bf16[1280,384]{1,0:T(8,128)(2,1)} %get-tuple-element.260.v, ...), custom_call_target="tpu_custom_call" | custom-call | flops 9999999827968 | bytes 1 | tf_op jit(solution)/shard_map/input_pull/pallas_call | solution.py:849
  214.5 4.5 %collective-permute-done.35 = bf16[48,3072]{1,0:T(8,128)(2,1)} collective-permute-done((bf16[48,3072]{1,0:T(8,128)(2,1)}, bf16[48,3072]{1,0:T(8,128)(2,1)}, u32[]{:S(2)}, u32[]{:S(2)}) %collective-permute-start.35) | collective-permute-done | bytes 294944 | tf_op jit(solution)/shard_map/ppermute | solution.py:46
  219.1 2.0 add_convert_fusion.1
  222.5 2.3 fold_line.3
  224.8 3.0 %collective-permute-start.31 = (bf16[48,1664]{1,0:T(8,128)(2,1)}, bf16[48,1664]{1,0:T(8,128)(2,1)S(1)}, u32[]{:S(2)}, u32[]{:S(2)}) collective-permute-start(bf16[48,1664]{1,0:T(8,128)(2,1)} %get-tuple-element.269), channel_id=1, source_target_pairs={{0,16},{4,20},{8,24},{12,28},{16,0},{20,4},{24,8},{28,12},{1,17},{... | collective-permute-start | bytes 479240 | tf_op jit(solution)/shard_map/ppermute | solution.py:46
  230.6 1.8 add_convert_fusion
  233.8 1.7 convert_add_fusion
  236.5 2.7 %collective-permute-done.32 = bf16[48,1664]{1,0:T(8,128)(2,1)S(1)} collective-permute-done((bf16[48,1664]{1,0:T(8,128)(2,1)}, bf16[48,1664]{1,0:T(8,128)(2,1)S(1)}, u32[]{:S(2)}, u32[]{:S(2)}) %collective-permute-start.32) | collective-permute-done | bytes 159776 | tf_op jit(solution)/shard_map/ppermute | solution.py:46
  243.4 3.6 %collective-permute-done.37 = bf16[48,1664]{1,0:T(8,128)(2,1)S(1)} collective-permute-done((bf16[48,1664]{1,0:T(8,128)(2,1)S(1)}, bf16[48,1664]{1,0:T(8,128)(2,1)S(1)}, u32[]{:S(2)}, u32[]{:S(2)}) %collective-permute-start.37) | collective-permute-done | bytes 159776 | tf_op jit(solution)/shard_map/ppermute | solution.py:49
  (152 shorter events, 51.2 us)
Async XLA Ops:
  1.3 5.5 %copy-start = (bf16[1,512,768]{2,1,0:T(8,128)(2,1)S(1)}, bf16[1,512,768]{2,1,0:T(8,128)(2,1)}, u32[]{:S(2)}) copy-start(bf16[1,512,768]{2,1,0:T(8,128)(2,1)} %param.22) | copy-start | bytes 2359300
  3.2 13.1 %collective-permute-start = (bf16[48,1664]{1,0:T(8,128)(2,1)}, bf16[48,1664]{1,0:T(8,128)(2,1)}, u32[]{:S(2)}, u32[]{:S(2)}) collective-permute-start(bf16[48,1664]{1,0:T(8,128)(2,1)} %get-tuple-element.150), channel_id=1, source_target_pairs={{0,8},{4,12},{8,0},{12,4},{16,24},{20,28},{24,16},{28,20},{1,9},{5... | collective-permute-start | bytes 479240 | tf_op jit(solution)/shard_map/ppermute | solution.py:46
  3.2 14.5 %collective-permute-start.1 = (bf16[48,1664]{1,0:T(8,128)(2,1)}, bf16[48,1664]{1,0:T(8,128)(2,1)}, u32[]{:S(2)}, u32[]{:S(2)}) collective-permute-start(bf16[48,1664]{1,0:T(8,128)(2,1)} %get-tuple-element.150), channel_id=1, source_target_pairs={{0,16},{4,20},{8,24},{12,28},{16,0},{20,4},{24,8},{28,12},{1,17},{... | collective-permute-start | bytes 479240 | tf_op jit(solution)/shard_map/ppermute | solution.py:46
  6.3 14.6 %collective-permute-start.2 = (bf16[48,1664]{1,0:T(8,128)(2,1)}, bf16[48,1664]{1,0:T(8,128)(2,1)}, u32[]{:S(2)}, u32[]{:S(2)}) collective-permute-start(bf16[48,1664]{1,0:T(8,128)(2,1)} %get-tuple-element.150), channel_id=1, source_target_pairs={{0,24},{4,28},{8,16},{12,20},{16,8},{20,12},{24,0},{28,4},{1,25},{... | collective-permute-start | bytes 479240 | tf_op jit(solution)/shard_map/ppermute | solution.py:46
  7.9 18.8 %collective-permute-start.3 = (bf16[512,768]{0,1:T(8,128)(2,1)}, bf16[512,768]{0,1:T(8,128)(2,1)}, u32[]{:S(2)}, u32[]{:S(2)}) collective-permute-start(bf16[512,768]{0,1:T(8,128)(2,1)} %bitcast.4), channel_id=1, source_target_pairs={{0,2},{2,0},{1,3},{3,1},{4,6},{6,4},{5,7},{7,5},{8,10},{10,8},{9,1... | collective-permute-start | bytes 2359304 | tf_op jit(solution)/shard_map/ppermute | solution.py:49
  11.7 33.5 %collective-permute-start.8 = (bf16[96,4736]{1,0:T(8,128)(2,1)}, bf16[96,4736]{1,0:T(8,128)(2,1)}, u32[]{:S(2)}, u32[]{:S(2)}) collective-permute-start(bf16[96,4736]{1,0:T(8,128)(2,1)} %get-tuple-element.158.own_ref), channel_id=1, source_target_pairs={{0,4},{4,0},{8,12},{12,8},{16,20},{20,16},{24,28},{28,24},{1,5},{5... | collective-permute-start | bytes 2727944 | tf_op jit(solution)/shard_map/ppermute | solution.py:43
  13.4 15.1 %copy-start.13 = (bf16[1,1,256,768]{2,3,1,0:T(8,128)(2,1)}, bf16[1,1,256,768]{2,3,1,0:T(8,128)(2,1)S(1)}, u32[]{:S(2)}) copy-start(bf16[1,1,256,768]{2,3,1,0:T(8,128)(2,1)S(1)} %copy.55) | copy-start | bytes 1179652
  28.5 14.6 %collective-permute-start.4 = (bf16[144,1664]{1,0:T(8,128)(2,1)}, bf16[144,1664]{1,0:T(8,128)(2,1)S(1)}, u32[]{:S(2)}, u32[]{:S(2)}) collective-permute-start(bf16[144,1664]{1,0:T(8,128)(2,1)} %join.2.came_ref), channel_id=1, source_target_pairs={{0,4},{4,0},{8,12},{12,8},{16,20},{20,16},{24,28},{28,24},{1,5},{5... | collective-permute-start | bytes 1437704 | tf_op jit(solution)/shard_map/ppermute | solution.py:43
  30.0 6.5 %copy-start.14 = (bf16[1,1,256,768]{2,3,1,0:T(8,128)(2,1)S(1)}, bf16[1,1,256,768]{2,3,1,0:T(8,128)(2,1)}, u32[]{:S(2)}) copy-start(bf16[1,1,256,768]{2,3,1,0:T(8,128)(2,1)} %copy-done.13) | copy-start | bytes 1179652
  30.0 10.9 %collective-permute-start.6 = (bf16[144,1664]{1,0:T(8,128)(2,1)}, bf16[144,1664]{1,0:T(8,128)(2,1)S(1)}, u32[]{:S(2)}, u32[]{:S(2)}) collective-permute-start(bf16[144,1664]{1,0:T(8,128)(2,1)} %join.2.came_ref), channel_id=1, source_target_pairs={{0,2},{2,0},{1,3},{3,1},{4,6},{6,4},{5,7},{7,5},{8,10},{10,8},{9,1... | collective-permute-start | bytes 1437704 | tf_op jit(solution)/shard_map/ppermute | solution.py:49
  31.5 23.7 %collective-permute-start.10 = (bf16[48,3072]{1,0:T(8,128)(2,1)}, bf16[48,3072]{1,0:T(8,128)(2,1)}, u32[]{:S(2)}, u32[]{:S(2)}) collective-permute-start(bf16[48,3072]{1,0:T(8,128)(2,1)} %get-tuple-element.167), channel_id=1, source_target_pairs={{0,16},{4,20},{8,24},{12,28},{16,0},{20,4},{24,8},{28,12},{1,17},{... | collective-permute-start | bytes 884744 | tf_op jit(solution)/shard_map/ppermute | solution.py:46
  35.0 23.2 %collective-permute-start.11 = (bf16[48,3072]{1,0:T(8,128)(2,1)}, bf16[48,3072]{1,0:T(8,128)(2,1)}, u32[]{:S(2)}, u32[]{:S(2)}) collective-permute-start(bf16[48,3072]{1,0:T(8,128)(2,1)} %get-tuple-element.167), channel_id=1, source_target_pairs={{0,24},{4,28},{8,16},{12,20},{16,8},{20,12},{24,0},{28,4},{1,25},{... | collective-permute-start | bytes 884744 | tf_op jit(solution)/shard_map/ppermute | solution.py:46
  40.9 5.0 %copy-start.26 = (bf16[144,1664]{1,0:T(8,128)(2,1)}, bf16[144,1664]{1,0:T(8,128)(2,1)S(1)}, u32[]{:S(2)}) copy-start(bf16[144,1664]{1,0:T(8,128)(2,1)S(1)} %collective-permute-done.6.along_ref) | copy-start | bytes 1437700
  40.9 17.3 %collective-permute-start.9 = (bf16[48,3072]{1,0:T(8,128)(2,1)}, bf16[48,3072]{1,0:T(8,128)(2,1)}, u32[]{:S(2)}, u32[]{:S(2)}) collective-permute-start(bf16[48,3072]{1,0:T(8,128)(2,1)} %get-tuple-element.167), channel_id=1, source_target_pairs={{0,8},{4,12},{8,0},{12,4},{16,24},{20,28},{24,16},{28,20},{1,9},{5... | collective-permute-start | bytes 884744 | tf_op jit(solution)/shard_map/ppermute | solution.py:46
  43.1 8.3 %collective-permute-start.7 = (bf16[144,896]{1,0:T(8,128)(2,1)}, bf16[144,896]{1,0:T(8,128)(2,1)}, u32[]{:S(2)}, u32[]{:S(2)}) collective-permute-start(bf16[144,896]{1,0:T(8,128)(2,1)} %slice.94), channel_id=1, source_target_pairs={{0,4},{4,0},{8,12},{12,8},{16,20},{20,16},{24,28},{28,24},{1,5},{5... | collective-permute-start | bytes 774152 | tf_op jit(solution)/shard_map/ppermute | solution.py:43
  45.2 6.2 %collective-permute-start.5 = (bf16[144,768]{1,0:T(8,128)(2,1)}, bf16[144,768]{1,0:T(8,128)(2,1)}, u32[]{:S(2)}, u32[]{:S(2)}) collective-permute-start(bf16[144,768]{1,0:T(8,128)(2,1)} %slice.93), channel_id=1, source_target_pairs={{0,2},{2,0},{1,3},{3,1},{4,6},{6,4},{5,7},{7,5},{8,10},{10,8},{9,1... | collective-permute-start | bytes 663560 | tf_op jit(solution)/shard_map/ppermute | solution.py:49
  60.5 22.1 %collective-permute-start.12 = (bf16[144,3072]{1,0:T(8,128)(2,1)}, bf16[144,3072]{1,0:T(8,128)(2,1)}, u32[]{:S(2)}, u32[]{:S(2)}) collective-permute-start(bf16[144,3072]{1,0:T(8,128)(2,1)} %join.3.came_ref), channel_id=1, source_target_pairs={{0,4},{4,0},{8,12},{12,8},{16,20},{20,16},{24,28},{28,24},{1,5},{5... | collective-permute-start | bytes 2654216 | tf_op jit(solution)/shard_map/ppermute | solution.py:43
  61.1 21.6 %collective-permute-start.13 = (bf16[144,3072]{1,0:T(8,128)(2,1)}, bf16[144,3072]{1,0:T(8,128)(2,1)}, u32[]{:S(2)}, u32[]{:S(2)}) collective-permute-start(bf16[144,3072]{1,0:T(8,128)(2,1)} %join.3.came_ref), channel_id=1, source_target_pairs={{0,2},{2,0},{1,3},{3,1},{4,6},{6,4},{5,7},{7,5},{8,10},{10,8},{9,1... | collective-permute-start | bytes 2654216 | tf_op jit(solution)/shard_map/ppermute | solution.py:49
  84.7 17.6 %collective-permute-start.15 = (bf16[144,1536]{1,0:T(8,128)(2,1)}, bf16[144,1536]{1,0:T(8,128)(2,1)}, u32[]{:S(2)}, u32[]{:S(2)}) collective-permute-start(bf16[144,1536]{1,0:T(8,128)(2,1)} %get-tuple-element.195), channel_id=1, source_target_pairs={{0,2},{2,0},{1,3},{3,1},{4,6},{6,4},{5,7},{7,5},{8,10},{10,8},{9,1... | collective-permute-start | bytes 1327112 | tf_op jit(solution)/shard_map/ppermute | solution.py:49
  86.0 16.3 %collective-permute-start.16 = (bf16[144,1536]{1,0:T(8,128)(2,1)}, bf16[144,1536]{1,0:T(8,128)(2,1)}, u32[]{:S(2)}, u32[]{:S(2)}) collective-permute-start(bf16[144,1536]{1,0:T(8,128)(2,1)} %get-tuple-element.204), channel_id=1, source_target_pairs={{0,4},{4,0},{8,12},{12,8},{16,20},{20,16},{24,28},{28,24},{1,5},{5... | collective-permute-start | bytes 1327112 | tf_op jit(solution)/shard_map/ppermute | solution.py:43
  87.5 7.2 %copy-start.23 = (bf16[768,384]{1,0:T(8,128)(2,1)S(1)}, bf16[768,384]{1,0:T(8,128)(2,1)}, u32[]{:S(2)}) copy-start(bf16[768,384]{1,0:T(8,128)(2,1)} %get-tuple-element.201.ot) | copy-start | bytes 1769476
  97.6 6.9 %collective-permute-start.14 = (bf16[768,768]{1,0:T(8,128)(2,1)}, bf16[768,768]{1,0:T(8,128)(2,1)}, u32[]{:S(2)}, u32[]{:S(2)}) collective-permute-start(bf16[768,768]{1,0:T(8,128)(2,1)} %convolution_convert_fusion.1.p), channel_id=1, source_target_pairs={{0,1},{1,0},{2,3},{3,2},{4,5},{5,4},{6,7},{7,6},{8,9},{9,8},{10,11... | collective-permute-start | bytes 3538952 | tf_op jit(solution)/shard_map/ppermute | solution.py:52
  104.6 4.9 %copy-start.5 = (bf16[768,1536]{1,0:T(8,128)(2,1)S(1)}, bf16[768,1536]{1,0:T(8,128)(2,1)}, u32[]{:S(2)}) copy-start(bf16[768,1536]{1,0:T(8,128)(2,1)} %get-tuple-element.207.up) | copy-start | bytes 7077892
  104.6 4.9 %copy-start.6 = (bf16[768,1536]{1,0:T(8,128)(2,1)S(1)}, bf16[768,1536]{1,0:T(8,128)(2,1)}, u32[]{:S(2)}) copy-start(bf16[768,1536]{1,0:T(8,128)(2,1)} %get-tuple-element.209.dn) | copy-start | bytes 7077892
  109.5 5.7 %copy-start.8 = (f32[768,128]{1,0:T(8,128)}, f32[768,128]{1,0:T(8,128)S(1)}, u32[]{:S(2)}) copy-start(f32[768,128]{1,0:T(8,128)S(1)} %get-tuple-element.219.r1) | copy-start | bytes 1179652
  115.1 3.3 %collective-permute-start.17 = (bf16[768,768]{1,0:T(8,128)(2,1)}, bf16[768,768]{1,0:T(8,128)(2,1)}, u32[]{:S(2)}, u32[]{:S(2)}) collective-permute-start(bf16[768,768]{1,0:T(8,128)(2,1)} %get-tuple-element.210.p), channel_id=1, source_target_pairs={{0,1},{1,0},{2,3},{3,2},{4,5},{5,4},{6,7},{7,6},{8,9},{9,8},{10,11... | collective-permute-start | bytes 3538952 | tf_op jit(solution)/shard_map/ppermute | solution.py:52
  140.3 3.3 %collective-permute-start.18 = (bf16[768,768]{1,0:T(8,128)(2,1)}, bf16[768,768]{1,0:T(8,128)(2,1)S(1)}, u32[]{:S(2)}, u32[]{:S(2)}) collective-permute-start(bf16[768,768]{1,0:T(8,128)(2,1)} %get-tuple-element.218.p), channel_id=1, source_target_pairs={{0,1},{1,0},{2,3},{3,2},{4,5},{5,4},{6,7},{7,6},{8,9},{9,8},{10,11... | collective-permute-start | bytes 3538952 | tf_op jit(solution)/shard_map/ppermute | solution.py:52
  140.8 28.3 %collective-permute-start.19 = (bf16[384,1536]{1,0:T(8,128)(2,1)}, bf16[384,1536]{1,0:T(8,128)(2,1)}, u32[]{:S(2)}, u32[]{:S(2)}) collective-permute-start(bf16[384,1536]{1,0:T(8,128)(2,1)} %get-tuple-element.226), channel_id=1, source_target_pairs={{0,4},{4,0},{8,12},{12,8},{16,20},{20,16},{24,28},{28,24},{1,5},{5... | collective-permute-start | bytes 3538952 | tf_op jit(solution)/shard_map/ppermute | solution.py:43
  141.3 28.0 %collective-permute-start.20 = (bf16[384,1536]{1,0:T(8,128)(2,1)}, bf16[384,1536]{1,0:T(8,128)(2,1)}, u32[]{:S(2)}, u32[]{:S(2)}) collective-permute-start(bf16[384,1536]{1,0:T(8,128)(2,1)} %get-tuple-element.227), channel_id=1, source_target_pairs={{0,2},{2,0},{1,3},{3,1},{4,6},{6,4},{5,7},{7,5},{8,10},{10,8},{9,1... | collective-permute-start | bytes 3538952 | tf_op jit(solution)/shard_map/ppermute | solution.py:49
  173.5 16.5 %collective-permute-start.23 = (bf16[192,1536]{1,0:T(8,128)(2,1)}, bf16[192,1536]{1,0:T(8,128)(2,1)}, u32[]{:S(2)}, u32[]{:S(2)}) collective-permute-start(bf16[192,1536]{1,0:T(8,128)(2,1)} %get-tuple-element.232), channel_id=1, source_target_pairs={{0,2},{2,0},{1,3},{3,1},{4,6},{6,4},{5,7},{7,5},{8,10},{10,8},{9,1... | collective-permute-start | bytes 1769480 | tf_op jit(solution)/shard_map/ppermute | solution.py:49
  174.2 16.5 %collective-permute-start.24 = (bf16[192,1536]{1,0:T(8,128)(2,1)}, bf16[192,1536]{1,0:T(8,128)(2,1)}, u32[]{:S(2)}, u32[]{:S(2)}) collective-permute-start(bf16[192,1536]{1,0:T(8,128)(2,1)} %get-tuple-element.234), channel_id=1, source_target_pairs={{0,4},{4,0},{8,12},{12,8},{16,20},{20,16},{24,28},{28,24},{1,5},{5... | collective-permute-start | bytes 1769480 | tf_op jit(solution)/shard_map/ppermute | solution.py:43
  183.9 19.2 %collective-permute-start.22 = (bf16[384,896]{1,0:T(8,128)(2,1)}, bf16[384,896]{1,0:T(8,128)(2,1)}, u32[]{:S(2)}, u32[]{:S(2)}) collective-permute-start(bf16[384,896]{1,0:T(8,128)(2,1)} %get-tuple-element.245), channel_id=1, source_target_pairs={{0,2},{2,0},{1,3},{3,1},{4,6},{6,4},{5,7},{7,5},{8,10},{10,8},{9,1... | collective-permute-start | bytes 2064392 | tf_op jit(solution)/shard_map/ppermute | solution.py:49
  185.4 15.8 %collective-permute-start.21 = (bf16[384,768]{1,0:T(8,128)(2,1)}, bf16[384,768]{1,0:T(8,128)(2,1)}, u32[]{:S(2)}, u32[]{:S(2)}) collective-permute-start(bf16[384,768]{1,0:T(8,128)(2,1)} %get-tuple-element.244), channel_id=1, source_target_pairs={{0,4},{4,0},{8,12},{12,8},{16,20},{20,16},{24,28},{28,24},{1,5},{5... | collective-permute-start | bytes 1769480 | tf_op jit(solution)/shard_map/ppermute | solution.py:43
  193.7 20.4 %collective-permute-start.33 = (bf16[48,3072]{1,0:T(8,128)(2,1)}, bf16[48,3072]{1,0:T(8,128)(2,1)}, u32[]{:S(2)}, u32[]{:S(2)}) collective-permute-start(bf16[48,3072]{1,0:T(8,128)(2,1)} %get-tuple-element.249), channel_id=1, source_target_pairs={{0,8},{4,12},{8,0},{12,4},{16,24},{20,28},{24,16},{28,20},{1,9},{5... | collective-permute-start | bytes 884744 | tf_op jit(solution)/shard_map/ppermute | solution.py:46
  194.4 20.1 %collective-permute-start.34 = (bf16[48,3072]{1,0:T(8,128)(2,1)}, bf16[48,3072]{1,0:T(8,128)(2,1)}, u32[]{:S(2)}, u32[]{:S(2)}) collective-permute-start(bf16[48,3072]{1,0:T(8,128)(2,1)} %get-tuple-element.250), channel_id=1, source_target_pairs={{0,16},{4,20},{8,24},{12,28},{16,0},{20,4},{24,8},{28,12},{1,17},{... | collective-permute-start | bytes 884744 | tf_op jit(solution)/shard_map/ppermute | solution.py:46
  196.7 22.4 %collective-permute-start.35 = (bf16[48,3072]{1,0:T(8,128)(2,1)}, bf16[48,3072]{1,0:T(8,128)(2,1)}, u32[]{:S(2)}, u32[]{:S(2)}) collective-permute-start(bf16[48,3072]{1,0:T(8,128)(2,1)} %get-tuple-element.251), channel_id=1, source_target_pairs={{0,24},{4,28},{8,16},{12,20},{16,8},{20,12},{24,0},{28,4},{1,25},{... | collective-permute-start | bytes 884744 | tf_op jit(solution)/shard_map/ppermute | solution.py:46
  206.0 16.5 %collective-permute-start.29 = (bf16[192,896]{1,0:T(8,128)(2,1)}, bf16[192,896]{1,0:T(8,128)(2,1)}, u32[]{:S(2)}, u32[]{:S(2)}) collective-permute-start(bf16[192,896]{1,0:T(8,128)(2,1)} %get-tuple-element.257), channel_id=1, source_target_pairs={{0,4},{4,0},{8,12},{12,8},{16,20},{20,16},{24,28},{28,24},{1,5},{5... | collective-permute-start | bytes 1032200 | tf_op jit(solution)/shard_map/ppermute | solution.py:43
  207.2 15.3 %collective-permute-start.28 = (bf16[192,768]{1,0:T(8,128)(2,1)}, bf16[192,768]{1,0:T(8,128)(2,1)}, u32[]{:S(2)}, u32[]{:S(2)}) collective-permute-start(bf16[192,768]{1,0:T(8,128)(2,1)} %get-tuple-element.255), channel_id=1, source_target_pairs={{0,2},{2,0},{1,3},{3,1},{4,6},{6,4},{5,7},{7,5},{8,10},{10,8},{9,1... | collective-permute-start | bytes 884744 | tf_op jit(solution)/shard_map/ppermute | solution.py:49
  207.7 11.4 %copy-start.22 = (f32[48,3072]{1,0:T(8,128)S(1)}, f32[48,3072]{1,0:T(8,128)}, u32[]{:S(2)}) copy-start(f32[48,3072]{1,0:T(8,128)} %get-tuple-element.271) | copy-start | bytes 1769476
  214.1 16.5 %collective-permute-start.25 = (bf16[1024,768]{1,0:T(8,128)(2,1)}, bf16[1024,768]{1,0:T(8,128)(2,1)}, u32[]{:S(2)}, u32[]{:S(2)}) collective-permute-start(bf16[1024,768]{1,0:T(8,128)(2,1)} %get-tuple-element.262), channel_id=1, source_target_pairs={{0,1},{1,0},{2,3},{3,2},{4,5},{5,4},{6,7},{7,6},{8,9},{9,8},{10,11... | collective-permute-start | bytes 4718600 | tf_op jit(solution)/shard_map/ppermute | solution.py:52
  221.1 7.2 %collective-permute-start.36 = (bf16[48,3072]{1,0:T(8,128)(2,1)}, bf16[48,3072]{1,0:T(8,128)(2,1)}, u32[]{:S(2)}, u32[]{:S(2)}) collective-permute-start(bf16[48,3072]{1,0:T(8,128)(2,1)} %add_convert_fusion.1), channel_id=1, source_target_pairs={{0,2},{2,0},{1,3},{3,1},{4,6},{6,4},{5,7},{7,5},{8,10},{10,8},{9,1... | collective-permute-start | bytes 884744 | tf_op jit(solution)/shard_map/ppermute | solution.py:49
  224.8 11.7 %collective-permute-start.30 = (bf16[48,1664]{1,0:T(8,128)(2,1)}, bf16[48,1664]{1,0:T(8,128)(2,1)S(1)}, u32[]{:S(2)}, u32[]{:S(2)}) collective-permute-start(bf16[48,1664]{1,0:T(8,128)(2,1)} %get-tuple-element.268), channel_id=1, source_target_pairs={{0,8},{4,12},{8,0},{12,4},{16,24},{20,28},{24,16},{28,20},{1,9},{5... | collective-permute-start | bytes 479240 | tf_op jit(solution)/shard_map/ppermute | solution.py:46
  224.8 11.7 %collective-permute-start.31 = (bf16[48,1664]{1,0:T(8,128)(2,1)}, bf16[48,1664]{1,0:T(8,128)(2,1)S(1)}, u32[]{:S(2)}, u32[]{:S(2)}) collective-permute-start(bf16[48,1664]{1,0:T(8,128)(2,1)} %get-tuple-element.269), channel_id=1, source_target_pairs={{0,16},{4,20},{8,24},{12,28},{16,0},{20,4},{24,8},{28,12},{1,17},{... | collective-permute-start | bytes 479240 | tf_op jit(solution)/shard_map/ppermute | solution.py:46
  227.8 11.4 %collective-permute-start.32 = (bf16[48,1664]{1,0:T(8,128)(2,1)}, bf16[48,1664]{1,0:T(8,128)(2,1)S(1)}, u32[]{:S(2)}, u32[]{:S(2)}) collective-permute-start(bf16[48,1664]{1,0:T(8,128)(2,1)} %get-tuple-element.270), channel_id=1, source_target_pairs={{0,24},{4,28},{8,16},{12,20},{16,8},{20,12},{24,0},{28,4},{1,25},{... | collective-permute-start | bytes 479240 | tf_op jit(solution)/shard_map/ppermute | solution.py:46
  232.5 7.9 %copy-start.25 = (f32[48,1664]{1,0:T(8,128)S(1)}, f32[48,1664]{1,0:T(8,128)}, u32[]{:S(2)}) copy-start(f32[48,1664]{1,0:T(8,128)} %get-tuple-element.267) | copy-start | bytes 958468
  232.5 7.8 %collective-permute-start.26 = (bf16[256,768]{1,0:T(8,128)(2,1)S(1)}, bf16[256,768]{1,0:T(8,128)(2,1)S(1)}, u32[]{:S(2)}, u32[]{:S(2)}) collective-permute-start(bf16[256,768]{1,0:T(8,128)(2,1)S(1)} %add_convert_fusion), channel_id=1, source_target_pairs={{0,2},{2,0},{1,3},{3,1},{4,6},{6,4},{5,7},{7,5},{8,10},{10,8},{9,1... | collective-permute-start | bytes 1179656 | tf_op jit(solution)/shard_map/ppermute | solution.py:49
  240.3 1.7 collective-permute-start.27
  240.4 6.6 %collective-permute-start.37 = (bf16[48,1664]{1,0:T(8,128)(2,1)S(1)}, bf16[48,1664]{1,0:T(8,128)(2,1)S(1)}, u32[]{:S(2)}, u32[]{:S(2)}) collective-permute-start(bf16[48,1664]{1,0:T(8,128)(2,1)S(1)} %add_convert_fusion.2), channel_id=1, source_target_pairs={{0,2},{2,0},{1,3},{3,1},{4,6},{6,4},{5,7},{7,5},{8,10},{10,8},{9,1... | collective-permute-start | bytes 479240 | tf_op jit(solution)/shard_map/ppermute | solution.py:49
  (22 other events, 61.3 us)
